TPU v7x, 512 devices: a whole 4x8x8 slice. The times are simulated.
512 devices in a mesh: sub: 128 (over y, z, core), case: 4 (over x).
Axes of the slice: x: 4, y: 8, z: 8, core: 2. Of those that a mesh axis runs over, the one named last changes fastest.
Arguments:
- multipliers: float32 [64, 196608], P('case', 'sub'), may hold values from -6 to 6
- right_side: float32 [64, 196608], P('case', 'sub')
- dual_ops: bfloat16 [196608, 1536], P('sub'), as said below
- glue_match: int32 [128, 2, 128], P('sub'), may hold values from 0 to 127, as said below
- mortar: bfloat16 [128, 4, 128, 128], P('sub'), may hold values from -0.5 to 0.5
- contact_ids: int32 [128, 4], P('sub'), may hold values from 0 to 3
- contact_count: int32 [128], P('sub'), may hold values from 1 to 4
Outputs:
- solved: float32 [64, 196608], P('case', 'sub')
- grad_norm: float32 [1], replicated
Inputs may be any that keep to these rules, and one draw needn't show every extreme that they name: glue_match[s,1] is a permutation of 0 to 127, and glue_match[(s+1) mod 128,0] is its inverse. `dual_ops`: each subdomain's block is symmetric positive definite.
All inputs are finite; a program needn't handle non-finite values.
Results may differ from a plain program's by a relative error of at most 0.002.
Values may be sent and summed in bfloat16 or wider, within the bound.
No kernel may reach another device: no remote copies, remote signals or barrier semaphores. Data moves between devices by JAX's collectives and lax.ppermute only.
A program may use at most 64 MiB of HBM per device.

v0:
```python
import jax
import jax.numpy as jnp
from jax import lax
from jax.sharding import PartitionSpec as P

M = 1536
BLK = 128
ITERS = 4


penalty = 0.5
exact_mode = lax.Precision.HIGHEST


def shifted(value, axis, by):
    devices = lax.axis_size(axis)
    return lax.ppermute(value, axis, [(i, (i + by) % devices) for i in range(devices)])


def shortened(value):

    def short(part):
        return part.astype(jnp.bfloat16) if part.dtype == jnp.float32 else part

    return jax.tree.map(short, value)


def face_partner(face, offset):
    return shifted(face, "sub", offset)


def jump_terms(slave_blocks, own_blocks, contact_ids, live_count, mortar):
    onehot = (contact_ids[:, None] == jnp.arange(4, dtype=jnp.int32)[None, :]).astype(jnp.float32)
    selected = jnp.einsum("kb,cbe->cke", onehot, slave_blocks, precision=exact_mode)
    active = (jnp.arange(4, dtype=jnp.int32) < live_count).astype(jnp.float32)
    mortar_jump = (
        jnp.einsum("cke,kef->ckf", selected, mortar, precision=exact_mode) - own_blocks
    ) * active[None, :, None]
    return (mortar_jump, onehot)


def back_terms(mortar_jump, onehot, mortar):
    reply_rows = jnp.einsum("ckf,kef->cke", mortar_jump, mortar, precision=exact_mode)
    return jnp.einsum("kb,cke->cbe", onehot, reply_rows, precision=exact_mode)


def apply_operator(vector, dual_op, glue_match, mortar, contact_ids, live_count):
    case_cols = vector.shape[0]
    blocks = vector.reshape(case_cols, 12, BLK)
    half_axis = lax.axis_size("sub") // 2
    prev_face = face_partner(blocks[:, 1, :], 1)
    next_face = face_partner(blocks[:, 0, :], -1)
    swapped_first = jnp.take(prev_face, glue_match[0], axis=1)
    swapped_second = jnp.take(next_face, glue_match[1], axis=1)
    own_blocks = blocks[:, 2:6, :]
    slave_blocks = shifted(shortened(own_blocks), "sub", half_axis).astype(own_blocks.dtype)
    mortar_jump, onehot = jump_terms(slave_blocks, own_blocks, contact_ids, live_count, mortar)
    returned = shifted(shortened(back_terms(mortar_jump, onehot, mortar)), "sub", half_axis)
    local_part = jnp.dot(vector.astype(jnp.bfloat16), dual_op, preferred_element_type=jnp.float32)
    face_part = penalty * (blocks[:, 0:2, :] - jnp.stack([swapped_first, swapped_second], axis=1))
    correction = jnp.concatenate(
        [face_part, returned - mortar_jump, jnp.zeros((case_cols, 6, BLK), jnp.float32)], axis=1
    )
    return local_part + correction.reshape(case_cols, M)


def on_device(multipliers, right_side, dual_ops, glue_match, mortar, contact_ids, contact_count):
    own_mortar = mortar[0].astype(jnp.float32)

    def operate(vector):
        return apply_operator(
            vector, dual_ops, glue_match[0], own_mortar, contact_ids[0], contact_count[0]
        )

    current = multipliers
    grad_norms = jnp.zeros((multipliers.shape[0],), jnp.float32)
    for iteration in range(ITERS):
        gradient = operate(current) - right_side
        grad_norms = lax.psum(jnp.sum(gradient * gradient, axis=1), "sub")
        curved = operate(gradient)
        grad_curves = lax.psum(jnp.sum(gradient * curved, axis=1), "sub")
        step_size = grad_norms / grad_curves
        moved = current - step_size[:, None] * gradient
        moved_blocks = moved.reshape(moved.shape[0], 12, BLK)
        clipped = jnp.concatenate(
            [moved_blocks[:, 0:2], jnp.maximum(moved_blocks[:, 2:6], 0.0), moved_blocks[:, 6:12]],
            axis=1,
        )
        current = clipped.reshape(moved.shape)
    total_norm = lax.psum(jnp.sum(grad_norms), "case")
    return (current, jnp.sqrt(total_norm).reshape(1))


def solution(mesh):
    in_specs = (
        P("case", "sub"),
        P("case", "sub"),
        P("sub", None),
        P("sub", None, None),
        P("sub", None, None, None),
        P("sub", None),
        P("sub"),
    )
    out_specs = (P("case", "sub"), P())
    return jax.shard_map(
        on_device, mesh=mesh, in_specs=in_specs, out_specs=out_specs, check_vma=False
    )
```

profile of v0, /device:TPU:1, one launch (start us, length us, event | category | flops | bytes accessed | tf_op | source)
XLA Modules:
  0.0 1256.7 jit_solution(6448773023984545315)
XLA Ops:
  1.6 8.3 collective-permute-start.2
  19.1 4.6 collective-permute-done
  26.8 4.8 collective-permute-start.3
  38.6 9.3 collective-permute-start.5
  48.0 4.8 collective-permute-start.6
  69.4 253.3 %all-reduce.3 = (f32[16]{0:T(128)S(1)}, f32[16]{0:T(128)S(1)}) all-reduce(f32[16]{0:T(128)S(1)} %get-tuple-element.41, f32[16]{0:T(128)S(1)} %fusion.8), channel_id=1, replica_groups=mesh['sub'=128,'case'=4] {'sub'}, use_global_device_ids=true, to_apply=%region_1.3 | all-reduce | flops 32 | bytes 256 | tf_op jit(solution)/shard_map/psum | solution.py:79
  336.5 4.7 collective-permute-start.11
  348.3 7.6 collective-permute-start.13
  356.0 4.7 collective-permute-start.14
  365.8 4.4 collective-permute-start.15
  377.4 253.3 %all-reduce.2 = (f32[16]{0:T(128)S(1)}, f32[16]{0:T(128)S(1)}) all-reduce(f32[16]{0:T(128)S(1)} %get-tuple-element.43, f32[16]{0:T(128)S(1)} %fusion.9), channel_id=1, replica_groups=mesh['sub'=128,'case'=4] {'sub'}, use_global_device_ids=true, to_apply=%region_5.7 | all-reduce | flops 32 | bytes 256 | tf_op jit(solution)/shard_map/psum | solution.py:79
  633.6 4.4 collective-permute-start.18
  644.5 4.7 collective-permute-start.19
  656.3 7.6 collective-permute-start.21
  664.0 4.7 collective-permute-start.22
  673.7 4.4 collective-permute-start.23
  685.4 253.3 %all-reduce.1 = (f32[16]{0:T(128)S(1)}, f32[16]{0:T(128)S(1)}) all-reduce(f32[16]{0:T(128)S(1)} %get-tuple-element.45, f32[16]{0:T(128)S(1)} %fusion.10), channel_id=1, replica_groups=mesh['sub'=128,'case'=4] {'sub'}, use_global_device_ids=true, to_apply=%region_9.11 | all-reduce | flops 32 | bytes 256 | tf_op jit(solution)/shard_map/psum | solution.py:79
  941.5 4.5 collective-permute-start.26
  952.4 4.7 collective-permute-start.27
  964.2 8.0 collective-permute-start.29
  974.3 4.7 collective-permute-start.30
  983.7 4.7 collective-permute-start.31
  995.3 249.0 %all-reduce = (f32[16]{0:T(128)S(1)}, f32[16]{0:T(128)S(1)}) all-reduce(f32[16]{0:T(128)S(1)} %get-tuple-element.47, f32[16]{0:T(128)S(1)} %fusion.11), channel_id=1, replica_groups=mesh['sub'=128,'case'=4] {'sub'}, use_global_device_ids=true, to_apply=%region_13.15 | all-reduce | flops 32 | bytes 256 | tf_op jit(solution)/shard_map/psum | solution.py:79
  1245.1 9.1 psum.71
  (254 shorter events, 128.7 us)
Async XLA Ops:
  1.6 22.8 %collective-permute-start.2 = (bf16[16,4,128]{2,1,0:T(4,128)(2,1)S(1)}, bf16[16,4,128]{2,1,0:T(4,128)(2,1)S(1)}, u32[]{:S(2)}, u32[]{:S(2)}) collective-permute-start(bf16[16,4,128]{2,1,0:T(4,128)(2,1)S(1)} %slice.284), channel_id=1, source_target_pairs={{0,256},{4,260},{8,264},{12,268},{16,272},{20,276},{24,280},{28,28... | collective-permute-start | bytes 49160 | tf_op jit(solution)/shard_map/ppermute | solution.py:17
  10.0 8.4 collective-permute-start.1
  13.0 10.7 collective-permute-start
  26.8 8.4 collective-permute-start.3
  38.6 16.1 %collective-permute-start.5 = (f32[16,128]{0,1:T(8,128)S(1)}, f32[16,128]{0,1:T(8,128)S(1)}, u32[]{:S(2)}, u32[]{:S(2)}) collective-permute-start(f32[16,128]{0,1:T(8,128)S(1)} %bitcast.356), channel_id=1, source_target_pairs={{0,508},{4,0},{8,4},{12,8},{16,12},{20,16},{24,20},{28,24},{32,28}... | collective-permute-start | bytes 24584 | tf_op jit(solution)/shard_map/ppermute | solution.py:17
  48.0 8.8 collective-permute-start.6
  57.8 8.4 collective-permute-start.7
  323.0 10.5 collective-permute-start.9
  325.6 9.9 collective-permute-start.10
  336.5 8.4 collective-permute-start.11
  348.3 14.5 %collective-permute-start.13 = (f32[16,128]{0,1:T(8,128)S(1)}, f32[16,128]{0,1:T(8,128)S(1)}, u32[]{:S(2)}, u32[]{:S(2)}) collective-permute-start(f32[16,128]{0,1:T(8,128)S(1)} %bitcast.357), channel_id=1, source_target_pairs={{0,508},{4,0},{8,4},{12,8},{16,12},{20,16},{24,20},{28,24},{32,28}... | collective-permute-start | bytes 24584 | tf_op jit(solution)/shard_map/ppermute | solution.py:17
  356.0 8.8 collective-permute-start.14
  365.8 8.4 collective-permute-start.15
  630.9 10.5 collective-permute-start.17
  633.6 9.9 collective-permute-start.18
  644.5 8.4 collective-permute-start.19
  656.3 14.5 %collective-permute-start.21 = (f32[16,128]{0,1:T(8,128)S(1)}, f32[16,128]{0,1:T(8,128)S(1)}, u32[]{:S(2)}, u32[]{:S(2)}) collective-permute-start(f32[16,128]{0,1:T(8,128)S(1)} %bitcast.358), channel_id=1, source_target_pairs={{0,508},{4,0},{8,4},{12,8},{16,12},{20,16},{24,20},{28,24},{32,28}... | collective-permute-start | bytes 24584 | tf_op jit(solution)/shard_map/ppermute | solution.py:17
  664.0 8.8 collective-permute-start.22
  673.7 8.4 collective-permute-start.23
  938.9 10.5 collective-permute-start.25
  941.5 9.9 collective-permute-start.26
  952.4 8.4 collective-permute-start.27
  964.2 14.8 %collective-permute-start.29 = (f32[16,128]{0,1:T(8,128)S(1)}, f32[16,128]{0,1:T(8,128)S(1)}, u32[]{:S(2)}, u32[]{:S(2)}) collective-permute-start(f32[16,128]{0,1:T(8,128)S(1)} %bitcast.359), channel_id=1, source_target_pairs={{0,508},{4,0},{8,4},{12,8},{16,12},{20,16},{24,20},{28,24},{32,28}... | collective-permute-start | bytes 24584 | tf_op jit(solution)/shard_map/ppermute | solution.py:17
  974.3 8.4 collective-permute-start.30
  (12 other events, 714.1 us)
where the time goes:
time: 1260 us
  blocking collectives  1020 us (81%)
  starting transfers between devices  142 us (11%)
  waiting for transfers between devices  40.1 us (3%)
  matrix products  33.9 us (3%)
  local copies, waits for them, and re-layouts  15 us (1%)
    psum x4, blocking collectives, on_device(): grad_norms = lax.psum(jnp.sum(gradient * gradient, axis=1), 'sub')  1010 us
    ppermute x32, starting transfers between devices, shifted(): lax.ppermute(value, axis, [(i, (i + by) % devices) for i in range(devices)])  142 us
    ppermute x32, waiting for transfers between devices, shifted(): lax.ppermute(value, axis, [(i, (i + by) % devices) for i in range(devices)])  40.1 us
    dot_general x8, matrix products, apply_operator(): jnp.dot(vector.astype(jnp.bfloat16), dual_op, preferred_element_type=jnp....  25.4 us
  transfers between devices with their start and end apart: 32, of which 16 were waited for; matrix products, arithmetic and copies ran while one was open for 1% of the time, Pallas kernels for 0%

commit v1 on v0

v1 whole, which is shorter than its diff:
```python
import jax
import jax.numpy as jnp
from jax import lax
from jax.sharding import PartitionSpec as P

M = 1536
BLK = 128
ITERS = 4
CASES = 16

penalty = 0.5


def shifted(value, axis, by):
    devices = lax.axis_size(axis)
    return lax.ppermute(value, axis, [(i, (i + by) % devices) for i in range(devices)])


def two_parts(value):
    high = value.astype(jnp.bfloat16)
    low = (value - high.astype(jnp.float32)).astype(jnp.bfloat16)
    return jnp.concatenate([high, low], axis=-2)


def joined(product):
    rows = product.shape[-2] // 2
    return product[..., :rows, :] + product[..., rows:, :]


def times(value, matrix):
    return joined(jnp.matmul(two_parts(value), matrix, preferred_element_type=jnp.float32))


def times_transposed(value, matrix):
    return joined(
        jnp.einsum("kcf,kef->kce", two_parts(value), matrix, preferred_element_type=jnp.float32)
    )


def blocks_of(rows):
    return jnp.stack([rows[:, k * BLK : (k + 1) * BLK] for k in range(rows.shape[1] // BLK)])


def jump_of(slave, own, onehot, active, mortar):
    selected = jnp.einsum("kb,bce->kce", onehot, slave, precision=lax.Precision.HIGHEST)
    return (times(selected, mortar) - own) * active[:, None, None]


def reply_of(jump, onehot, mortar):
    rows = times_transposed(jump, mortar)
    return jnp.einsum("kb,kce->bce", onehot, rows, precision=lax.Precision.HIGHEST)


def slot_terms(ids, count):
    onehot = (ids[:, None] == jnp.arange(4, dtype=ids.dtype)[None, :]).astype(jnp.float32)
    active = (jnp.arange(4, dtype=count.dtype) < count).astype(jnp.float32)
    return onehot, active


def summed_over(value, axis):
    devices = lax.axis_size(axis)
    copies = jnp.broadcast_to(value[None], (devices,) + value.shape)
    return lax.all_to_all(copies, axis, 0, 0).sum(0)


def on_device(multipliers, right_side, dual_ops, glue_match, mortar, contact_ids, contact_count):
    half_axis = lax.axis_size("sub") // 2
    mortar = mortar[0]
    onehot, active = slot_terms(contact_ids[0], contact_count[0])

    meta = jnp.concatenate([contact_ids[0], contact_count]).astype(jnp.bfloat16)
    meta = jnp.zeros((16, BLK), jnp.bfloat16).at[0, :5].set(meta)
    contact = multipliers[:, 2 * BLK : 6 * BLK]
    packed = jnp.concatenate(
        [
            blocks_of(contact).astype(jnp.bfloat16).reshape(4 * CASES, BLK),
            mortar.reshape(4 * BLK, BLK),
            meta,
        ]
    )
    packed = shifted(packed, "sub", half_axis)
    mate = packed[: 4 * CASES].astype(jnp.float32).reshape(4, CASES, BLK)
    mate_mortar = packed[4 * CASES : 4 * CASES + 4 * BLK].reshape(4, BLK, BLK)
    mate_meta = packed[4 * CASES + 4 * BLK].astype(jnp.int32)
    mate_onehot, mate_active = slot_terms(mate_meta[:4], mate_meta[4])

    lanes = jnp.arange(BLK, dtype=jnp.int32)
    pick = (lanes[None, :, None] == glue_match[0][:, None, :]).astype(jnp.bfloat16)

    x = multipliers
    prev_x = shifted(multipliers[:, BLK : 2 * BLK], "sub", 1)
    next_x = shifted(multipliers[:, :BLK], "sub", -1)
    total_norm = None
    for iteration in range(ITERS):
        local = jnp.dot(x.astype(jnp.bfloat16), dual_ops, preferred_element_type=jnp.float32)
        faces = [x[:, :BLK] - times(prev_x, pick[0]), x[:, BLK : 2 * BLK] - times(next_x, pick[1])]
        own = blocks_of(x[:, 2 * BLK : 6 * BLK])
        jump = jump_of(mate, own, onehot, active, mortar)
        mate_jump = jump_of(own, mate, mate_onehot, mate_active, mate_mortar)
        part = reply_of(mate_jump, mate_onehot, mate_mortar) - jump
        correction = jnp.concatenate(
            [penalty * face for face in faces]
            + [part[k] for k in range(4)]
            + [jnp.zeros((CASES, 6 * BLK), jnp.float32)],
            axis=1,
        )
        gradient = local + correction - right_side

        own_g = blocks_of(gradient[:, 2 * BLK : 6 * BLK])
        mate_g = shifted(own_g.astype(jnp.bfloat16), "sub", half_axis).astype(jnp.float32)
        prev_g = shifted(gradient[:, BLK : 2 * BLK], "sub", 1)
        next_g = shifted(gradient[:, :BLK], "sub", -1)
        image = jnp.dot(
            gradient.astype(jnp.bfloat16), dual_ops, preferred_element_type=jnp.float32
        )
        first, second = gradient[:, :BLK], gradient[:, BLK : 2 * BLK]
        jump = jump_of(mate_g, own_g, onehot, active, mortar)
        face_curve = penalty * (first * first + second * second) - first * times(prev_g, pick[0])
        curve = (
            jnp.sum(gradient * image, axis=1)
            + jnp.sum(face_curve, axis=1)
            + jnp.sum(jump * jump, axis=(0, 2))
        )
        norm = jnp.sum(gradient * gradient, axis=1)
        both = jnp.concatenate([norm, curve, jnp.zeros((BLK - 2 * CASES,), jnp.float32)])
        both = summed_over(both.reshape(1, BLK), "sub")[0]
        norm, curve = both[:CASES], both[CASES : 2 * CASES]
        step = (norm / curve)[:, None]
        moved = x - step * gradient
        x = jnp.concatenate(
            [
                moved[:, : 2 * BLK],
                jnp.maximum(moved[:, 2 * BLK : 6 * BLK], 0.0),
                moved[:, 6 * BLK :],
            ],
            axis=1,
        )
        if iteration < ITERS - 1:
            mate = jnp.maximum(mate - step[None] * mate_g, 0.0)
            prev_x = prev_x - step * prev_g
            next_x = next_x - step * next_g
    total_norm = summed_over(jnp.full((1, BLK), jnp.sum(norm), jnp.float32), "case")
    return (x, jnp.sqrt(total_norm[0, :1]))


def solution(mesh):
    in_specs = (
        P("case", "sub"),
        P("case", "sub"),
        P("sub", None),
        P("sub", None, None),
        P("sub", None, None, None),
        P("sub", None),
        P("sub"),
    )
    out_specs = (P("case", "sub"), P())
    return jax.shard_map(
        on_device, mesh=mesh, in_specs=in_specs, out_specs=out_specs, check_vma=False
    )
```

time: 1260 us -> 219 us (0.17)
  blocking collectives: 1020 us -> 22.6 us
  starting transfers between devices: 142 us -> 90.7 us
  waiting for transfers between devices: 40.1 us -> 55.3 us
    psum x5 -> x0, blocking collectives: 1020 us -> none  [the longest x4 1010 us: on_device(): grad_norms = lax.psum(jnp.sum(gradient * gradient, axis=1), 'sub')]
    ppermute x32 -> x14, starting transfers between devices: 142 us -> 50.3 us  [shifted(): lax.ppermute(value, axis, [(i, (i + by) % devices) for i in range(devices)])]
    all_to_all x0 -> x4, starting transfers between devices: none -> 40.3 us  [summed_over(): return lax.all_to_all(copies, axis, 0, 0).sum(0)]
    all_to_all x0 -> x4, waiting for transfers between devices: none -> 29.6 us  [summed_over(): return lax.all_to_all(copies, axis, 0, 0).sum(0)]
    all_to_all x0 -> x1, blocking collectives: none -> 22.6 us  [summed_over(): return lax.all_to_all(copies, axis, 0, 0).sum(0)]
    ppermute x32 -> x14, waiting for transfers between devices: 40.1 us -> 25.7 us  [shifted(): lax.ppermute(value, axis, [(i, (i + by) % devices) for i in range(devices)])]
    dot_general x40 -> x52, matrix products: 33.9 us -> 32 us  [the longest x4 12.7 us: on_device(): jnp.dot(x.astype(jnp.bfloat16), dual_ops, preferred_element_type=jnp.floa...]
  transfers between devices with their start and end apart: 32 -> 18, of which waited for: 16 -> 14; matrix products, arithmetic and copies ran while one was open for 1% -> 9% of each run, Pallas kernels for 0% -> 0%
where the time goes in v1:
time: 219 us; the launch traced here: 218 us
  starting transfers between devices  90.7 us (41%)
  waiting for transfers between devices  55.3 us (25%)
  matrix products  32 us (15%)
  blocking collectives  22.6 us (10%)
  other arithmetic  9.4 us (4%)
  local copies, waits for them, and re-layouts  4.9 us (2%)
  between operations  3.47 us (2%)
    ppermute x14, starting transfers between devices, shifted(): lax.ppermute(value, axis, [(i, (i + by) % devices) for i in range(devices)])  50.3 us
    all_to_all x4, starting transfers between devices, summed_over(): return lax.all_to_all(copies, axis, 0, 0).sum(0)  40.3 us
    all_to_all x4, waiting for transfers between devices, summed_over(): return lax.all_to_all(copies, axis, 0, 0).sum(0)  29.6 us
    ppermute x14, waiting for transfers between devices, shifted(): lax.ppermute(value, axis, [(i, (i + by) % devices) for i in range(devices)])  25.7 us
    all_to_all x1, blocking collectives, summed_over(): return lax.all_to_all(copies, axis, 0, 0).sum(0)  22.6 us
    dot_general x4, matrix products, on_device(): jnp.dot(x.astype(jnp.bfloat16), dual_ops, preferred_element_type=jnp.floa...  12.7 us
    dot_general x4, matrix products, on_device(): jnp.dot(gradient.astype(jnp.bfloat16), dual_ops, preferred_element_type=j...  10.3 us
  transfers between devices with their start and end apart: 18, of which 14 were waited for; matrix products, arithmetic and copies ran while one was open for 9% of the time, Pallas kernels for 0%

profile of v1, /device:TPU:1, one launch (start us, length us, event | category | flops | bytes accessed | tf_op | source)
XLA Modules:
  0.0 218.3 jit_solution(10099712684369474443)
XLA Ops:
  1.5 5.5 %collective-permute-start = (f32[16,128]{1,0:T(8,128)S(1)}, f32[16,128]{1,0:T(8,128)S(1)}, u32[]{:S(2)}, u32[]{:S(2)}) collective-permute-start(f32[16,128]{1,0:T(8,128)S(1)} %slice.528), channel_id=1, source_target_pairs={{0,4},{4,8},{8,12},{12,16},{16,20},{20,24},{24,28},{28,32},{32,36}... | collective-permute-start | bytes 24584 | tf_op jit(solution)/shard_map/ppermute | solution.py:16
  11.9 8.6 %collective-permute-start.1 = (f32[16,128]{1,0:T(8,128)S(1)}, f32[16,128]{1,0:T(8,128)S(1)}, u32[]{:S(2)}, u32[]{:S(2)}) collective-permute-start(f32[16,128]{1,0:T(8,128)S(1)} %get-tuple-element.103), channel_id=1, source_target_pairs={{0,508},{4,0},{8,4},{12,8},{16,12},{20,16},{24,20},{28,24},{32,28}... | collective-permute-start | bytes 24584 | tf_op jit(solution)/shard_map/ppermute | solution.py:16
  21.5 4.4 %collective-permute-start.2 = (bf16[592,128]{1,0:T(8,128)(2,1)S(1)}, bf16[592,128]{1,0:T(8,128)(2,1)S(1)}, u32[]{:S(2)}, u32[]{:S(2)}) collective-permute-start(bf16[592,128]{1,0:T(8,128)(2,1)S(1)} %pad_maximum_fusion), channel_id=1, source_target_pairs={{0,256},{4,260},{8,264},{12,268},{16,272},{20,276},{24,280},{28,28... | collective-permute-start | bytes 454664 | tf_op jit(solution)/shard_map/ppermute | solution.py:16
  26.8 8.4 %collective-permute-done.2 = bf16[592,128]{1,0:T(8,128)(2,1)S(1)} collective-permute-done((bf16[592,128]{1,0:T(8,128)(2,1)S(1)}, bf16[592,128]{1,0:T(8,128)(2,1)S(1)}, u32[]{:S(2)}, u32[]{:S(2)}) %collective-permute-start.2) | collective-permute-done | bytes 151584 | tf_op jit(solution)/shard_map/ppermute | solution.py:16
  39.5 3.2 %multiply_reduce_fusion.3 = (f32[16]{0:T(128)S(1)}, f32[16,1536]{1,0:T(8,128)S(1)}) fusion(f32[16,1536]{1,0:T(8,128)} %param.10, f32[16,1536]{1,0:T(8,128)S(1)} %constant_dynamic-update-slice_fusion, bf16[1536,1536]{1,0:T(8,128)(2,1)} %param.11, f32[16,1536]{1,0:T(8,128)} %param.9), kind=kOutput, calls=%fused_computation.45 | convolution fusion | flops 75620336 | bytes 5111872 | tf_op jit(solution)/shard_map/dot_general | solution.py:95
  47.4 4.2 %collective-permute-start.4 = (bf16[4,16,128]{2,1,0:T(8,128)(2,1)S(1)}, bf16[4,16,128]{2,1,0:T(8,128)(2,1)S(1)}, u32[]{:S(2)}, u32[]{:S(2)}) collective-permute-start(bf16[4,16,128]{2,1,0:T(8,128)(2,1)S(1)} %fusion.128), channel_id=1, source_target_pairs={{0,256},{4,260},{8,264},{12,268},{16,272},{20,276},{24,280},{28,28... | collective-permute-start | bytes 49160 | tf_op jit(solution)/shard_map/ppermute | solution.py:16
  52.4 3.4 %collective-permute-done.4 = bf16[4,16,128]{2,1,0:T(8,128)(2,1)S(1)} collective-permute-done((bf16[4,16,128]{2,1,0:T(8,128)(2,1)S(1)}, bf16[4,16,128]{2,1,0:T(8,128)(2,1)S(1)}, u32[]{:S(2)}, u32[]{:S(2)}) %collective-permute-start.4) | collective-permute-done | bytes 16416 | tf_op jit(solution)/shard_map/ppermute | solution.py:16
  57.1 13.2 %all-to-all-start = ((f32[128,1,128]{2,1,0:T(1,128)}), f32[128,1,128]{2,1,0:T(1,128)S(1)}, u32[]{:S(2)}, u32[]{:S(2)}) async-start(f32[128,1,128]{2,1,0:T(1,128)} %broadcast_in_dim.8), calls=%async_computation | async-start | bytes 131072 | tf_op jit(solution)/shard_map/all_to_all | solution.py:63
  73.1 8.7 %all-to-all-done = f32[128,1,128]{2,1,0:T(1,128)S(1)} async-done(((f32[128,1,128]{2,1,0:T(1,128)}), f32[128,1,128]{2,1,0:T(1,128)S(1)}, u32[]{:S(2)}, u32[]{:S(2)}) %all-to-all-start) | async-done | bytes 65568 | tf_op jit(solution)/shard_map/all_to_all | solution.py:63
  83.9 3.2 %multiply_reduce_fusion.2 = (f32[16]{0:T(128)S(1)}, f32[16,1536]{1,0:T(8,128)S(1)}) fusion(f32[16,1536]{1,0:T(8,128)S(1)} %copy-done.2, f32[16,1536]{1,0:T(8,128)S(1)} %constant_dynamic-update-slice_fusion.7, bf16[1536,1536]{1,0:T(8,128)(2,1)} %param.11, f32[16,768]{1,0:T(8,128)S(1)} %slice.707, f32[16,512]{1,0:T(8,128)S(1)} %slice_maximum_fusion.3, ...), kind=kOutput, calls=%fused_computation.43 | convolution fusion | flops 75743216 | bytes 5111872 | tf_op jit(solution)/shard_map/dot_general | solution.py:95
  93.8 3.2 %fusion.5 = f32[16]{0:T(128)S(1)} fusion(f32[16,1536]{1,0:T(8,128)S(1)} %get-tuple-element.134, bf16[1536,1536]{1,0:T(8,128)(2,1)} %param.11), kind=kOutput, calls=%fused_computation.13 | convolution fusion | flops 75571184 | bytes 4816960 | tf_op jit(solution)/shard_map/dot_general | solution.py:113
  100.7 11.5 %all-to-all-start.1 = ((f32[128,1,128]{2,1,0:T(1,128)}), f32[128,1,128]{2,1,0:T(1,128)S(1)}, u32[]{:S(2)}, u32[]{:S(2)}) async-start(f32[128,1,128]{2,1,0:T(1,128)} %broadcast_in_dim.9), calls=%async_computation.1 | async-start | bytes 131072 | tf_op jit(solution)/shard_map/all_to_all | solution.py:63
  112.2 2.9 %collective-permute-start.8 = (f32[16,128]{1,0:T(8,128)S(1)}, f32[16,128]{1,0:T(8,128)S(1)}, u32[]{:S(2)}, u32[]{:S(2)}) collective-permute-start(f32[16,128]{1,0:T(8,128)S(1)} %get-tuple-element.87), channel_id=1, source_target_pairs={{0,508},{4,0},{8,4},{12,8},{16,12},{20,16},{24,20},{28,24},{32,28}... | collective-permute-start | bytes 24584 | tf_op jit(solution)/shard_map/ppermute | solution.py:16
  115.1 8.7 %all-to-all-done.1 = f32[128,1,128]{2,1,0:T(1,128)S(1)} async-done(((f32[128,1,128]{2,1,0:T(1,128)}), f32[128,1,128]{2,1,0:T(1,128)S(1)}, u32[]{:S(2)}, u32[]{:S(2)}) %all-to-all-start.1) | async-done | bytes 65568 | tf_op jit(solution)/shard_map/all_to_all | solution.py:63
  125.9 3.2 %multiply_reduce_fusion.1 = (f32[16]{0:T(128)S(1)}, f32[16,1536]{1,0:T(8,128)S(1)}) fusion(f32[16,1536]{1,0:T(8,128)S(1)} %copy-done.2, f32[16,1536]{1,0:T(8,128)S(1)} %constant_dynamic-update-slice_fusion.14, bf16[1536,1536]{1,0:T(8,128)(2,1)} %param.11, f32[16,768]{1,0:T(8,128)S(1)} %slice.740, f32[16,512]{1,0:T(8,128)S(1)} %slice_maximum_fusion.2, ...), kind=kOutput, calls=%fused_computation.41 | convolution fusion | flops 75743216 | bytes 5111872 | tf_op jit(solution)/shard_map/dot_general | solution.py:95
  135.8 3.2 %fusion.6 = f32[16]{0:T(128)S(1)} fusion(f32[16,1536]{1,0:T(8,128)S(1)} %get-tuple-element.136, bf16[1536,1536]{1,0:T(8,128)(2,1)} %param.11), kind=kOutput, calls=%fused_computation.14 | convolution fusion | flops 75571184 | bytes 4816960 | tf_op jit(solution)/shard_map/dot_general | solution.py:113
  142.7 11.7 %all-to-all-start.2 = ((f32[128,1,128]{2,1,0:T(1,128)}), f32[128,1,128]{2,1,0:T(1,128)S(1)}, u32[]{:S(2)}, u32[]{:S(2)}) async-start(f32[128,1,128]{2,1,0:T(1,128)} %broadcast_in_dim.10), calls=%async_computation.2 | async-start | bytes 131072 | tf_op jit(solution)/shard_map/all_to_all | solution.py:63
  154.4 2.9 %collective-permute-start.11 = (f32[16,128]{1,0:T(8,128)S(1)}, f32[16,128]{1,0:T(8,128)S(1)}, u32[]{:S(2)}, u32[]{:S(2)}) collective-permute-start(f32[16,128]{1,0:T(8,128)S(1)} %get-tuple-element.81), channel_id=1, source_target_pairs={{0,508},{4,0},{8,4},{12,8},{16,12},{20,16},{24,20},{28,24},{32,28}... | collective-permute-start | bytes 24584 | tf_op jit(solution)/shard_map/ppermute | solution.py:16
  157.3 8.7 %all-to-all-done.2 = f32[128,1,128]{2,1,0:T(1,128)S(1)} async-done(((f32[128,1,128]{2,1,0:T(1,128)}), f32[128,1,128]{2,1,0:T(1,128)S(1)}, u32[]{:S(2)}, u32[]{:S(2)}) %all-to-all-start.2) | async-done | bytes 65568 | tf_op jit(solution)/shard_map/all_to_all | solution.py:63
  168.1 3.2 %multiply_reduce_fusion = (f32[16]{0:T(128)S(1)}, f32[16,1536]{1,0:T(8,128)S(1)}) fusion(f32[16,1536]{1,0:T(8,128)S(1)} %copy-done.2, f32[16,1536]{1,0:T(8,128)S(1)} %constant_dynamic-update-slice_fusion.21, bf16[1536,1536]{1,0:T(8,128)(2,1)} %param.11, f32[16,768]{1,0:T(8,128)S(1)} %slice.773, f32[16,512]{1,0:T(8,128)S(1)} %slice_maximum_fusion.1, ...), kind=kOutput, calls=%fused_computation.39 | convolution fusion | flops 75743216 | bytes 5111872 | tf_op jit(solution)/shard_map/dot_general | solution.py:95
  178.0 3.2 %fusion.7 = f32[16]{0:T(128)S(1)} fusion(f32[16,1536]{1,0:T(8,128)S(1)} %get-tuple-element.138, bf16[1536,1536]{1,0:T(8,128)(2,1)} %param.11), kind=kOutput, calls=%fused_computation.15 | convolution fusion | flops 75571184 | bytes 4816960 | tf_op jit(solution)/shard_map/dot_general | solution.py:113
  184.3 22.6 %all_to_all.25 = f32[128,1,128]{2,1,0:T(1,128)S(1)} all-to-all(f32[128,1,128]{2,1,0:T(1,128)S(1)} %broadcast_in_dim.11), channel_id=1, replica_groups=mesh['sub'=128,'case'=4] {'sub'}, dimensions={0} | all-to-all | bytes 131072 | tf_op jit(solution)/shard_map/all_to_all | solution.py:63
  208.9 4.0 %all-to-all-start.4 = ((f32[4,1,128]{2,1,0:T(1,128)}), f32[4,1,128]{2,1,0:T(1,128)S(1)}, u32[]{:S(2)}, u32[]{:S(2)}) async-start(f32[4,1,128]{2,1,0:T(1,128)} %broadcast_in_dim_broadcast_in_dim_broadcast_in_dim.3), calls=%async_computation.4 | async-start | bytes 4096 | tf_op jit(solution)/shard_map/all_to_all | solution.py:63
  213.5 3.5 %all-to-all-done.4 = f32[4,1,128]{2,1,0:T(1,128)S(1)} async-done(((f32[4,1,128]{2,1,0:T(1,128)}), f32[4,1,128]{2,1,0:T(1,128)S(1)}, u32[]{:S(2)}, u32[]{:S(2)}) %all-to-all-start.4) | async-done | bytes 2080 | tf_op jit(solution)/shard_map/all_to_all | solution.py:63
  (215 shorter events, 59.8 us)
Async XLA Ops:
  0.6 50.9 %copy-start = (bf16[1536,1536]{1,0:T(8,128)(2,1)S(1)}, bf16[1536,1536]{1,0:T(8,128)(2,1)}, u32[]{:S(2)}) copy-start(bf16[1536,1536]{1,0:T(8,128)(2,1)} %param.11) | copy-start | bytes 14155780
  1.5 9.5 %collective-permute-start = (f32[16,128]{1,0:T(8,128)S(1)}, f32[16,128]{1,0:T(8,128)S(1)}, u32[]{:S(2)}, u32[]{:S(2)}) collective-permute-start(f32[16,128]{1,0:T(8,128)S(1)} %slice.528), channel_id=1, source_target_pairs={{0,4},{4,8},{8,12},{12,16},{16,20},{20,24},{24,28},{28,32},{32,36}... | collective-permute-start | bytes 24584 | tf_op jit(solution)/shard_map/ppermute | solution.py:16
  11.9 14.0 %collective-permute-start.1 = (f32[16,128]{1,0:T(8,128)S(1)}, f32[16,128]{1,0:T(8,128)S(1)}, u32[]{:S(2)}, u32[]{:S(2)}) collective-permute-start(f32[16,128]{1,0:T(8,128)S(1)} %get-tuple-element.103), channel_id=1, source_target_pairs={{0,508},{4,0},{8,4},{12,8},{16,12},{20,16},{24,20},{28,24},{32,28}... | collective-permute-start | bytes 24584 | tf_op jit(solution)/shard_map/ppermute | solution.py:16
  21.5 13.7 %collective-permute-start.2 = (bf16[592,128]{1,0:T(8,128)(2,1)S(1)}, bf16[592,128]{1,0:T(8,128)(2,1)S(1)}, u32[]{:S(2)}, u32[]{:S(2)}) collective-permute-start(bf16[592,128]{1,0:T(8,128)(2,1)S(1)} %pad_maximum_fusion), channel_id=1, source_target_pairs={{0,256},{4,260},{8,264},{12,268},{16,272},{20,276},{24,280},{28,28... | collective-permute-start | bytes 454664 | tf_op jit(solution)/shard_map/ppermute | solution.py:16
  39.4 16.4 %copy-start.4 = (s32[1,4]{1,0:T(1,128)S(1)}, s32[1,4]{1,0:T(1,128)}, u32[]{:S(2)}) copy-start(s32[1,4]{1,0:T(1,128)} %param.14) | copy-start | bytes 52
  39.4 16.6 %copy-start.1 = (bf16[1,4,128,128]{3,2,1,0:T(8,128)(2,1)S(1)}, bf16[1,4,128,128]{3,2,1,0:T(8,128)(2,1)}, u32[]{:S(2)}) copy-start(bf16[1,4,128,128]{3,2,1,0:T(8,128)(2,1)} %param.13) | copy-start | bytes 393220
  39.5 42.5 %copy-start.3 = (f32[16,1536]{1,0:T(8,128)S(1)}, f32[16,1536]{1,0:T(8,128)}, u32[]{:S(2)}) copy-start(f32[16,1536]{1,0:T(8,128)} %param.9) | copy-start | bytes 294916
  42.7 41.2 %copy-start.2 = (f32[16,1536]{1,0:T(8,128)S(1)}, f32[16,1536]{1,0:T(8,128)}, u32[]{:S(2)}) copy-start(f32[16,1536]{1,0:T(8,128)} %param.10) | copy-start | bytes 294916
  42.7 4.4 %collective-permute-start.3 = (f32[16,128]{1,0:T(8,128)S(1)}, f32[16,128]{1,0:T(8,128)S(1)}, u32[]{:S(2)}, u32[]{:S(2)}) collective-permute-start(f32[16,128]{1,0:T(8,128)S(1)} %slice.696), channel_id=1, source_target_pairs={{0,4},{4,8},{8,12},{12,16},{16,20},{20,24},{24,28},{28,32},{32,36}... | collective-permute-start | bytes 24584 | tf_op jit(solution)/shard_map/ppermute | solution.py:16
  47.4 8.4 %collective-permute-start.4 = (bf16[4,16,128]{2,1,0:T(8,128)(2,1)S(1)}, bf16[4,16,128]{2,1,0:T(8,128)(2,1)S(1)}, u32[]{:S(2)}, u32[]{:S(2)}) collective-permute-start(bf16[4,16,128]{2,1,0:T(8,128)(2,1)S(1)} %fusion.128), channel_id=1, source_target_pairs={{0,256},{4,260},{8,264},{12,268},{16,272},{20,276},{24,280},{28,28... | collective-permute-start | bytes 49160 | tf_op jit(solution)/shard_map/ppermute | solution.py:16
  57.1 24.7 %all-to-all-start = ((f32[128,1,128]{2,1,0:T(1,128)}), f32[128,1,128]{2,1,0:T(1,128)S(1)}, u32[]{:S(2)}, u32[]{:S(2)}) async-start(f32[128,1,128]{2,1,0:T(1,128)} %broadcast_in_dim.8), calls=%async_computation | async-start | bytes 131072 | tf_op jit(solution)/shard_map/all_to_all | solution.py:63
  70.3 13.1 %collective-permute-start.5 = (f32[16,128]{1,0:T(8,128)S(1)}, f32[16,128]{1,0:T(8,128)S(1)}, u32[]{:S(2)}, u32[]{:S(2)}) collective-permute-start(f32[16,128]{1,0:T(8,128)S(1)} %get-tuple-element.93), channel_id=1, source_target_pairs={{0,508},{4,0},{8,4},{12,8},{16,12},{20,16},{24,20},{28,24},{32,28}... | collective-permute-start | bytes 24584 | tf_op jit(solution)/shard_map/ppermute | solution.py:16
  87.1 3.6 %collective-permute-start.6 = (f32[16,128]{1,0:T(8,128)S(1)}, f32[16,128]{1,0:T(8,128)S(1)}, u32[]{:S(2)}, u32[]{:S(2)}) collective-permute-start(f32[16,128]{1,0:T(8,128)S(1)} %slice.729), channel_id=1, source_target_pairs={{0,4},{4,8},{8,12},{12,16},{16,20},{20,24},{24,28},{28,32},{32,36}... | collective-permute-start | bytes 24584 | tf_op jit(solution)/shard_map/ppermute | solution.py:16
  91.0 8.4 %collective-permute-start.7 = (bf16[4,16,128]{2,1,0:T(8,128)(2,1)S(1)}, bf16[4,16,128]{2,1,0:T(8,128)(2,1)S(1)}, u32[]{:S(2)}, u32[]{:S(2)}) collective-permute-start(bf16[4,16,128]{2,1,0:T(8,128)(2,1)S(1)} %fusion.127), channel_id=1, source_target_pairs={{0,256},{4,260},{8,264},{12,268},{16,272},{20,276},{24,280},{28,28... | collective-permute-start | bytes 49160 | tf_op jit(solution)/shard_map/ppermute | solution.py:16
  100.7 23.1 %all-to-all-start.1 = ((f32[128,1,128]{2,1,0:T(1,128)}), f32[128,1,128]{2,1,0:T(1,128)S(1)}, u32[]{:S(2)}, u32[]{:S(2)}) async-start(f32[128,1,128]{2,1,0:T(1,128)} %broadcast_in_dim.9), calls=%async_computation.1 | async-start | bytes 131072 | tf_op jit(solution)/shard_map/all_to_all | solution.py:63
  112.2 13.2 %collective-permute-start.8 = (f32[16,128]{1,0:T(8,128)S(1)}, f32[16,128]{1,0:T(8,128)S(1)}, u32[]{:S(2)}, u32[]{:S(2)}) collective-permute-start(f32[16,128]{1,0:T(8,128)S(1)} %get-tuple-element.87), channel_id=1, source_target_pairs={{0,508},{4,0},{8,4},{12,8},{16,12},{20,16},{24,20},{28,24},{32,28}... | collective-permute-start | bytes 24584 | tf_op jit(solution)/shard_map/ppermute | solution.py:16
  129.1 3.6 %collective-permute-start.9 = (f32[16,128]{1,0:T(8,128)S(1)}, f32[16,128]{1,0:T(8,128)S(1)}, u32[]{:S(2)}, u32[]{:S(2)}) collective-permute-start(f32[16,128]{1,0:T(8,128)S(1)} %slice.762), channel_id=1, source_target_pairs={{0,4},{4,8},{8,12},{12,16},{16,20},{20,24},{24,28},{28,32},{32,36}... | collective-permute-start | bytes 24584 | tf_op jit(solution)/shard_map/ppermute | solution.py:16
  133.0 8.4 %collective-permute-start.10 = (bf16[4,16,128]{2,1,0:T(8,128)(2,1)S(1)}, bf16[4,16,128]{2,1,0:T(8,128)(2,1)S(1)}, u32[]{:S(2)}, u32[]{:S(2)}) collective-permute-start(bf16[4,16,128]{2,1,0:T(8,128)(2,1)S(1)} %fusion.126), channel_id=1, source_target_pairs={{0,256},{4,260},{8,264},{12,268},{16,272},{20,276},{24,280},{28,28... | collective-permute-start | bytes 49160 | tf_op jit(solution)/shard_map/ppermute | solution.py:16
  142.7 23.3 %all-to-all-start.2 = ((f32[128,1,128]{2,1,0:T(1,128)}), f32[128,1,128]{2,1,0:T(1,128)S(1)}, u32[]{:S(2)}, u32[]{:S(2)}) async-start(f32[128,1,128]{2,1,0:T(1,128)} %broadcast_in_dim.10), calls=%async_computation.2 | async-start | bytes 131072 | tf_op jit(solution)/shard_map/all_to_all | solution.py:63
  154.4 13.2 %collective-permute-start.11 = (f32[16,128]{1,0:T(8,128)S(1)}, f32[16,128]{1,0:T(8,128)S(1)}, u32[]{:S(2)}, u32[]{:S(2)}) collective-permute-start(f32[16,128]{1,0:T(8,128)S(1)} %get-tuple-element.81), channel_id=1, source_target_pairs={{0,508},{4,0},{8,4},{12,8},{16,12},{20,16},{24,20},{28,24},{32,28}... | collective-permute-start | bytes 24584 | tf_op jit(solution)/shard_map/ppermute | solution.py:16
  171.3 3.7 %collective-permute-start.12 = (f32[16,128]{1,0:T(8,128)S(1)}, f32[16,128]{1,0:T(8,128)S(1)}, u32[]{:S(2)}, u32[]{:S(2)}) collective-permute-start(f32[16,128]{1,0:T(8,128)S(1)} %slice.795), channel_id=1, source_target_pairs={{0,4},{4,8},{8,12},{12,16},{16,20},{20,24},{24,28},{28,32},{32,36}... | collective-permute-start | bytes 24584 | tf_op jit(solution)/shard_map/ppermute | solution.py:16
  175.2 8.4 %collective-permute-start.13 = (bf16[4,16,128]{2,1,0:T(8,128)(2,1)S(1)}, bf16[4,16,128]{2,1,0:T(8,128)(2,1)S(1)}, u32[]{:S(2)}, u32[]{:S(2)}) collective-permute-start(bf16[4,16,128]{2,1,0:T(8,128)(2,1)S(1)} %fusion.125), channel_id=1, source_target_pairs={{0,256},{4,260},{8,264},{12,268},{16,272},{20,276},{24,280},{28,28... | collective-permute-start | bytes 49160 | tf_op jit(solution)/shard_map/ppermute | solution.py:16
  208.9 8.1 %all-to-all-start.4 = ((f32[4,1,128]{2,1,0:T(1,128)}), f32[4,1,128]{2,1,0:T(1,128)S(1)}, u32[]{:S(2)}, u32[]{:S(2)}) async-start(f32[4,1,128]{2,1,0:T(1,128)} %broadcast_in_dim_broadcast_in_dim_broadcast_in_dim.3), calls=%async_computation.4 | async-start | bytes 4096 | tf_op jit(solution)/shard_map/all_to_all | solution.py:63

commit v2 on v0

v2 whole, which is shorter than its diff:
```python
import jax
import jax.numpy as jnp
from jax import lax
from jax.experimental import pallas as pl
from jax.experimental.pallas import tpu as pltpu
from jax.sharding import PartitionSpec as P

M = 1536
BLK = 128
ITERS = 4
CASES = 16
LOW, HIGH = 2 * BLK, 6 * BLK
CONTACT = HIGH - LOW

penalty = 0.5
f32, bf16 = jnp.float32, jnp.bfloat16


def dot(value, matrix, transposed=False):
    contract = 1 if transposed else 0
    return lax.dot_general(
        value, matrix, (((1,), (contract,)), ((), ())), preferred_element_type=f32
    )


def fine_dot(value, matrix, transposed=False):
    high = value.astype(bf16)
    low = (value - high.astype(f32)).astype(bf16)
    both = dot(jnp.concatenate([high, low], axis=0), matrix, transposed)
    return both[:CASES] + both[CASES:]


def split(value):
    return [value[:, k * BLK : (k + 1) * BLK] for k in range(value.shape[1] // BLK)]


def weighed(weights, values):
    total = weights[0] * values[0]
    for weight, value in zip(weights[1:], values[1:]):
        total = total + weight * value
    return total


def slots(meta):
    onehot = [[meta[:, 4 * k + b : 4 * k + b + 1] for b in range(4)] for k in range(4)]
    active = [meta[:, 16 + k : 17 + k] for k in range(4)]
    return onehot, active


def slot_table(ids, count):
    lane = lax.broadcasted_iota(jnp.int32, (CASES, BLK), 1)
    table = jnp.zeros((CASES, BLK), f32)
    for k in range(4):
        table = jnp.where(lane == ids[0, k] + 4 * k, 1.0, table)
        alive = jnp.where(count[0] > k, 1.0, 0.0).astype(f32)
        table = jnp.where(lane == 16 + k, alive, table)
    return table


def jump_of(slave, own, terms, mortar):
    onehot, active = terms
    return [
        (fine_dot(weighed(onehot[k], slave), mortar[k]) - own[k]) * active[k] for k in range(4)
    ]


def reply_of(jump, terms, mortar):
    onehot, _ = terms
    rows = [fine_dot(jump[k], mortar[k], True) for k in range(4)]
    return [weighed([onehot[k][b] for k in range(4)], rows) for b in range(4)]


def contact_terms(own, mate, statics, both):
    terms, mortar, mate_terms, mate_mortar = statics[:4]
    own, mate = split(own), split(mate)
    jump = jump_of(mate, own, terms, mortar)
    mate_jump = jump_of(own, mate, mate_terms, mate_mortar)
    part = [r - j for r, j in zip(reply_of(mate_jump, mate_terms, mate_mortar), jump)]
    if not both:
        return jnp.concatenate(part, axis=1), None
    mate_part = [r - j for r, j in zip(reply_of(jump, terms, mortar), mate_jump)]
    return jnp.concatenate(part, axis=1), jnp.concatenate(mate_part, axis=1)


def picks(match):
    rows = lax.broadcasted_iota(jnp.int32, (BLK, BLK), 0)
    return [
        jnp.where(rows == match[side : side + 1, :], 1.0, 0.0).astype(bf16) for side in range(2)
    ]


def whole_dot(value, pieces):
    high = value.astype(bf16)
    low = (value - high.astype(f32)).astype(bf16)
    both, total = jnp.concatenate([high, low], axis=0), None
    for start, size, piece in pieces:
        part = dot(both[:, start : start + size], piece())
        total = part if total is None else total + part
    return total[:CASES] + total[CASES:]


def begin(x, q, mate, prev, following, statics):
    pick = statics[4]
    mate_x, mate_q = mate[:, :CONTACT], mate[:, CONTACT:]
    prev_x, prev_q, prev_contact = prev[:, :BLK], prev[:, BLK : 2 * BLK], prev[:, 2 * BLK :]
    next_x, next_q = following[:, :BLK], following[:, BLK : 2 * BLK]
    next_contact = following[:, 2 * BLK :]
    first, second = x[:, :BLK], x[:, BLK:LOW]
    part, mate_part = contact_terms(x[:, LOW:HIGH], mate_x, statics, True)
    g = jnp.concatenate(
        [
            q[:, :BLK] + penalty * (first - fine_dot(prev_x, pick[0])),
            q[:, BLK:LOW] + penalty * (second - fine_dot(next_x, pick[1])),
            q[:, LOW:HIGH] + part,
            q[:, HIGH:],
        ],
        axis=1,
    )
    mate_g = mate_q + mate_part
    prev_face = prev_q + penalty * (prev_x - fine_dot(first, pick[0], True))
    next_face = next_q + penalty * (next_x - fine_dot(second, pick[1], True))
    others = jnp.concatenate([mate_x, mate_g, prev_contact, next_contact], axis=1)
    return g, others, prev_face, next_face


def tail(g, mate_g, prev_face, next_face, statics, pieces):
    pick = statics[4]
    part, _ = contact_terms(g[:, LOW:HIGH], mate_g, statics, False)
    first = penalty * (g[:, :BLK] - fine_dot(prev_face, pick[0]))
    second = penalty * (g[:, BLK:LOW] - fine_dot(next_face, pick[1]))
    zeros = jnp.zeros((CASES, M - HIGH), f32)
    image = whole_dot(g, pieces)
    image = image + jnp.concatenate([first, second, part, zeros], axis=1)
    norm = jnp.sum(g * g, axis=1, keepdims=True)
    curve = jnp.sum(g * image, axis=1, keepdims=True)
    lane = lax.broadcasted_iota(jnp.int32, (CASES, BLK), 1)
    row = lax.broadcasted_iota(jnp.int32, (CASES, BLK), 0)
    spread = jnp.where(lane == row, norm, 0.0) + jnp.where(lane == row + CASES, curve, 0.0)
    return image, jnp.sum(spread, axis=0, keepdims=True)


def step_of(sums):
    total = jnp.sum(sums, axis=0, keepdims=True)
    lane = lax.broadcasted_iota(jnp.int32, (CASES, BLK), 1)
    row = lax.broadcasted_iota(jnp.int32, (CASES, BLK), 0)
    norm = jnp.sum(jnp.where(lane == row, total, 0.0), axis=1, keepdims=True)
    curve = jnp.sum(jnp.where(lane == row + CASES, total, 0.0), axis=1, keepdims=True)
    return norm, norm / curve


def moved_by(x, step, g):
    moved = x - step * g
    return jnp.maximum(moved, 0.0), jnp.maximum(-moved, 0.0)


def all_moved(x, step, g):
    moved = x - step * g
    contact = moved[:, LOW:HIGH]
    x = jnp.concatenate([moved[:, :LOW], jnp.maximum(contact, 0.0), moved[:, HIGH:]], axis=1)
    return x, jnp.maximum(-contact, 0.0)


def advance(sums, own, others, mate, prev, following, statics, rows, coarse):
    _, step = step_of(sums)
    x, g, image = own
    x, lift = all_moved(x, step, g)
    mate_x, mate_g = others[:, :CONTACT], others[:, CONTACT : 2 * CONTACT]
    prev_x = others[:, 2 * CONTACT : 3 * CONTACT]
    next_x = others[:, 3 * CONTACT : 4 * CONTACT]
    prev_face = others[:, 4 * CONTACT : 4 * CONTACT + BLK]
    next_face = others[:, 4 * CONTACT + BLK :]
    mate_kernel, prev_kernel, next_kernel = coarse
    mate_x, mate_lift = moved_by(mate_x, step, mate_g)
    prev_x, prev_lift = moved_by(prev_x, step, prev[:, BLK:])
    next_x, next_lift = moved_by(next_x, step, following[:, BLK:])
    part, mate_part = contact_terms(lift, mate_lift, statics, True)
    mate_g = mate_g - step * mate + dot(mate_lift.astype(bf16), mate_kernel[...]) + mate_part
    prev_face = prev_face - step * prev[:, :BLK] + dot(prev_lift.astype(bf16), prev_kernel[...])
    next_face = next_face - step * following[:, :BLK] + dot(next_lift.astype(bf16), next_kernel[...])
    lifted = whole_dot(lift, [(start - LOW, size, piece) for start, size, piece in rows()])
    g = g - step * image + lifted
    g = jnp.concatenate([g[:, :LOW], g[:, LOW:HIGH] + part, g[:, HIGH:]], axis=1)
    others = jnp.concatenate([mate_x, mate_g, prev_x, next_x], axis=1)
    return x, g, others, prev_face, next_face


def to_partner(image):
    return image[:, LOW:HIGH]


def to_neighbour(image, g, side):
    face = image[:, side * BLK : (side + 1) * BLK]
    return jnp.concatenate([face, g[:, LOW:HIGH]], axis=1)


CHUNK = 256
STARTS = (LOW, LOW + CHUNK) + (0,) + tuple(range(HIGH, M, CHUNK))


def whole_copy(dual_hbm, dual_ref, sems):
    copies = []
    for index, start in enumerate(STARTS):
        rows = pl.ds(start, CHUNK)
        copies.append(
            pltpu.make_async_copy(dual_hbm.at[rows], dual_ref.at[rows], sems.at[index])
        )
    for copy in copies:
        copy.start()

    def piece(index, wait):
        def read():
            if wait:
                copies[index].wait()
            return dual_ref[pl.ds(STARTS[index], CHUNK), :]

        return (STARTS[index], CHUNK, read)

    return piece


def prepare_kernel(*refs):
    ids, count, x_ref, right_ref, mortar, dual_hbm = refs[:6]
    q_ref, packed, next_ref, prev_ref, dual_ref, sems = refs[6:]
    piece = whole_copy(dual_hbm, dual_ref, sems)
    packed[16 * CASES : 16 * CASES + CONTACT, :] = mortar[...]
    packed[16 * CASES + CONTACT :, :] = slot_table(ids, count).astype(bf16)
    x = x_ref[...]
    q = whole_dot(x, [piece(k, True) for k in range(len(STARTS))]) - right_ref[...]
    q_ref[...] = q
    for k, block in enumerate(split(x[:, LOW:HIGH]) + split(q[:, LOW:HIGH])):
        high = block.astype(bf16)
        packed[2 * k * CASES : (2 * k + 1) * CASES, :] = high
        low = (block - high.astype(f32)).astype(bf16)
        packed[(2 * k + 1) * CASES : (2 * k + 2) * CASES, :] = low
    next_ref[...] = jnp.concatenate([x[:, BLK:LOW], q[:, BLK:LOW], x[:, LOW:HIGH]], axis=1)
    prev_ref[...] = jnp.concatenate([x[:, :BLK], q[:, :BLK], x[:, LOW:HIGH]], axis=1)


def statics_of(ids, count, mortar, packed, match):
    start = 16 * CASES
    own = [mortar[k * BLK : (k + 1) * BLK, :] for k in range(4)]
    mate = [packed[start + k * BLK : start + (k + 1) * BLK, :] for k in range(4)]
    mate_table = packed[start + CONTACT :, :].astype(f32)
    return slots(slot_table(ids, count)), own, slots(mate_table), mate, picks(match[...])


def emit(outs, x, g, image, row, others, faces):
    own_out, others_out, row_out, mate_out, next_out, prev_out = outs
    row_out[...] = jnp.broadcast_to(row, row_out.shape)
    own_out[:, :M] = x
    own_out[:, M : 2 * M] = g
    own_out[:, 2 * M :] = image
    others_out[:, : 4 * CONTACT] = others
    others_out[:, 4 * CONTACT : 4 * CONTACT + BLK] = faces[0]
    others_out[:, 4 * CONTACT + BLK :] = faces[1]
    mate_out[...] = to_partner(image)
    next_out[...] = to_neighbour(image, g, 1)
    prev_out[...] = to_neighbour(image, g, 0)


def begin_kernel(*refs):
    ids, count, x_ref, q_ref, prev, following, mortar, packed, match, dual_hbm = refs[:10]
    outs, (dual_ref, sems) = refs[10:16], refs[16:]
    piece = whole_copy(dual_hbm, dual_ref, sems)
    statics = statics_of(ids, count, mortar, packed, match)
    x = x_ref[...]
    parts = [packed[k * CASES : (k + 1) * CASES, :].astype(f32) for k in range(16)]
    mate = jnp.concatenate([parts[2 * k] + parts[2 * k + 1] for k in range(8)], axis=1)
    g, others, prev_face, next_face = begin(
        x,
        q_ref[...],
        mate,
        prev[...],
        following[...],
        statics,
    )
    mate_g = others[:, CONTACT : 2 * CONTACT]
    pieces = [piece(k, True) for k in range(len(STARTS))]
    image, row = tail(g, mate_g, prev_face, next_face, statics, pieces)
    emit(outs, x, g, image, row, others, (prev_face, next_face))


def advance_kernel(*refs):
    ids, count, sums, own, others, mate, prev, following, mortar, packed, match = refs[:11]
    mate_kernel, prev_kernel, next_kernel, dual_hbm = refs[11:15]
    outs, (dual_ref, sems) = refs[15:21], refs[21:]
    piece = whole_copy(dual_hbm, dual_ref, sems)
    statics = statics_of(ids, count, mortar, packed, match)

    def rows():
        return [piece(k, True) for k in range(2)]

    x, g, others, prev_face, next_face = advance(
        sums[...],
        (own[:, :M], own[:, M : 2 * M], own[:, 2 * M :]),
        others[...],
        mate[...],
        prev[...],
        following[...],
        statics,
        rows,
        (mate_kernel, prev_kernel, next_kernel),
    )
    mate_g = others[:, CONTACT : 2 * CONTACT]
    pieces = [piece(k, k >= 2) for k in range(len(STARTS))]
    image, row = tail(g, mate_g, prev_face, next_face, statics, pieces)
    emit(outs, x, g, image, row, others, (prev_face, next_face))


def finish_kernel(sums, own, x_out, norm_out):
    norm, step = step_of(sums[...])
    x, _ = all_moved(own[:, :M], step, own[:, M : 2 * M])
    x_out[...] = x
    norm_out[...] = jnp.broadcast_to(jnp.sum(norm, axis=0, keepdims=True), norm_out.shape)


VMEM_SPEC = pl.BlockSpec(memory_space=pltpu.VMEM)
SMEM_SPEC = pl.BlockSpec(memory_space=pltpu.SMEM)
HBM_SPEC = pl.BlockSpec(memory_space=pltpu.HBM)


def call(kernel, specs, shapes, operands, scratch=True):
    scratch_shapes = [pltpu.VMEM((M, M), bf16), pltpu.SemaphoreType.DMA((len(STARTS),))] if scratch else []
    return pl.pallas_call(
        kernel,
        in_specs=specs,
        out_specs=[VMEM_SPEC] * len(shapes),
        out_shape=[jax.ShapeDtypeStruct(shape, kind) for shape, kind in shapes],
        scratch_shapes=scratch_shapes,
        compiler_params=pltpu.CompilerParams(vmem_limit_bytes=(52 if scratch else 16) << 20),
    )(*operands)


def shifted(value, by):
    devices = lax.axis_size("sub")
    return lax.ppermute(value, "sub", [(i, (i + by) % devices) for i in range(devices)])


def spread_sums(copies, axis):
    devices = lax.axis_size(axis)
    rows = lax.all_to_all(copies.reshape(devices, 1, BLK), axis, 0, 0)
    return rows.reshape(devices, BLK)


def on_device(multipliers, right_side, dual_ops, glue_match, mortar, contact_ids, contact_count):
    devices = lax.axis_size("sub")
    half_axis = devices // 2
    mortar = mortar.reshape(CONTACT, BLK)
    match = glue_match[0]
    scalars = [SMEM_SPEC, SMEM_SPEC]

    q, packed, following, prev = call(
        prepare_kernel,
        scalars + [VMEM_SPEC] * 3 + [HBM_SPEC],
        [
            ((CASES, M), f32),
            ((17 * CASES + CONTACT, BLK), bf16),
            ((CASES, 2 * BLK + CONTACT), f32),
            ((CASES, 2 * BLK + CONTACT), f32),
        ],
        (contact_ids, contact_count, multipliers, right_side, mortar, dual_ops),
    )
    packed = shifted(packed, half_axis)
    prev, following = shifted(following, 1), shifted(prev, -1)
    mate_kernel = shifted(dual_ops[LOW:HIGH, LOW:HIGH], half_axis)
    prev_kernel = shifted(dual_ops[LOW:HIGH, BLK:LOW], 1)
    next_kernel = shifted(dual_ops[LOW:HIGH, :BLK], -1)

    shapes = [
        ((CASES, 3 * M), f32),
        ((CASES, 4 * CONTACT + 2 * BLK), f32),
        ((devices, BLK), f32),
        ((CASES, CONTACT), f32),
        ((CASES, BLK + CONTACT), f32),
        ((CASES, BLK + CONTACT), f32),
    ]
    own, others, copies, to_mate, to_next, to_prev = call(
        begin_kernel,
        scalars + [VMEM_SPEC] * 7 + [HBM_SPEC],
        shapes,
        (
            contact_ids, contact_count, multipliers, q, prev, following, mortar, packed, match,
            dual_ops,
        ),
    )
    for _ in range(1, ITERS):
        sums = spread_sums(copies, "sub")
        mate = shifted(to_mate, half_axis)
        prev, following = shifted(to_next, 1), shifted(to_prev, -1)
        own, others, copies, to_mate, to_next, to_prev = call(
            advance_kernel,
            scalars + [VMEM_SPEC] * 12 + [HBM_SPEC],
            shapes,
            (
                contact_ids, contact_count, sums, own, others, mate, prev, following, mortar,
                packed, match, mate_kernel, prev_kernel, next_kernel, dual_ops,
            ),
        )
    sums = spread_sums(copies, "sub")
    x, norm = call(
        finish_kernel,
        [VMEM_SPEC, VMEM_SPEC],
        [((CASES, M), f32), ((lax.axis_size("case"), BLK), f32)],
        (sums, own),
        scratch=False,
    )
    total = spread_sums(norm, "case").sum(0)
    return (x, jnp.sqrt(total[:1]))


def solution(mesh):
    in_specs = (
        P("case", "sub"),
        P("case", "sub"),
        P("sub", None),
        P("sub", None, None),
        P("sub", None, None, None),
        P("sub", None),
        P("sub"),
    )
    out_specs = (P("case", "sub"), P())
    return jax.shard_map(
        on_device, mesh=mesh, in_specs=in_specs, out_specs=out_specs, check_vma=False
    )
```

time: 1260 us -> 195 us (0.15)
  blocking collectives: 1020 us -> 35.7 us
  matrix products: 33.9 us -> 0 us
  waiting for transfers between devices: 40.1 us -> 6.75 us
  Pallas kernels: 0 us -> 23.3 us
  starting transfers between devices: 142 us -> 119 us
    psum x5 -> x0, blocking collectives: 1020 us -> none  [the longest x4 1010 us: on_device(): grad_norms = lax.psum(jnp.sum(gradient * gradient, axis=1), 'sub')]
    ppermute x32 -> x15, starting transfers between devices: 142 us -> 68.6 us  [shifted(): lax.ppermute(value, 'sub', [(i, (i + by) % devices) for i in range(device...]
    all_to_all x0 -> x3, starting transfers between devices: none -> 50.6 us  [spread_sums(): rows = lax.all_to_all(copies.reshape(devices, 1, BLK), axis, 0, 0)]
    all_to_all x0 -> x2, blocking collectives: none -> 35.7 us  [spread_sums(): rows = lax.all_to_all(copies.reshape(devices, 1, BLK), axis, 0, 0)]
    dot_general x40 -> x0, matrix products: 33.9 us -> none  [the longest x8 25.4 us: apply_operator(): jnp.dot(vector.astype(jnp.bfloat16), dual_op, preferred_element_type=jnp....]
    ppermute x32 -> x15, waiting for transfers between devices: 40.1 us -> 6.74 us  [shifted(): lax.ppermute(value, 'sub', [(i, (i + by) % devices) for i in range(device...]
    pallas_call x0 -> x6, Pallas kernels: none -> 23.3 us  [call(): pl.pallas_call(kernel, in_specs=specs, out_specs=[VMEM_SPEC] * len(shapes...]
  transfers between devices with their start and end apart: 32 -> 18, of which waited for: 16 -> 4; matrix products, arithmetic and copies ran while one was open for 1% -> 1% of each run, Pallas kernels for 0% -> 4%
where the time goes in v2:
time: 195 us; the launch traced here: 194 us
  starting transfers between devices  119 us (61%)
  blocking collectives  35.7 us (18%)
  Pallas kernels  23.3 us (12%)
  waiting for transfers between devices  6.75 us (3%)
  local copies, waits for them, and re-layouts  6.24 us (3%)
  between operations  2.77 us (1%)
    ppermute x15, starting transfers between devices, shifted(): lax.ppermute(value, 'sub', [(i, (i + by) % devices) for i in range(device...  68.6 us
    all_to_all x3, starting transfers between devices, spread_sums(): rows = lax.all_to_all(copies.reshape(devices, 1, BLK), axis, 0, 0)  50.6 us
    all_to_all x2, blocking collectives, spread_sums(): rows = lax.all_to_all(copies.reshape(devices, 1, BLK), axis, 0, 0)  35.7 us
    pallas_call x6, Pallas kernels, call(): pl.pallas_call(kernel, in_specs=specs, out_specs=[VMEM_SPEC] * len(shapes...  23.3 us
    ppermute x15, waiting for transfers between devices, shifted(): lax.ppermute(value, 'sub', [(i, (i + by) % devices) for i in range(device...  6.74 us
    unnamed x16, local copies, waits for them, and re-layouts  4.13 us
  transfers between devices with their start and end apart: 18, of which 4 were waited for; matrix products, arithmetic and copies ran while one was open for 1% of the time, Pallas kernels for 4%

profile of v2, /device:TPU:1, one launch (start us, length us, event | category | flops | bytes accessed | tf_op | source)
XLA Modules:
  0.0 194.0 jit_solution(9790560985861951346)
XLA Ops:
  1.8 8.3 %collective-permute-start.6 = (bf16[512,512]{1,0:T(8,128)(2,1)S(1)}, bf16[512,512]{1,0:T(8,128)(2,1)S(1)}, u32[]{:S(2)}, u32[]{:S(2)}) collective-permute-start(bf16[512,512]{1,0:T(8,128)(2,1)S(1)} %slice.12), channel_id=1, source_target_pairs={{0,256},{4,260},{8,264},{12,268},{16,272},{20,276},{24,280},{28,28... | collective-permute-start | bytes 1572872 | tf_op jit(solution)/shard_map/ppermute | solution.py:336
  14.0 3.2 %shard_map.86 = (f32[16,1536]{1,0:T(8,128)S(1)}, bf16[784,128]{1,0:T(8,128)(2,1)S(1)}, f32[16,768]{1,0:T(8,128)S(1)}, f32[16,768]{1,0:T(8,128)S(1)}) custom-call(s32[1,4]{1,0:T(1,128)S(1)} %copy-done.5, s32[1]{0:T(128)S(6)} %copy.14.refs_1_, f32[16,1536]{1,0:T(8,128)S(1)} %copy-done.2, f32[16,1536]{1,0:T(8,128)S(1)} %copy-done.3, ...), custom_call_target="tpu_custom_call" | custom-call | tf_op jit(solution)/shard_map/pallas_call | solution.py:324
  17.2 4.8 %collective-permute-start = (f32[16,768]{1,0:T(8,128)S(1)}, f32[16,768]{1,0:T(8,128)S(1)}, u32[]{:S(2)}, u32[]{:S(2)}) collective-permute-start(f32[16,768]{1,0:T(8,128)S(1)} %get-tuple-element.29), channel_id=1, source_target_pairs={{0,4},{4,8},{8,12},{12,16},{16,20},{20,24},{24,28},{28,32},{32,36}... | collective-permute-start | bytes 147464 | tf_op jit(solution)/shard_map/ppermute | solution.py:336
  22.1 1.9 collective-permute-start.1
  24.0 5.1 %collective-permute-start.2 = (bf16[784,128]{1,0:T(8,128)(2,1)S(1)}, bf16[784,128]{1,0:T(8,128)(2,1)S(1)}, u32[]{:S(2)}, u32[]{:S(2)}) collective-permute-start(bf16[784,128]{1,0:T(8,128)(2,1)S(1)} %get-tuple-element.31), channel_id=1, source_target_pairs={{0,256},{4,260},{8,264},{12,268},{16,272},{20,276},{24,280},{28,28... | collective-permute-start | bytes 602120 | tf_op jit(solution)/shard_map/ppermute | solution.py:336
  30.1 7.9 %collective-permute-start.8 = (bf16[512,128]{1,0:T(8,128)(2,1)S(1)}, bf16[512,128]{1,0:T(8,128)(2,1)S(1)}, u32[]{:S(2)}, u32[]{:S(2)}) collective-permute-start(bf16[512,128]{1,0:T(8,128)(2,1)S(1)} %get-tuple-element.54), channel_id=1, source_target_pairs={{0,508},{4,0},{8,4},{12,8},{16,12},{20,16},{24,20},{28,24},{32,28}... | collective-permute-start | bytes 393224 | tf_op jit(solution)/shard_map/ppermute | solution.py:336
  38.1 1.9 collective-permute-start.7
  40.0 3.0 %collective-permute-done.2.refs_7_.refs_9_ = bf16[784,128]{1,0:T(8,128)(2,1)S(1)} collective-permute-done((bf16[784,128]{1,0:T(8,128)(2,1)S(1)}, bf16[784,128]{1,0:T(8,128)(2,1)S(1)}, u32[]{:S(2)}, u32[]{:S(2)}) %collective-permute-start.2) | collective-permute-done | bytes 200736 | tf_op jit(solution)/shard_map/ppermute | solution.py:336
  43.0 4.4 %shard_map.87 = (f32[16,4608]{1,0:T(8,128)S(1)}, f32[16,2304]{1,0:T(8,128)S(1)}, f32[128,128]{1,0:T(8,128)}, f32[16,512]{1,0:T(8,128)S(1)}, f32[16,640]{1,0:T(8,128)S(1)}, /*index=5*/f32[16,640]{1,0:T(8,128)S(1)}) custom-call(s32[1,4]{1,0:T(1,128)S(1)} %copy-done.5, s32[1]{0:T(128)S(6)} %copy.14.refs_1_, f32[16,1536]{1,0:T(8,128)S(1)} %copy-done.2, ...), custom_call_target="tpu_custom_call" | custom-call | tf_op jit(solution)/shard_map/pallas_call | solution.py:324
  47.4 17.7 %all-to-all-start = ((f32[128,1,128]{2,1,0:T(1,128)}), f32[128,1,128]{2,1,0:T(1,128)S(1)}, u32[]{:S(2)}, u32[]{:S(2)}) async-start(f32[128,1,128]{2,1,0:T(1,128)} %bitcast.3), calls=%async_computation | async-start | bytes 131072 | tf_op jit(solution)/shard_map/all_to_all | solution.py:341
  65.1 3.5 %collective-permute-start.4 = (f32[16,640]{1,0:T(8,128)S(1)}, f32[16,640]{1,0:T(8,128)S(1)}, u32[]{:S(2)}, u32[]{:S(2)}) collective-permute-start(f32[16,640]{1,0:T(8,128)S(1)} %get-tuple-element.36), channel_id=1, source_target_pairs={{0,4},{4,8},{8,12},{12,16},{16,20},{20,24},{24,28},{28,32},{32,36}... | collective-permute-start | bytes 122888 | tf_op jit(solution)/shard_map/ppermute | solution.py:336
  68.7 1.9 collective-permute-start.5
  70.6 7.3 %collective-permute-start.3 = (f32[16,512]{1,0:T(8,128)S(1)}, f32[16,512]{1,0:T(8,128)S(1)}, u32[]{:S(2)}, u32[]{:S(2)}) collective-permute-start(f32[16,512]{1,0:T(8,128)S(1)} %get-tuple-element.35), channel_id=1, source_target_pairs={{0,256},{4,260},{8,264},{12,268},{16,272},{20,276},{24,280},{28,28... | collective-permute-start | bytes 98312 | tf_op jit(solution)/shard_map/ppermute | solution.py:336
  80.1 5.0 %shard_map.88 = (f32[16,4608]{1,0:T(8,128)S(1)}, f32[16,2304]{1,0:T(8,128)S(1)}, f32[128,128]{1,0:T(8,128)}, f32[16,512]{1,0:T(8,128)S(1)}, f32[16,640]{1,0:T(8,128)S(1)}, /*index=5*/f32[16,640]{1,0:T(8,128)S(1)}) custom-call(s32[1,4]{1,0:T(1,128)S(1)} %copy-done.6, s32[1]{0:T(128)S(6)} %copy.14.refs_1_, f32[128,128]{1,0:T(8,128)S(1)} %bitcast.28, ...), custom_call_target="tpu_custom_call" | custom-call | tf_op jit(solution)/shard_map/pallas_call | solution.py:324
  85.1 16.4 %all-to-all-start.1 = ((f32[128,1,128]{2,1,0:T(1,128)}), f32[128,1,128]{2,1,0:T(1,128)S(1)}, u32[]{:S(2)}, u32[]{:S(2)}) async-start(f32[128,1,128]{2,1,0:T(1,128)} %bitcast.6), calls=%async_computation.1 | async-start | bytes 131072 | tf_op jit(solution)/shard_map/all_to_all | solution.py:341
  101.5 3.5 %collective-permute-start.10 = (f32[16,640]{1,0:T(8,128)S(1)}, f32[16,640]{1,0:T(8,128)S(1)}, u32[]{:S(2)}, u32[]{:S(2)}) collective-permute-start(f32[16,640]{1,0:T(8,128)S(1)} %get-tuple-element.42), channel_id=1, source_target_pairs={{0,4},{4,8},{8,12},{12,16},{16,20},{20,24},{24,28},{28,32},{32,36}... | collective-permute-start | bytes 122888 | tf_op jit(solution)/shard_map/ppermute | solution.py:336
  107.0 7.3 %collective-permute-start.9 = (f32[16,512]{1,0:T(8,128)S(1)}, f32[16,512]{1,0:T(8,128)S(1)}, u32[]{:S(2)}, u32[]{:S(2)}) collective-permute-start(f32[16,512]{1,0:T(8,128)S(1)} %get-tuple-element.41), channel_id=1, source_target_pairs={{0,256},{4,260},{8,264},{12,268},{16,272},{20,276},{24,280},{28,28... | collective-permute-start | bytes 98312 | tf_op jit(solution)/shard_map/ppermute | solution.py:336
  115.7 5.0 %shard_map.89 = (f32[16,4608]{1,0:T(8,128)S(1)}, f32[16,2304]{1,0:T(8,128)S(1)}, f32[128,128]{1,0:T(8,128)}, f32[16,512]{1,0:T(8,128)S(1)}, f32[16,640]{1,0:T(8,128)S(1)}, /*index=5*/f32[16,640]{1,0:T(8,128)S(1)}) custom-call(s32[1,4]{1,0:T(1,128)S(1)} %copy-done.6, s32[1]{0:T(128)S(6)} %copy.14.refs_1_, f32[128,128]{1,0:T(8,128)S(1)} %bitcast.30, ...), custom_call_target="tpu_custom_call" | custom-call | tf_op jit(solution)/shard_map/pallas_call | solution.py:324
  120.7 16.4 %all-to-all-start.2 = ((f32[128,1,128]{2,1,0:T(1,128)}), f32[128,1,128]{2,1,0:T(1,128)S(1)}, u32[]{:S(2)}, u32[]{:S(2)}) async-start(f32[128,1,128]{2,1,0:T(1,128)} %bitcast.9), calls=%async_computation.2 | async-start | bytes 131072 | tf_op jit(solution)/shard_map/all_to_all | solution.py:341
  137.2 3.5 %collective-permute-start.13 = (f32[16,640]{1,0:T(8,128)S(1)}, f32[16,640]{1,0:T(8,128)S(1)}, u32[]{:S(2)}, u32[]{:S(2)}) collective-permute-start(f32[16,640]{1,0:T(8,128)S(1)} %get-tuple-element.48), channel_id=1, source_target_pairs={{0,4},{4,8},{8,12},{12,16},{16,20},{20,24},{24,28},{28,32},{32,36}... | collective-permute-start | bytes 122888 | tf_op jit(solution)/shard_map/ppermute | solution.py:336
  142.6 7.5 %collective-permute-start.12 = (f32[16,512]{1,0:T(8,128)S(1)}, f32[16,512]{1,0:T(8,128)S(1)}, u32[]{:S(2)}, u32[]{:S(2)}) collective-permute-start(f32[16,512]{1,0:T(8,128)S(1)} %get-tuple-element.47), channel_id=1, source_target_pairs={{0,256},{4,260},{8,264},{12,268},{16,272},{20,276},{24,280},{28,28... | collective-permute-start | bytes 98312 | tf_op jit(solution)/shard_map/ppermute | solution.py:336
  151.3 5.0 %shard_map.90 = (f32[16,4608]{1,0:T(8,128)S(1)}, f32[16,2304]{1,0:T(8,128)}, f32[128,128]{1,0:T(8,128)S(1)}, f32[16,512]{1,0:T(8,128)}, f32[16,640]{1,0:T(8,128)}, /*index=5*/f32[16,640]{1,0:T(8,128)}) custom-call(s32[1,4]{1,0:T(1,128)S(1)} %copy-done.6, s32[1]{0:T(128)S(6)} %copy.14.refs_1_, f32[128,128]{1,0:T(8,128)S(1)} %bitcast.29, ...), custom_call_target="tpu_custom_call" | custom-call | tf_op jit(solution)/shard_map/pallas_call | solution.py:324
  156.3 27.8 %all_to_all.25 = f32[128,1,128]{2,1,0:T(1,128)S(1)} all-to-all(f32[128,1,128]{2,1,0:T(1,128)S(1)} %bitcast.31), channel_id=1, replica_groups=mesh['sub'=128,'case'=4] {'sub'}, dimensions={0} | all-to-all | bytes 131072 | tf_op jit(solution)/shard_map/all_to_all | solution.py:341
  184.8 7.9 %all_to_all.26 = f32[4,1,128]{2,1,0:T(1,128)S(1)} all-to-all(f32[4,1,128]{2,1,0:T(1,128)S(1)} %bitcast.36), channel_id=1, replica_groups=mesh['sub'=128,'case'=4] {'case'}, dimensions={0} | all-to-all | bytes 4096 | tf_op jit(solution)/shard_map/all_to_all | solution.py:341
  (39 shorter events, 14.7 us)
Async XLA Ops:
  0.6 42.3 %copy-start.1 = (bf16[1,4,128,128]{3,2,1,0:T(8,128)(2,1)S(1)}, bf16[1,4,128,128]{3,2,1,0:T(8,128)(2,1)}, u32[]{:S(2)}) copy-start(bf16[1,4,128,128]{3,2,1,0:T(8,128)(2,1)} %param.11) | copy-start | bytes 393220
  0.6 42.3 %copy-start.4 = (s32[1,2,128]{2,1,0:T(2,128)S(1)}, s32[1,2,128]{2,1,0:T(2,128)}, u32[]{:S(2)}) copy-start(s32[1,2,128]{2,1,0:T(2,128)} %param.10) | copy-start | bytes 3076
  1.8 77.5 %collective-permute-start.6 = (bf16[512,512]{1,0:T(8,128)(2,1)S(1)}, bf16[512,512]{1,0:T(8,128)(2,1)S(1)}, u32[]{:S(2)}, u32[]{:S(2)}) collective-permute-start(bf16[512,512]{1,0:T(8,128)(2,1)S(1)} %slice.12), channel_id=1, source_target_pairs={{0,256},{4,260},{8,264},{12,268},{16,272},{20,276},{24,280},{28,28... | collective-permute-start | bytes 1572872 | tf_op jit(solution)/shard_map/ppermute | solution.py:336
  10.7 0.9 copy-start
  11.6 0.9 copy-start.2
  12.5 0.9 copy-start.3
  14.0 66.0 %copy-start.6 = (s32[1,4]{1,0:T(1,128)S(1)}, s32[1,4]{1,0:T(1,128)}, u32[]{:S(2)}) copy-start(s32[1,4]{1,0:T(1,128)} %refs_0_.9) | copy-start | bytes 52
  17.2 20.8 %collective-permute-start = (f32[16,768]{1,0:T(8,128)S(1)}, f32[16,768]{1,0:T(8,128)S(1)}, u32[]{:S(2)}, u32[]{:S(2)}) collective-permute-start(f32[16,768]{1,0:T(8,128)S(1)} %get-tuple-element.29), channel_id=1, source_target_pairs={{0,4},{4,8},{8,12},{12,16},{16,20},{20,24},{24,28},{28,32},{32,36}... | collective-permute-start | bytes 147464 | tf_op jit(solution)/shard_map/ppermute | solution.py:336
  22.1 17.9 %collective-permute-start.1 = (f32[16,768]{1,0:T(8,128)S(1)}, f32[16,768]{1,0:T(8,128)S(1)}, u32[]{:S(2)}, u32[]{:S(2)}) collective-permute-start(f32[16,768]{1,0:T(8,128)S(1)} %get-tuple-element.30), channel_id=1, source_target_pairs={{0,508},{4,0},{8,4},{12,8},{16,12},{20,16},{24,20},{28,24},{32,28}... | collective-permute-start | bytes 147464 | tf_op jit(solution)/shard_map/ppermute | solution.py:336
  24.0 19.0 %collective-permute-start.2 = (bf16[784,128]{1,0:T(8,128)(2,1)S(1)}, bf16[784,128]{1,0:T(8,128)(2,1)S(1)}, u32[]{:S(2)}, u32[]{:S(2)}) collective-permute-start(bf16[784,128]{1,0:T(8,128)(2,1)S(1)} %get-tuple-element.31), channel_id=1, source_target_pairs={{0,256},{4,260},{8,264},{12,268},{16,272},{20,276},{24,280},{28,28... | collective-permute-start | bytes 602120 | tf_op jit(solution)/shard_map/ppermute | solution.py:336
  30.1 40.5 %collective-permute-start.8 = (bf16[512,128]{1,0:T(8,128)(2,1)S(1)}, bf16[512,128]{1,0:T(8,128)(2,1)S(1)}, u32[]{:S(2)}, u32[]{:S(2)}) collective-permute-start(bf16[512,128]{1,0:T(8,128)(2,1)S(1)} %get-tuple-element.54), channel_id=1, source_target_pairs={{0,508},{4,0},{8,4},{12,8},{16,12},{20,16},{24,20},{28,24},{32,28}... | collective-permute-start | bytes 393224 | tf_op jit(solution)/shard_map/ppermute | solution.py:336
  38.1 39.9 %collective-permute-start.7 = (bf16[512,128]{1,0:T(8,128)(2,1)S(1)}, bf16[512,128]{1,0:T(8,128)(2,1)S(1)}, u32[]{:S(2)}, u32[]{:S(2)}) collective-permute-start(bf16[512,128]{1,0:T(8,128)(2,1)S(1)} %get-tuple-element.55), channel_id=1, source_target_pairs={{0,4},{4,8},{8,12},{12,16},{16,20},{20,24},{24,28},{28,32},{32,36}... | collective-permute-start | bytes 393224 | tf_op jit(solution)/shard_map/ppermute | solution.py:336
  47.4 31.9 %all-to-all-start = ((f32[128,1,128]{2,1,0:T(1,128)}), f32[128,1,128]{2,1,0:T(1,128)S(1)}, u32[]{:S(2)}, u32[]{:S(2)}) async-start(f32[128,1,128]{2,1,0:T(1,128)} %bitcast.3), calls=%async_computation | async-start | bytes 131072 | tf_op jit(solution)/shard_map/all_to_all | solution.py:341
  65.1 14.1 %collective-permute-start.4 = (f32[16,640]{1,0:T(8,128)S(1)}, f32[16,640]{1,0:T(8,128)S(1)}, u32[]{:S(2)}, u32[]{:S(2)}) collective-permute-start(f32[16,640]{1,0:T(8,128)S(1)} %get-tuple-element.36), channel_id=1, source_target_pairs={{0,4},{4,8},{8,12},{12,16},{16,20},{20,24},{24,28},{28,32},{32,36}... | collective-permute-start | bytes 122888 | tf_op jit(solution)/shard_map/ppermute | solution.py:336
  68.7 10.6 %collective-permute-start.5 = (f32[16,640]{1,0:T(8,128)S(1)}, f32[16,640]{1,0:T(8,128)S(1)}, u32[]{:S(2)}, u32[]{:S(2)}) collective-permute-start(f32[16,640]{1,0:T(8,128)S(1)} %get-tuple-element.37), channel_id=1, source_target_pairs={{0,508},{4,0},{8,4},{12,8},{16,12},{20,16},{24,20},{28,24},{32,28}... | collective-permute-start | bytes 122888 | tf_op jit(solution)/shard_map/ppermute | solution.py:336
  70.6 8.7 %collective-permute-start.3 = (f32[16,512]{1,0:T(8,128)S(1)}, f32[16,512]{1,0:T(8,128)S(1)}, u32[]{:S(2)}, u32[]{:S(2)}) collective-permute-start(f32[16,512]{1,0:T(8,128)S(1)} %get-tuple-element.35), channel_id=1, source_target_pairs={{0,256},{4,260},{8,264},{12,268},{16,272},{20,276},{24,280},{28,28... | collective-permute-start | bytes 98312 | tf_op jit(solution)/shard_map/ppermute | solution.py:336
  85.1 30.6 %all-to-all-start.1 = ((f32[128,1,128]{2,1,0:T(1,128)}), f32[128,1,128]{2,1,0:T(1,128)S(1)}, u32[]{:S(2)}, u32[]{:S(2)}) async-start(f32[128,1,128]{2,1,0:T(1,128)} %bitcast.6), calls=%async_computation.1 | async-start | bytes 131072 | tf_op jit(solution)/shard_map/all_to_all | solution.py:341
  101.5 14.1 %collective-permute-start.10 = (f32[16,640]{1,0:T(8,128)S(1)}, f32[16,640]{1,0:T(8,128)S(1)}, u32[]{:S(2)}, u32[]{:S(2)}) collective-permute-start(f32[16,640]{1,0:T(8,128)S(1)} %get-tuple-element.42), channel_id=1, source_target_pairs={{0,4},{4,8},{8,12},{12,16},{16,20},{20,24},{24,28},{28,32},{32,36}... | collective-permute-start | bytes 122888 | tf_op jit(solution)/shard_map/ppermute | solution.py:336
  105.1 10.6 %collective-permute-start.11 = (f32[16,640]{1,0:T(8,128)S(1)}, f32[16,640]{1,0:T(8,128)S(1)}, u32[]{:S(2)}, u32[]{:S(2)}) collective-permute-start(f32[16,640]{1,0:T(8,128)S(1)} %get-tuple-element.43), channel_id=1, source_target_pairs={{0,508},{4,0},{8,4},{12,8},{16,12},{20,16},{24,20},{28,24},{32,28}... | collective-permute-start | bytes 122888 | tf_op jit(solution)/shard_map/ppermute | solution.py:336
  107.0 8.7 %collective-permute-start.9 = (f32[16,512]{1,0:T(8,128)S(1)}, f32[16,512]{1,0:T(8,128)S(1)}, u32[]{:S(2)}, u32[]{:S(2)}) collective-permute-start(f32[16,512]{1,0:T(8,128)S(1)} %get-tuple-element.41), channel_id=1, source_target_pairs={{0,256},{4,260},{8,264},{12,268},{16,272},{20,276},{24,280},{28,28... | collective-permute-start | bytes 98312 | tf_op jit(solution)/shard_map/ppermute | solution.py:336
  120.7 30.6 %all-to-all-start.2 = ((f32[128,1,128]{2,1,0:T(1,128)}), f32[128,1,128]{2,1,0:T(1,128)S(1)}, u32[]{:S(2)}, u32[]{:S(2)}) async-start(f32[128,1,128]{2,1,0:T(1,128)} %bitcast.9), calls=%async_computation.2 | async-start | bytes 131072 | tf_op jit(solution)/shard_map/all_to_all | solution.py:341
  137.2 14.1 %collective-permute-start.13 = (f32[16,640]{1,0:T(8,128)S(1)}, f32[16,640]{1,0:T(8,128)S(1)}, u32[]{:S(2)}, u32[]{:S(2)}) collective-permute-start(f32[16,640]{1,0:T(8,128)S(1)} %get-tuple-element.48), channel_id=1, source_target_pairs={{0,4},{4,8},{8,12},{12,16},{16,20},{20,24},{24,28},{28,32},{32,36}... | collective-permute-start | bytes 122888 | tf_op jit(solution)/shard_map/ppermute | solution.py:336
  140.7 10.6 %collective-permute-start.14 = (f32[16,640]{1,0:T(8,128)S(1)}, f32[16,640]{1,0:T(8,128)S(1)}, u32[]{:S(2)}, u32[]{:S(2)}) collective-permute-start(f32[16,640]{1,0:T(8,128)S(1)} %get-tuple-element.49), channel_id=1, source_target_pairs={{0,508},{4,0},{8,4},{12,8},{16,12},{20,16},{24,20},{28,24},{32,28}... | collective-permute-start | bytes 122888 | tf_op jit(solution)/shard_map/ppermute | solution.py:336
  142.6 8.7 %collective-permute-start.12 = (f32[16,512]{1,0:T(8,128)S(1)}, f32[16,512]{1,0:T(8,128)S(1)}, u32[]{:S(2)}, u32[]{:S(2)}) collective-permute-start(f32[16,512]{1,0:T(8,128)S(1)} %get-tuple-element.47), channel_id=1, source_target_pairs={{0,256},{4,260},{8,264},{12,268},{16,272},{20,276},{24,280},{28,28... | collective-permute-start | bytes 98312 | tf_op jit(solution)/shard_map/ppermute | solution.py:336
  (2 other events, 1.4 us)

commit v3 on v2

v3 whole, which is shorter than its diff:
```python
import jax
import jax.numpy as jnp
from jax import lax
from jax.experimental import pallas as pl
from jax.experimental.pallas import tpu as pltpu
from jax.sharding import PartitionSpec as P

M = 1536
BLK = 128
ITERS = 4
CASES = 16
LOW, HIGH = 2 * BLK, 6 * BLK
CONTACT = HIGH - LOW

penalty = 0.5
f32, bf16 = jnp.float32, jnp.bfloat16


def dot(value, matrix, transposed=False):
    contract = 1 if transposed else 0
    return lax.dot_general(
        value, matrix, (((1,), (contract,)), ((), ())), preferred_element_type=f32
    )


def fine_dot(value, matrix, transposed=False):
    high = value.astype(bf16)
    low = (value - high.astype(f32)).astype(bf16)
    both = dot(jnp.concatenate([high, low], axis=0), matrix, transposed)
    return both[:CASES] + both[CASES:]


def split(value):
    return [value[:, k * BLK : (k + 1) * BLK] for k in range(value.shape[1] // BLK)]


def weighed(weights, values):
    total = weights[0] * values[0]
    for weight, value in zip(weights[1:], values[1:]):
        total = total + weight * value
    return total


def slots(meta):
    onehot = [[meta[:, 4 * k + b : 4 * k + b + 1] for b in range(4)] for k in range(4)]
    active = [meta[:, 16 + k : 17 + k] for k in range(4)]
    return onehot, active


def slot_table(ids, count):
    lane = lax.broadcasted_iota(jnp.int32, (CASES, BLK), 1)
    table = jnp.zeros((CASES, BLK), f32)
    for k in range(4):
        table = jnp.where(lane == ids[0, k] + 4 * k, 1.0, table)
        alive = jnp.where(count[0] > k, 1.0, 0.0).astype(f32)
        table = jnp.where(lane == 16 + k, alive, table)
    return table


def jump_of(slave, own, terms, mortar):
    onehot, active = terms
    return [
        (fine_dot(weighed(onehot[k], slave), mortar[k]) - own[k]) * active[k] for k in range(4)
    ]


def reply_of(jump, terms, mortar):
    onehot, _ = terms
    rows = [fine_dot(jump[k], mortar[k], True) for k in range(4)]
    return [weighed([onehot[k][b] for k in range(4)], rows) for b in range(4)]


def contact_terms(own, mate, statics, both):
    terms, mortar, mate_terms, mate_mortar = statics[:4]
    own, mate = split(own), split(mate)
    jump = jump_of(mate, own, terms, mortar)
    mate_jump = jump_of(own, mate, mate_terms, mate_mortar)
    part = [r - j for r, j in zip(reply_of(mate_jump, mate_terms, mate_mortar), jump)]
    if not both:
        return jnp.concatenate(part, axis=1), None
    mate_part = [r - j for r, j in zip(reply_of(jump, terms, mortar), mate_jump)]
    return jnp.concatenate(part, axis=1), jnp.concatenate(mate_part, axis=1)


def chosen(even, first, second):
    return jnp.where(even, first, second)


def picks(match, even):
    rows = lax.broadcasted_iota(jnp.int32, (BLK, BLK), 0)
    first, second = match[0:1, :], match[1:2, :]
    sides = (chosen(even, second, first), chosen(even, first, second))
    return [jnp.where(rows == side, 1.0, 0.0).astype(bf16) for side in sides]


def faces_of(value, even):
    first, second = value[:, :BLK], value[:, BLK:LOW]
    return chosen(even, second, first), chosen(even, first, second)


def placed(near, far, even):
    return [chosen(even, far, near), chosen(even, near, far)]


def whole_dot(value, pieces):
    high = value.astype(bf16)
    low = (value - high.astype(f32)).astype(bf16)
    both, total = jnp.concatenate([high, low], axis=0), None
    for start, size, piece in pieces:
        part = dot(both[:, start : start + size], piece())
        total = part if total is None else total + part
    return total[:CASES] + total[CASES:]


def begin(x, q, mate, near, far, statics, pick, even):
    mate_x, mate_q = mate
    part, mate_part = contact_terms(x[:, LOW:HIGH], mate_x, statics, True)
    own = faces_of(x, even)
    glued, grads, contacts = [], [], []
    for side, face, matrix in zip((near, far), own, pick):
        side_x, side_q, contact = side[:, :BLK], side[:, BLK : 2 * BLK], side[:, 2 * BLK :]
        glued.append(penalty * (face - fine_dot(side_x, matrix)))
        grads.append(side_q + penalty * (side_x - fine_dot(face, matrix, True)))
        contacts.append(contact)
    faces = jnp.concatenate(placed(*glued, even), axis=1)
    g = jnp.concatenate(
        [q[:, :LOW] + faces, q[:, LOW:HIGH] + part, q[:, HIGH:]],
        axis=1,
    )
    return g, [mate_x, mate_q + mate_part] + contacts + grads


def tail(g, others, statics, pick, even, pieces):
    part, _ = contact_terms(g[:, LOW:HIGH], others[1], statics, False)
    glued = [
        penalty * (face - fine_dot(side, matrix))
        for face, side, matrix in zip(faces_of(g, even), others[4:], pick)
    ]
    zeros = jnp.zeros((CASES, M - HIGH), f32)
    image = whole_dot(g, pieces)
    image = image + jnp.concatenate(placed(*glued, even) + [part, zeros], axis=1)
    norm = jnp.sum(g * g, axis=1, keepdims=True)
    curve = jnp.sum(g * image, axis=1, keepdims=True)
    lane = lax.broadcasted_iota(jnp.int32, (CASES, BLK), 1)
    row = lax.broadcasted_iota(jnp.int32, (CASES, BLK), 0)
    spread = jnp.where(lane == row, norm, 0.0) + jnp.where(lane == row + CASES, curve, 0.0)
    return image, jnp.sum(spread, axis=0, keepdims=True)


def step_of(sums):
    total = jnp.sum(sums, axis=0, keepdims=True)
    lane = lax.broadcasted_iota(jnp.int32, (CASES, BLK), 1)
    row = lax.broadcasted_iota(jnp.int32, (CASES, BLK), 0)
    norm = jnp.sum(jnp.where(lane == row, total, 0.0), axis=1, keepdims=True)
    curve = jnp.sum(jnp.where(lane == row + CASES, total, 0.0), axis=1, keepdims=True)
    return norm, norm / curve


def moved_by(x, step, g):
    moved = x - step * g
    return jnp.maximum(moved, 0.0), jnp.maximum(-moved, 0.0)


def all_moved(x, step, g):
    moved = x - step * g
    contact = moved[:, LOW:HIGH]
    x = jnp.concatenate([moved[:, :LOW], jnp.maximum(contact, 0.0), moved[:, HIGH:]], axis=1)
    return x, jnp.maximum(-contact, 0.0)


def advance(sums, own, others, mate, near, far, statics, rows, coarse):
    _, step = step_of(sums)
    x, g, image = own
    x, lift = all_moved(x, step, g)
    mate_x, mate_g, near_x, far_x, near_face, far_face = others
    mate_kernel, near_kernel, far_kernel = coarse
    mate_x, mate_lift = moved_by(mate_x, step, mate_g)
    near_x, near_lift = moved_by(near_x, step, near[:, BLK:])
    far_x, far_lift = moved_by(far_x, step, far[:, BLK:])
    part, mate_part = contact_terms(lift, mate_lift, statics, True)
    mate_g = mate_g - step * mate + fine_dot(mate_lift, mate_kernel[...]) + mate_part
    near_face = near_face - step * near[:, :BLK] + fine_dot(near_lift, near_kernel[...])
    far_face = far_face - step * far[:, :BLK] + fine_dot(far_lift, far_kernel[...])
    lifted = whole_dot(lift, [(start - LOW, size, piece) for start, size, piece in rows()])
    g = g - step * image + lifted
    g = jnp.concatenate([g[:, :LOW], g[:, LOW:HIGH] + part, g[:, HIGH:]], axis=1)
    return x, g, [mate_x, mate_g, near_x, far_x, near_face, far_face]


CHUNK = 256
STARTS = (LOW, LOW + CHUNK) + (0,) + tuple(range(HIGH, M, CHUNK))


def whole_copy(dual_hbm, dual_ref, sems):
    copies = []
    for index, start in enumerate(STARTS):
        rows = pl.ds(start, CHUNK)
        copies.append(
            pltpu.make_async_copy(dual_hbm.at[rows], dual_ref.at[rows], sems.at[index])
        )
    for copy in copies:
        copy.start()

    def piece(index, wait):
        def read():
            if wait:
                copies[index].wait()
            return dual_ref[pl.ds(STARTS[index], CHUNK), :]

        return (STARTS[index], CHUNK, read)

    return piece


TABLE = 4 * CASES
SLOTS = TABLE + CASES
QUARTER = SLOTS + BLK
PACKED = QUARTER + BLK
SIDE = 12 * CASES


def is_even():
    return lax.rem(lax.axis_index("sub"), 2) == 0


def halves(block):
    high = block.astype(bf16)
    return high, (block - high.astype(f32)).astype(bf16)


def prepare_kernel(*refs):
    ids, count, x_ref, right_ref, mortar, dual_hbm = refs[:6]
    q_ref, packed, near_ref, far_ref, dual_ref, sems = refs[6:]
    piece = whole_copy(dual_hbm, dual_ref, sems)
    even = is_even()
    for k in range(4):
        packed[SLOTS:QUARTER, k * BLK : (k + 1) * BLK] = mortar[k * BLK : (k + 1) * BLK, :]
    table = slot_table(ids, count).astype(bf16)
    packed[TABLE:SLOTS, :] = jnp.concatenate([table] * 4, axis=1)
    x = x_ref[...]
    q = whole_dot(x, [piece(k, True) for k in range(len(STARTS))]) - right_ref[...]
    q_ref[...] = q
    start = pl.multiple_of(LOW + lax.rem(lax.axis_index("case"), 4) * BLK, BLK)
    packed[QUARTER:, :] = dual_ref[pl.ds(start, BLK), LOW:HIGH]
    parts = halves(x[:, LOW:HIGH]) + halves(q[:, LOW:HIGH])
    for k, part in enumerate(parts):
        packed[k * CASES : (k + 1) * CASES, :] = part
    contacts = split(x[:, LOW:HIGH])
    both = [(near_ref,), (far_ref,)]
    for (ref,), face, grad in zip(both, faces_of(x, even), faces_of(q, even)):
        for k, block in enumerate([face, grad] + contacts):
            high, low = halves(block)
            ref[2 * k * CASES : (2 * k + 1) * CASES, :] = high
            ref[(2 * k + 1) * CASES : (2 * k + 2) * CASES, :] = low
    first, second = dual_ref[LOW:HIGH, :BLK], dual_ref[LOW:HIGH, BLK:LOW]
    near_ref[SIDE:, :] = chosen(even, second, first)
    far_ref[SIDE:, :] = chosen(even, first, second)


def statics_of(ids, count, mortar, packed):
    own = [mortar[k * BLK : (k + 1) * BLK, :] for k in range(4)]
    mate = [packed[SLOTS:QUARTER, k * BLK : (k + 1) * BLK] for k in range(4)]
    mate_table = packed[TABLE:SLOTS, :BLK].astype(f32)
    return slots(slot_table(ids, count)), own, slots(mate_table), mate


def side_values(ref):
    parts = [ref[k * CASES : (k + 1) * CASES, :].astype(f32) for k in range(12)]
    return jnp.concatenate([parts[2 * k] + parts[2 * k + 1] for k in range(6)], axis=1)


def emit(outs, x, g, image, row, others):
    own_out, others_out, row_out, mate_out, near_out, far_out = outs
    row_out[...] = jnp.broadcast_to(row, row_out.shape)
    own_out[:, :M] = x
    own_out[:, M : 2 * M] = g
    own_out[:, 2 * M :] = image
    others_out[...] = jnp.concatenate(others, axis=1)
    mate_out[...] = image[:, LOW:HIGH]
    contact = g[:, LOW:HIGH]
    for ref, face in zip((near_out, far_out), faces_of(image, is_even())):
        ref[:, :BLK] = face
        ref[:, BLK:] = contact


def begin_kernel(*refs):
    ids, count, x_ref, q_ref, near, far, mortar, packed, match, dual_hbm = refs[:10]
    outs, (dual_ref, sems) = refs[10:16], refs[16:]
    piece = whole_copy(dual_hbm, dual_ref, sems)
    even = is_even()
    statics = statics_of(ids, count, mortar, packed)
    pick = picks(match[...], even)
    x = x_ref[...]
    parts = [packed[k * CASES : (k + 1) * CASES, :].astype(f32) for k in range(4)]
    mate = parts[0] + parts[1], parts[2] + parts[3]
    sides = side_values(near), side_values(far)
    g, others = begin(x, q_ref[...], mate, *sides, statics, pick, even)
    pieces = [piece(k, True) for k in range(len(STARTS))]
    image, row = tail(g, others, statics, pick, even, pieces)
    emit(outs, x, g, image, row, others)


WIDTHS = (CONTACT, CONTACT, CONTACT, CONTACT, BLK, BLK)


def advance_kernel(*refs):
    ids, count, sums, own, others, mate, near, far, mortar, packed, match = refs[:11]
    mate_kernel, near_kernel, far_kernel, dual_hbm = refs[11:15]
    outs, (dual_ref, sems) = refs[15:21], refs[21:]
    piece = whole_copy(dual_hbm, dual_ref, sems)
    even = is_even()
    statics = statics_of(ids, count, mortar, packed)
    pick = picks(match[...], even)

    def rows():
        return [piece(k, True) for k in range(2)]

    offsets = [sum(WIDTHS[:k]) for k in range(len(WIDTHS))]
    x, g, others = advance(
        sums[...],
        (own[:, :M], own[:, M : 2 * M], own[:, 2 * M :]),
        [others[:, start : start + size] for start, size in zip(offsets, WIDTHS)],
        mate[...],
        near[...],
        far[...],
        statics,
        rows,
        (mate_kernel, near_kernel.at[SIDE:], far_kernel.at[SIDE:]),
    )
    pieces = [piece(k, k >= 2) for k in range(len(STARTS))]
    image, row = tail(g, others, statics, pick, even, pieces)
    emit(outs, x, g, image, row, others)


def finish_kernel(sums, own, x_out, norm_out):
    norm, step = step_of(sums[...])
    x, _ = all_moved(own[:, :M], step, own[:, M : 2 * M])
    x_out[...] = x
    norm_out[...] = jnp.broadcast_to(jnp.sum(norm, axis=0, keepdims=True), norm_out.shape)


VMEM_SPEC = pl.BlockSpec(memory_space=pltpu.VMEM)
SMEM_SPEC = pl.BlockSpec(memory_space=pltpu.SMEM)
HBM_SPEC = pl.BlockSpec(memory_space=pltpu.HBM)


def call(kernel, specs, shapes, operands, scratch=True, grant=52):
    scratch_shapes = [pltpu.VMEM((M, M), bf16), pltpu.SemaphoreType.DMA((len(STARTS),))] if scratch else []
    return pl.pallas_call(
        kernel,
        in_specs=specs,
        out_specs=[VMEM_SPEC] * len(shapes),
        out_shape=[jax.ShapeDtypeStruct(shape, kind) for shape, kind in shapes],
        scratch_shapes=scratch_shapes,
        compiler_params=pltpu.CompilerParams(vmem_limit_bytes=grant << 20),
    )(*operands)


def swapped(value, other):
    devices = lax.axis_size("sub")
    return lax.ppermute(value, "sub", [(i, other(i) % devices) for i in range(devices)])


def with_mate(value):
    half_axis = lax.axis_size("sub") // 2
    return swapped(value, lambda i: i + half_axis)


def with_near(value):
    return swapped(value, lambda i: i ^ 1)


def with_far(value):
    return swapped(value, lambda i: i + 1 if i % 2 else i - 1)


def spread_sums(copies, axis):
    devices = lax.axis_size(axis)
    rows = lax.all_to_all(copies.reshape(devices, 1, BLK), axis, 0, 0)
    return rows.reshape(devices, BLK)


def on_device(multipliers, right_side, dual_ops, glue_match, mortar, contact_ids, contact_count):
    devices = lax.axis_size("sub")
    mortar = mortar.reshape(CONTACT, BLK)
    match = glue_match[0]
    scalars = [SMEM_SPEC, SMEM_SPEC]

    q, packed, to_near, to_far = call(
        prepare_kernel,
        scalars + [VMEM_SPEC] * 3 + [HBM_SPEC],
        [
            ((CASES, M), f32),
            ((PACKED, CONTACT), bf16),
            ((SIDE + CONTACT, BLK), bf16),
            ((SIDE + CONTACT, BLK), bf16),
        ],
        (contact_ids, contact_count, multipliers, right_side, mortar, dual_ops),
        grant=PREPARE_GRANT,
    )
    packed = with_mate(packed)
    near = near_kernel = with_near(to_near)
    far = far_kernel = with_far(to_far)
    cases = lax.axis_size("case")
    quarter = packed[QUARTER:]
    quarters = jnp.broadcast_to(quarter[None], (cases,) + quarter.shape)
    quarters = lax.all_to_all(quarters, "case", 0, 0)
    mate_kernel = quarters.reshape(cases * BLK, CONTACT)

    shapes = [
        ((CASES, 3 * M), f32),
        ((CASES, sum(WIDTHS)), f32),
        ((devices, BLK), f32),
        ((CASES, CONTACT), f32),
        ((CASES, BLK + CONTACT), f32),
        ((CASES, BLK + CONTACT), f32),
    ]
    own, others, copies, to_mate, to_near, to_far = call(
        begin_kernel,
        scalars + [VMEM_SPEC] * 7 + [HBM_SPEC],
        shapes,
        (
            contact_ids, contact_count, multipliers, q, near, far, mortar, packed, match,
            dual_ops,
        ),
    )
    copies, mate_kernel = lax.optimization_barrier((copies, mate_kernel))
    for _ in range(1, ITERS):
        sums = spread_sums(copies, "sub")
        mate = with_mate(to_mate)
        far = with_far(to_far)
        near = with_near(to_near)
        own, others, copies, to_mate, to_near, to_far = call(
            advance_kernel,
            scalars + [VMEM_SPEC] * 12 + [HBM_SPEC],
            shapes,
            (
                contact_ids, contact_count, sums, own, others, mate, near, far, mortar,
                packed, match, mate_kernel, near_kernel, far_kernel, dual_ops,
            ),
        )
    sums = spread_sums(copies, "sub")
    x, norm = call(
        finish_kernel,
        [VMEM_SPEC, VMEM_SPEC],
        [((CASES, M), f32), ((lax.axis_size("case"), BLK), f32)],
        (sums, own),
        scratch=False,
        grant=16,
    )
    total = spread_sums(norm, "case").sum(0)
    return (x, jnp.sqrt(total[:1]))


PREPARE_GRANT = 60


def solution(mesh):
    in_specs = (
        P("case", "sub"),
        P("case", "sub"),
        P("sub", None),
        P("sub", None, None),
        P("sub", None, None, None),
        P("sub", None),
        P("sub"),
    )
    out_specs = (P("case", "sub"), P())
    return jax.shard_map(
        on_device, mesh=mesh, in_specs=in_specs, out_specs=out_specs, check_vma=False
    )
```

time: 195 us -> 192 us (0.985)
  waiting for transfers between devices: 6.75 us -> 16.8 us
  starting transfers between devices: 119 us -> 111 us
  local copies, waits for them, and re-layouts: 6.24 us -> 1.86 us
    ppermute x15 -> x12, waiting for transfers between devices: 6.74 us -> 16.8 us  [swapped(): lax.ppermute(value, 'sub', [(i, other(i) % devices) for i in range(device...]
    ppermute x15 -> x12, starting transfers between devices: 68.6 us -> 59.6 us  [swapped(): lax.ppermute(value, 'sub', [(i, other(i) % devices) for i in range(device...]
    all_to_all x0 -> x1, starting transfers between devices: none -> 3.9 us  [on_device(): quarters = lax.all_to_all(quarters, 'case', 0, 0)]
    unnamed x16 -> x14, local copies, waits for them, and re-layouts: 4.13 us -> 0.91 us
    all_to_all x3, starting transfers between devices: 50.6 us -> 47.5 us  [spread_sums(): rows = lax.all_to_all(copies.reshape(devices, 1, BLK), axis, 0, 0)]
    slice x2 -> x1, local copies, waits for them, and re-layouts: 2.11 us -> 0.01 us  [on_device(): quarter = packed[QUARTER:]]
  transfers between devices with their start and end apart: 18 -> 16, of which waited for: 4 -> 5; matrix products, arithmetic and copies ran while one was open for 1% -> 0% of each run, Pallas kernels for 4% -> 2%
where the time goes in v3:
time: 192 us; the launch traced here: 191 us
  starting transfers between devices  111 us (58%)
  blocking collectives  33.9 us (18%)
  Pallas kernels  25 us (13%)
  waiting for transfers between devices  16.8 us (9%)
  between operations  2.8 us (1%)
    ppermute x12, starting transfers between devices, swapped(): lax.ppermute(value, 'sub', [(i, other(i) % devices) for i in range(device...  59.6 us
    all_to_all x3, starting transfers between devices, spread_sums(): rows = lax.all_to_all(copies.reshape(devices, 1, BLK), axis, 0, 0)  47.5 us
    all_to_all x2, blocking collectives, spread_sums(): rows = lax.all_to_all(copies.reshape(devices, 1, BLK), axis, 0, 0)  33.9 us
    pallas_call x6, Pallas kernels, call(): pl.pallas_call(kernel, in_specs=specs, out_specs=[VMEM_SPEC] * len(shapes...  25 us
    ppermute x12, waiting for transfers between devices, swapped(): lax.ppermute(value, 'sub', [(i, other(i) % devices) for i in range(device...  16.8 us
    all_to_all x1, starting transfers between devices, on_device(): quarters = lax.all_to_all(quarters, 'case', 0, 0)  3.9 us
  transfers between devices with their start and end apart: 16, of which 5 were waited for; matrix products, arithmetic and copies ran while one was open for 0% of the time, Pallas kernels for 2%

profile of v3, /device:TPU:1, one launch (start us, length us, event | category | flops | bytes accessed | tf_op | source)
XLA Modules:
  0.0 191.4 jit_solution(3039442468854447342)
XLA Ops:
  1.4 4.5 %shard_map.86 = (f32[16,1536]{1,0:T(8,128)}, bf16[336,512]{1,0:T(8,128)(2,1)}, bf16[704,128]{1,0:T(8,128)(2,1)}, bf16[704,128]{1,0:T(8,128)(2,1)}) custom-call(s32[1,4]{1,0:T(1,128)} %refs_0_.9, s32[1]{0:T(128)S(6)} %copy.14.refs_1_, f32[16,1536]{1,0:T(8,128)} %refs_2_.3, f32[16,1536]{1,0:T(8,128)} %refs_3_.1, bf16[512,128]{1,0:T(8,128)(2,1)} %bitcast.23, ...), custom_call_target="tpu_custom_call" | custom-call | tf_op jit(solution)/shard_map/pallas_call | solution.py:349
  5.8 8.3 %collective-permute-start.2 = (bf16[336,512]{1,0:T(8,128)(2,1)}, bf16[336,512]{1,0:T(8,128)(2,1)S(1)}, u32[]{:S(2)}, u32[]{:S(2)}) collective-permute-start(bf16[336,512]{1,0:T(8,128)(2,1)} %get-tuple-element.33), channel_id=1, source_target_pairs={{0,256},{4,260},{8,264},{12,268},{16,272},{20,276},{24,280},{28,28... | collective-permute-start | bytes 1032200 | tf_op jit(solution)/shard_map/ppermute | solution.py:361
  14.1 9.7 %collective-permute-done.2.refs_7_.refs_9_ = bf16[336,512]{1,0:T(8,128)(2,1)S(1)} collective-permute-done((bf16[336,512]{1,0:T(8,128)(2,1)}, bf16[336,512]{1,0:T(8,128)(2,1)S(1)}, u32[]{:S(2)}, u32[]{:S(2)}) %collective-permute-start.2) | collective-permute-done | bytes 344096 | tf_op jit(solution)/shard_map/ppermute | solution.py:361
  24.7 3.9 %all-to-all-start = ((bf16[4,128,512]{2,1,0:T(8,128)(2,1)}), bf16[4,128,512]{2,1,0:T(8,128)(2,1)S(1)}, u32[]{:S(2)}, u32[]{:S(2)}) async-start(bf16[4,128,512]{2,1,0:T(8,128)(2,1)} %broadcast_in_dim.2), calls=%async_computation | async-start | bytes 1048576 | tf_op jit(solution)/shard_map/all_to_all | solution.py:407
  28.6 8.6 %collective-permute-start = (bf16[704,128]{1,0:T(8,128)(2,1)}, bf16[704,128]{1,0:T(8,128)(2,1)S(1)}, u32[]{:S(2)}, u32[]{:S(2)}) collective-permute-start(bf16[704,128]{1,0:T(8,128)(2,1)} %get-tuple-element.31), channel_id=1, source_target_pairs={{0,4},{4,0},{8,12},{12,8},{16,20},{20,16},{24,28},{28,24},{32,36},... | collective-permute-start | bytes 540680 | tf_op jit(solution)/shard_map/ppermute | solution.py:361
  37.2 3.9 %collective-permute-start.1 = (bf16[704,128]{1,0:T(8,128)(2,1)}, bf16[704,128]{1,0:T(8,128)(2,1)S(1)}, u32[]{:S(2)}, u32[]{:S(2)}) collective-permute-start(bf16[704,128]{1,0:T(8,128)(2,1)} %get-tuple-element.32), channel_id=1, source_target_pairs={{0,508},{4,8},{8,4},{12,16},{16,12},{20,24},{24,20},{28,32},{32,28... | collective-permute-start | bytes 540680 | tf_op jit(solution)/shard_map/ppermute | solution.py:361
  41.1 3.4 %collective-permute-done.1.refs_5_.refs_13_ = bf16[704,128]{1,0:T(8,128)(2,1)S(1)} collective-permute-done((bf16[704,128]{1,0:T(8,128)(2,1)}, bf16[704,128]{1,0:T(8,128)(2,1)S(1)}, u32[]{:S(2)}, u32[]{:S(2)}) %collective-permute-start.1) | collective-permute-done | bytes 180256 | tf_op jit(solution)/shard_map/ppermute | solution.py:361
  45.4 4.4 %shard_map.87 = (f32[16,4608]{1,0:T(8,128)S(1)}, f32[16,2304]{1,0:T(8,128)S(1)}, f32[128,128]{1,0:T(8,128)}, f32[16,512]{1,0:T(8,128)S(1)}, f32[16,640]{1,0:T(8,128)S(1)}, /*index=5*/f32[16,640]{1,0:T(8,128)S(1)}) custom-call(s32[1,4]{1,0:T(1,128)S(1)} %copy-done.5, s32[1]{0:T(128)S(6)} %copy.14.refs_1_, f32[16,1536]{1,0:T(8,128)S(1)} %copy-done.2, ...), custom_call_target="tpu_custom_call" | custom-call | tf_op jit(solution)/shard_map/pallas_call | solution.py:349
  49.9 19.4 %all-to-all-start.1 = ((f32[128,1,128]{2,1,0:T(1,128)}), f32[128,1,128]{2,1,0:T(1,128)S(1)}, u32[]{:S(2)}, u32[]{:S(2)}) async-start(f32[128,1,128]{2,1,0:T(1,128)} %bitcast.4), calls=%async_computation.1 | async-start | bytes 131072 | tf_op jit(solution)/shard_map/all_to_all | solution.py:379
  69.3 2.8 %collective-permute-start.4 = (f32[16,640]{1,0:T(8,128)S(1)}, f32[16,640]{1,0:T(8,128)S(1)}, u32[]{:S(2)}, u32[]{:S(2)}) collective-permute-start(f32[16,640]{1,0:T(8,128)S(1)} %get-tuple-element.39), channel_id=1, source_target_pairs={{0,4},{4,0},{8,12},{12,8},{16,20},{20,16},{24,28},{28,24},{32,36},... | collective-permute-start | bytes 122888 | tf_op jit(solution)/shard_map/ppermute | solution.py:361
  72.1 2.8 %collective-permute-start.5 = (f32[16,640]{1,0:T(8,128)S(1)}, f32[16,640]{1,0:T(8,128)S(1)}, u32[]{:S(2)}, u32[]{:S(2)}) collective-permute-start(f32[16,640]{1,0:T(8,128)S(1)} %get-tuple-element.40), channel_id=1, source_target_pairs={{0,508},{4,8},{8,4},{12,16},{16,12},{20,24},{24,20},{28,32},{32,28... | collective-permute-start | bytes 122888 | tf_op jit(solution)/shard_map/ppermute | solution.py:361
  74.9 7.3 %collective-permute-start.3 = (f32[16,512]{1,0:T(8,128)S(1)}, f32[16,512]{1,0:T(8,128)S(1)}, u32[]{:S(2)}, u32[]{:S(2)}) collective-permute-start(f32[16,512]{1,0:T(8,128)S(1)} %get-tuple-element.38), channel_id=1, source_target_pairs={{0,256},{4,260},{8,264},{12,268},{16,272},{20,276},{24,280},{28,28... | collective-permute-start | bytes 98312 | tf_op jit(solution)/shard_map/ppermute | solution.py:361
  83.5 5.1 %shard_map.88 = (f32[16,4608]{1,0:T(8,128)S(1)}, f32[16,2304]{1,0:T(8,128)S(1)}, f32[128,128]{1,0:T(8,128)}, f32[16,512]{1,0:T(8,128)S(1)}, f32[16,640]{1,0:T(8,128)S(1)}, /*index=5*/f32[16,640]{1,0:T(8,128)S(1)}) custom-call(s32[1,4]{1,0:T(1,128)S(1)} %copy-done.5, s32[1]{0:T(128)S(6)} %copy.14.refs_1_, f32[128,128]{1,0:T(8,128)S(1)} %bitcast.29, ...), custom_call_target="tpu_custom_call" | custom-call | tf_op jit(solution)/shard_map/pallas_call | solution.py:349
  88.7 14.1 %all-to-all-start.2 = ((f32[128,1,128]{2,1,0:T(1,128)}), f32[128,1,128]{2,1,0:T(1,128)S(1)}, u32[]{:S(2)}, u32[]{:S(2)}) async-start(f32[128,1,128]{2,1,0:T(1,128)} %bitcast.7), calls=%async_computation.2 | async-start | bytes 131072 | tf_op jit(solution)/shard_map/all_to_all | solution.py:379
  102.7 2.8 %collective-permute-start.7 = (f32[16,640]{1,0:T(8,128)S(1)}, f32[16,640]{1,0:T(8,128)S(1)}, u32[]{:S(2)}, u32[]{:S(2)}) collective-permute-start(f32[16,640]{1,0:T(8,128)S(1)} %get-tuple-element.46), channel_id=1, source_target_pairs={{0,4},{4,0},{8,12},{12,8},{16,20},{20,16},{24,28},{28,24},{32,36},... | collective-permute-start | bytes 122888 | tf_op jit(solution)/shard_map/ppermute | solution.py:361
  105.6 2.8 %collective-permute-start.8 = (f32[16,640]{1,0:T(8,128)S(1)}, f32[16,640]{1,0:T(8,128)S(1)}, u32[]{:S(2)}, u32[]{:S(2)}) collective-permute-start(f32[16,640]{1,0:T(8,128)S(1)} %get-tuple-element.47), channel_id=1, source_target_pairs={{0,508},{4,8},{8,4},{12,16},{16,12},{20,24},{24,20},{28,32},{32,28... | collective-permute-start | bytes 122888 | tf_op jit(solution)/shard_map/ppermute | solution.py:361
  108.3 7.3 %collective-permute-start.6 = (f32[16,512]{1,0:T(8,128)S(1)}, f32[16,512]{1,0:T(8,128)S(1)}, u32[]{:S(2)}, u32[]{:S(2)}) collective-permute-start(f32[16,512]{1,0:T(8,128)S(1)} %get-tuple-element.45), channel_id=1, source_target_pairs={{0,256},{4,260},{8,264},{12,268},{16,272},{20,276},{24,280},{28,28... | collective-permute-start | bytes 98312 | tf_op jit(solution)/shard_map/ppermute | solution.py:361
  117.0 5.1 %shard_map.89 = (f32[16,4608]{1,0:T(8,128)S(1)}, f32[16,2304]{1,0:T(8,128)S(1)}, f32[128,128]{1,0:T(8,128)}, f32[16,512]{1,0:T(8,128)S(1)}, f32[16,640]{1,0:T(8,128)S(1)}, /*index=5*/f32[16,640]{1,0:T(8,128)S(1)}) custom-call(s32[1,4]{1,0:T(1,128)S(1)} %copy-done.5, s32[1]{0:T(128)S(6)} %copy.14.refs_1_, f32[128,128]{1,0:T(8,128)S(1)} %bitcast.30, ...), custom_call_target="tpu_custom_call" | custom-call | tf_op jit(solution)/shard_map/pallas_call | solution.py:349
  122.1 14.1 %all-to-all-start.3 = ((f32[128,1,128]{2,1,0:T(1,128)}), f32[128,1,128]{2,1,0:T(1,128)S(1)}, u32[]{:S(2)}, u32[]{:S(2)}) async-start(f32[128,1,128]{2,1,0:T(1,128)} %bitcast.10), calls=%async_computation.3 | async-start | bytes 131072 | tf_op jit(solution)/shard_map/all_to_all | solution.py:379
  136.2 2.8 %collective-permute-start.10 = (f32[16,640]{1,0:T(8,128)S(1)}, f32[16,640]{1,0:T(8,128)S(1)}, u32[]{:S(2)}, u32[]{:S(2)}) collective-permute-start(f32[16,640]{1,0:T(8,128)S(1)} %get-tuple-element.52), channel_id=1, source_target_pairs={{0,4},{4,0},{8,12},{12,8},{16,20},{20,16},{24,28},{28,24},{32,36},... | collective-permute-start | bytes 122888 | tf_op jit(solution)/shard_map/ppermute | solution.py:361
  141.8 7.5 %collective-permute-start.9 = (f32[16,512]{1,0:T(8,128)S(1)}, f32[16,512]{1,0:T(8,128)S(1)}, u32[]{:S(2)}, u32[]{:S(2)}) collective-permute-start(f32[16,512]{1,0:T(8,128)S(1)} %get-tuple-element.51), channel_id=1, source_target_pairs={{0,256},{4,260},{8,264},{12,268},{16,272},{20,276},{24,280},{28,28... | collective-permute-start | bytes 98312 | tf_op jit(solution)/shard_map/ppermute | solution.py:361
  150.5 5.1 %shard_map.90 = (f32[16,4608]{1,0:T(8,128)S(1)}, f32[16,2304]{1,0:T(8,128)}, f32[128,128]{1,0:T(8,128)S(1)}, f32[16,512]{1,0:T(8,128)}, f32[16,640]{1,0:T(8,128)}, /*index=5*/f32[16,640]{1,0:T(8,128)}) custom-call(s32[1,4]{1,0:T(1,128)S(1)} %copy-done.5, s32[1]{0:T(128)S(6)} %copy.14.refs_1_, f32[128,128]{1,0:T(8,128)S(1)} %bitcast.28, ...), custom_call_target="tpu_custom_call" | custom-call | tf_op jit(solution)/shard_map/pallas_call | solution.py:349
  155.5 25.4 %all_to_all.30 = f32[128,1,128]{2,1,0:T(1,128)S(1)} all-to-all(f32[128,1,128]{2,1,0:T(1,128)S(1)} %bitcast.32), channel_id=1, replica_groups=mesh['sub'=128,'case'=4] {'sub'}, dimensions={0} | all-to-all | bytes 131072 | tf_op jit(solution)/shard_map/all_to_all | solution.py:379
  181.7 8.4 %all_to_all.31 = f32[4,1,128]{2,1,0:T(1,128)S(1)} all-to-all(f32[4,1,128]{2,1,0:T(1,128)S(1)} %bitcast.37), channel_id=1, replica_groups=mesh['sub'=128,'case'=4] {'case'}, dimensions={0} | all-to-all | bytes 4096 | tf_op jit(solution)/shard_map/all_to_all | solution.py:379
  (33 shorter events, 9.2 us)
Async XLA Ops:
  0.6 43.9 %copy-start.5 = (s32[1,4]{1,0:T(1,128)S(1)}, s32[1,4]{1,0:T(1,128)}, u32[]{:S(2)}) copy-start(s32[1,4]{1,0:T(1,128)} %refs_0_.9) | copy-start | bytes 52
  0.6 43.9 %copy-start.2 = (f32[16,1536]{1,0:T(8,128)S(1)}, f32[16,1536]{1,0:T(8,128)}, u32[]{:S(2)}) copy-start(f32[16,1536]{1,0:T(8,128)} %refs_2_.3) | copy-start | bytes 294916
  0.7 43.9 %copy-start.1 = (bf16[1,4,128,128]{3,2,1,0:T(8,128)(2,1)S(1)}, bf16[1,4,128,128]{3,2,1,0:T(8,128)(2,1)}, u32[]{:S(2)}) copy-start(bf16[1,4,128,128]{3,2,1,0:T(8,128)(2,1)} %param.11) | copy-start | bytes 393220
  0.7 43.9 %copy-start.4 = (s32[1,2,128]{2,1,0:T(2,128)S(1)}, s32[1,2,128]{2,1,0:T(2,128)}, u32[]{:S(2)}) copy-start(s32[1,2,128]{2,1,0:T(2,128)} %param.10) | copy-start | bytes 3076
  5.8 18.0 %collective-permute-start.2 = (bf16[336,512]{1,0:T(8,128)(2,1)}, bf16[336,512]{1,0:T(8,128)(2,1)S(1)}, u32[]{:S(2)}, u32[]{:S(2)}) collective-permute-start(bf16[336,512]{1,0:T(8,128)(2,1)} %get-tuple-element.33), channel_id=1, source_target_pairs={{0,256},{4,260},{8,264},{12,268},{16,272},{20,276},{24,280},{28,28... | collective-permute-start | bytes 1032200 | tf_op jit(solution)/shard_map/ppermute | solution.py:361
  23.8 59.7 %copy-start = (bf16[336,512]{1,0:T(8,128)(2,1)}, bf16[336,512]{1,0:T(8,128)(2,1)S(1)}, u32[]{:S(2)}) copy-start(bf16[336,512]{1,0:T(8,128)(2,1)S(1)} %collective-permute-done.2.refs_7_.refs_9_) | copy-start | bytes 1032196
  24.7 25.1 %all-to-all-start = ((bf16[4,128,512]{2,1,0:T(8,128)(2,1)}), bf16[4,128,512]{2,1,0:T(8,128)(2,1)S(1)}, u32[]{:S(2)}, u32[]{:S(2)}) async-start(bf16[4,128,512]{2,1,0:T(8,128)(2,1)} %broadcast_in_dim.2), calls=%async_computation | async-start | bytes 1048576 | tf_op jit(solution)/shard_map/all_to_all | solution.py:407
  28.6 12.5 %collective-permute-start = (bf16[704,128]{1,0:T(8,128)(2,1)}, bf16[704,128]{1,0:T(8,128)(2,1)S(1)}, u32[]{:S(2)}, u32[]{:S(2)}) collective-permute-start(bf16[704,128]{1,0:T(8,128)(2,1)} %get-tuple-element.31), channel_id=1, source_target_pairs={{0,4},{4,0},{8,12},{12,8},{16,20},{20,16},{24,28},{28,24},{32,36},... | collective-permute-start | bytes 540680 | tf_op jit(solution)/shard_map/ppermute | solution.py:361
  37.2 7.3 %collective-permute-start.1 = (bf16[704,128]{1,0:T(8,128)(2,1)}, bf16[704,128]{1,0:T(8,128)(2,1)S(1)}, u32[]{:S(2)}, u32[]{:S(2)}) collective-permute-start(bf16[704,128]{1,0:T(8,128)(2,1)} %get-tuple-element.32), channel_id=1, source_target_pairs={{0,508},{4,8},{8,4},{12,16},{16,12},{20,24},{24,20},{28,32},{32,28... | collective-permute-start | bytes 540680 | tf_op jit(solution)/shard_map/ppermute | solution.py:361
  44.5 0.9 copy-start.3
  49.9 33.7 %copy-start.6 = (bf16[4,128,512]{2,1,0:T(8,128)(2,1)}, bf16[4,128,512]{2,1,0:T(8,128)(2,1)S(1)}, u32[]{:S(2)}) copy-start(bf16[4,128,512]{2,1,0:T(8,128)(2,1)S(1)} %all-to-all-done) | copy-start | bytes 1572868
  49.9 33.6 %all-to-all-start.1 = ((f32[128,1,128]{2,1,0:T(1,128)}), f32[128,1,128]{2,1,0:T(1,128)S(1)}, u32[]{:S(2)}, u32[]{:S(2)}) async-start(f32[128,1,128]{2,1,0:T(1,128)} %bitcast.4), calls=%async_computation.1 | async-start | bytes 131072 | tf_op jit(solution)/shard_map/all_to_all | solution.py:379
  69.3 14.2 %collective-permute-start.4 = (f32[16,640]{1,0:T(8,128)S(1)}, f32[16,640]{1,0:T(8,128)S(1)}, u32[]{:S(2)}, u32[]{:S(2)}) collective-permute-start(f32[16,640]{1,0:T(8,128)S(1)} %get-tuple-element.39), channel_id=1, source_target_pairs={{0,4},{4,0},{8,12},{12,8},{16,20},{20,16},{24,28},{28,24},{32,36},... | collective-permute-start | bytes 122888 | tf_op jit(solution)/shard_map/ppermute | solution.py:361
  72.1 11.4 %collective-permute-start.5 = (f32[16,640]{1,0:T(8,128)S(1)}, f32[16,640]{1,0:T(8,128)S(1)}, u32[]{:S(2)}, u32[]{:S(2)}) collective-permute-start(f32[16,640]{1,0:T(8,128)S(1)} %get-tuple-element.40), channel_id=1, source_target_pairs={{0,508},{4,8},{8,4},{12,16},{16,12},{20,24},{24,20},{28,32},{32,28... | collective-permute-start | bytes 122888 | tf_op jit(solution)/shard_map/ppermute | solution.py:361
  74.9 8.7 %collective-permute-start.3 = (f32[16,512]{1,0:T(8,128)S(1)}, f32[16,512]{1,0:T(8,128)S(1)}, u32[]{:S(2)}, u32[]{:S(2)}) collective-permute-start(f32[16,512]{1,0:T(8,128)S(1)} %get-tuple-element.38), channel_id=1, source_target_pairs={{0,256},{4,260},{8,264},{12,268},{16,272},{20,276},{24,280},{28,28... | collective-permute-start | bytes 98312 | tf_op jit(solution)/shard_map/ppermute | solution.py:361
  88.7 28.3 %all-to-all-start.2 = ((f32[128,1,128]{2,1,0:T(1,128)}), f32[128,1,128]{2,1,0:T(1,128)S(1)}, u32[]{:S(2)}, u32[]{:S(2)}) async-start(f32[128,1,128]{2,1,0:T(1,128)} %bitcast.7), calls=%async_computation.2 | async-start | bytes 131072 | tf_op jit(solution)/shard_map/all_to_all | solution.py:379
  102.7 14.2 %collective-permute-start.7 = (f32[16,640]{1,0:T(8,128)S(1)}, f32[16,640]{1,0:T(8,128)S(1)}, u32[]{:S(2)}, u32[]{:S(2)}) collective-permute-start(f32[16,640]{1,0:T(8,128)S(1)} %get-tuple-element.46), channel_id=1, source_target_pairs={{0,4},{4,0},{8,12},{12,8},{16,20},{20,16},{24,28},{28,24},{32,36},... | collective-permute-start | bytes 122888 | tf_op jit(solution)/shard_map/ppermute | solution.py:361
  105.6 11.4 %collective-permute-start.8 = (f32[16,640]{1,0:T(8,128)S(1)}, f32[16,640]{1,0:T(8,128)S(1)}, u32[]{:S(2)}, u32[]{:S(2)}) collective-permute-start(f32[16,640]{1,0:T(8,128)S(1)} %get-tuple-element.47), channel_id=1, source_target_pairs={{0,508},{4,8},{8,4},{12,16},{16,12},{20,24},{24,20},{28,32},{32,28... | collective-permute-start | bytes 122888 | tf_op jit(solution)/shard_map/ppermute | solution.py:361
  108.3 8.7 %collective-permute-start.6 = (f32[16,512]{1,0:T(8,128)S(1)}, f32[16,512]{1,0:T(8,128)S(1)}, u32[]{:S(2)}, u32[]{:S(2)}) collective-permute-start(f32[16,512]{1,0:T(8,128)S(1)} %get-tuple-element.45), channel_id=1, source_target_pairs={{0,256},{4,260},{8,264},{12,268},{16,272},{20,276},{24,280},{28,28... | collective-permute-start | bytes 98312 | tf_op jit(solution)/shard_map/ppermute | solution.py:361
  122.1 28.3 %all-to-all-start.3 = ((f32[128,1,128]{2,1,0:T(1,128)}), f32[128,1,128]{2,1,0:T(1,128)S(1)}, u32[]{:S(2)}, u32[]{:S(2)}) async-start(f32[128,1,128]{2,1,0:T(1,128)} %bitcast.10), calls=%async_computation.3 | async-start | bytes 131072 | tf_op jit(solution)/shard_map/all_to_all | solution.py:379
  136.2 14.2 %collective-permute-start.10 = (f32[16,640]{1,0:T(8,128)S(1)}, f32[16,640]{1,0:T(8,128)S(1)}, u32[]{:S(2)}, u32[]{:S(2)}) collective-permute-start(f32[16,640]{1,0:T(8,128)S(1)} %get-tuple-element.52), channel_id=1, source_target_pairs={{0,4},{4,0},{8,12},{12,8},{16,20},{20,16},{24,28},{28,24},{32,36},... | collective-permute-start | bytes 122888 | tf_op jit(solution)/shard_map/ppermute | solution.py:361
  139.0 11.4 %collective-permute-start.11 = (f32[16,640]{1,0:T(8,128)S(1)}, f32[16,640]{1,0:T(8,128)S(1)}, u32[]{:S(2)}, u32[]{:S(2)}) collective-permute-start(f32[16,640]{1,0:T(8,128)S(1)} %get-tuple-element.53), channel_id=1, source_target_pairs={{0,508},{4,8},{8,4},{12,16},{16,12},{20,24},{24,20},{28,32},{32,28... | collective-permute-start | bytes 122888 | tf_op jit(solution)/shard_map/ppermute | solution.py:361
  141.8 8.7 %collective-permute-start.9 = (f32[16,512]{1,0:T(8,128)S(1)}, f32[16,512]{1,0:T(8,128)S(1)}, u32[]{:S(2)}, u32[]{:S(2)}) collective-permute-start(f32[16,512]{1,0:T(8,128)S(1)} %get-tuple-element.51), channel_id=1, source_target_pairs={{0,256},{4,260},{8,264},{12,268},{16,272},{20,276},{24,280},{28,28... | collective-permute-start | bytes 98312 | tf_op jit(solution)/shard_map/ppermute | solution.py:361

commit v4 on v3

--- a/solution.py
+++ b/solution.py
@@ -178,10 +178,10 @@
     near_x, near_lift = moved_by(near_x, step, near[:, BLK:])
     far_x, far_lift = moved_by(far_x, step, far[:, BLK:])
     part, mate_part = contact_terms(lift, mate_lift, statics, True)
-    mate_g = mate_g - step * mate + fine_dot(mate_lift, mate_kernel[...]) + mate_part
+    mate_g = mate_g - step * mate + symmetric_dot(mate_lift, mate_kernel) + mate_part
     near_face = near_face - step * near[:, :BLK] + fine_dot(near_lift, near_kernel[...])
     far_face = far_face - step * far[:, :BLK] + fine_dot(far_lift, far_kernel[...])
-    lifted = whole_dot(lift, [(start - LOW, size, piece) for start, size, piece in rows()])
+    lifted = whole_dot(lift, rows)
     g = g - step * image + lifted
     g = jnp.concatenate([g[:, :LOW], g[:, LOW:HIGH] + part, g[:, HIGH:]], axis=1)
     return x, g, [mate_x, mate_g, near_x, far_x, near_face, far_face]
@@ -191,12 +191,12 @@
 STARTS = (LOW, LOW + CHUNK) + (0,) + tuple(range(HIGH, M, CHUNK))
 
 
-def whole_copy(dual_hbm, dual_ref, sems):
+def whole_copy(dual_hbm, dual_ref, sems, starts=None):
     copies = []
-    for index, start in enumerate(STARTS):
-        rows = pl.ds(start, CHUNK)
+    for index, start in enumerate(starts or STARTS):
+        span = pl.ds(start, CHUNK)
         copies.append(
-            pltpu.make_async_copy(dual_hbm.at[rows], dual_ref.at[rows], sems.at[index])
+            pltpu.make_async_copy(dual_hbm.at[span], dual_ref.at[span], sems.at[index])
         )
     for copy in copies:
         copy.start()
@@ -214,8 +214,8 @@
 
 TABLE = 4 * CASES
 SLOTS = TABLE + CASES
-QUARTER = SLOTS + BLK
-PACKED = QUARTER + BLK
+UPPER = SLOTS + BLK
+PACKED = UPPER + 2 * BLK + BLK // 2
 SIDE = 12 * CASES
 
 
@@ -226,6 +226,46 @@
 def halves(block):
     high = block.astype(bf16)
     return high, (block - high.astype(f32)).astype(bf16)
+
+
+def upper_places():
+    half = BLK // 2
+    places = {}
+    for k in range(4):
+        places[0, k] = [(UPPER, BLK, k)]
+    for k in range(1, 4):
+        places[1, k] = [(UPPER + BLK, BLK, k)]
+    places[3, 3] = [(UPPER + BLK, BLK, 0)]
+    for k in (2, 3):
+        lane = 2 * (k - 2)
+        places[2, k] = [(UPPER + 2 * BLK, half, lane), (UPPER + 2 * BLK, half, lane + 1)]
+    return places
+
+
+def store_upper(packed, dual_ref):
+    for (i, j), places in upper_places().items():
+        start = LOW + i * BLK
+        for row, size, lane in places:
+            block = dual_ref[start : start + size, LOW + j * BLK : LOW + (j + 1) * BLK]
+            packed[row : row + size, lane * BLK : (lane + 1) * BLK] = block
+            start = start + size
+
+
+def symmetric_dot(value, packed):
+    high, low = halves(value)
+    both = split(jnp.concatenate([high, low], axis=0))
+    blocks = {}
+    for key, places in upper_places().items():
+        parts = [packed[row : row + n, lane * BLK : (lane + 1) * BLK] for row, n, lane in places]
+        blocks[key] = parts[0] if len(parts) == 1 else jnp.concatenate(parts, axis=0)
+    outs = []
+    for j in range(4):
+        total = None
+        for i in range(4):
+            part = dot(both[i], blocks[min(i, j), max(i, j)], i > j)
+            total = part if total is None else total + part
+        outs.append(total[:CASES] + total[CASES:])
+    return jnp.concatenate(outs, axis=1)
 
 
 def prepare_kernel(*refs):
@@ -234,14 +274,13 @@
     piece = whole_copy(dual_hbm, dual_ref, sems)
     even = is_even()
     for k in range(4):
-        packed[SLOTS:QUARTER, k * BLK : (k + 1) * BLK] = mortar[k * BLK : (k + 1) * BLK, :]
+        packed[SLOTS:UPPER, k * BLK : (k + 1) * BLK] = mortar[k * BLK : (k + 1) * BLK, :]
     table = slot_table(ids, count).astype(bf16)
     packed[TABLE:SLOTS, :] = jnp.concatenate([table] * 4, axis=1)
     x = x_ref[...]
     q = whole_dot(x, [piece(k, True) for k in range(len(STARTS))]) - right_ref[...]
     q_ref[...] = q
-    start = pl.multiple_of(LOW + lax.rem(lax.axis_index("case"), 4) * BLK, BLK)
-    packed[QUARTER:, :] = dual_ref[pl.ds(start, BLK), LOW:HIGH]
+    store_upper(packed, dual_ref)
     parts = halves(x[:, LOW:HIGH]) + halves(q[:, LOW:HIGH])
     for k, part in enumerate(parts):
         packed[k * CASES : (k + 1) * CASES, :] = part
@@ -259,7 +298,7 @@
 
 def statics_of(ids, count, mortar, packed):
     own = [mortar[k * BLK : (k + 1) * BLK, :] for k in range(4)]
-    mate = [packed[SLOTS:QUARTER, k * BLK : (k + 1) * BLK] for k in range(4)]
+    mate = [packed[SLOTS:UPPER, k * BLK : (k + 1) * BLK] for k in range(4)]
     mate_table = packed[TABLE:SLOTS, :BLK].astype(f32)
     return slots(slot_table(ids, count)), own, slots(mate_table), mate
 
@@ -303,19 +342,12 @@
 WIDTHS = (CONTACT, CONTACT, CONTACT, CONTACT, BLK, BLK)
 
 
-def advance_kernel(*refs):
-    ids, count, sums, own, others, mate, near, far, mortar, packed, match = refs[:11]
-    mate_kernel, near_kernel, far_kernel, dual_hbm = refs[11:15]
-    outs, (dual_ref, sems) = refs[15:21], refs[21:]
-    piece = whole_copy(dual_hbm, dual_ref, sems)
-    even = is_even()
+def advanced(refs, piece):
+    ids, count, sums, own, others, mate, near, far, mortar, packed, _ = refs[:11]
+    near_kernel, far_kernel = refs[11:13]
     statics = statics_of(ids, count, mortar, packed)
-    pick = picks(match[...], even)
-
-    def rows():
-        return [piece(k, True) for k in range(2)]
-
     offsets = [sum(WIDTHS[:k]) for k in range(len(WIDTHS))]
+    lift_rows = [(k * CHUNK, CHUNK, piece(k, True)[2]) for k in range(2)]
     x, g, others = advance(
         sums[...],
         (own[:, :M], own[:, M : 2 * M], own[:, 2 * M :]),
@@ -324,19 +356,61 @@
         near[...],
         far[...],
         statics,
-        rows,
-        (mate_kernel, near_kernel.at[SIDE:], far_kernel.at[SIDE:]),
-    )
+        lift_rows,
+        (packed, near_kernel.at[SIDE:], far_kernel.at[SIDE:]),
+    )
+    return x, g, others, statics
+
+
+def advance_kernel(*refs):
+    dual_hbm, outs, (dual_ref, sems) = refs[13], refs[14:20], refs[20:]
+    piece = whole_copy(dual_hbm, dual_ref, sems)
+    even = is_even()
+    x, g, others, statics = advanced(refs[:13], piece)
+    pick = picks(refs[10][...], even)
     pieces = [piece(k, k >= 2) for k in range(len(STARTS))]
     image, row = tail(g, others, statics, pick, even, pieces)
     emit(outs, x, g, image, row, others)
 
 
+def last_advance_kernel(*refs):
+    dual_hbm, (own_out, others_out, row_out), (dual_ref, sems) = refs[13], refs[14:17], refs[17:]
+    piece = whole_copy(dual_hbm, dual_ref, sems, STARTS[:2])
+    x, g, others, _ = advanced(refs[:13], piece)
+    own_out[:, :M] = x
+    own_out[:, M:] = g
+    others_out[...] = jnp.concatenate([others[1], others[4], others[5]], axis=1)
+    total = jnp.sum(jnp.sum(g * g, axis=1, keepdims=True), axis=0, keepdims=True)
+    row_out[...] = jnp.broadcast_to(total, row_out.shape)
+
+
+def last_tail_kernel(*refs):
+    ids, count, own, others, mortar, packed, match, dual_hbm = refs[:8]
+    row_out, dual_ref, sems = refs[8:]
+    piece = whole_copy(dual_hbm, dual_ref, sems)
+    even = is_even()
+    statics = statics_of(ids, count, mortar, packed)
+    pick = picks(match[...], even)
+    others = [
+        None,
+        others[:, :CONTACT],
+        None,
+        None,
+        others[:, CONTACT : CONTACT + BLK],
+        others[:, CONTACT + BLK :],
+    ]
+    pieces = [piece(k, True) for k in range(len(STARTS))]
+    _, row = tail(own[:, M:], others, statics, pick, even, pieces)
+    row_out[...] = jnp.broadcast_to(row, row_out.shape)
+
+
 def finish_kernel(sums, own, x_out, norm_out):
-    norm, step = step_of(sums[...])
+    rows = sums[...]
+    _, step = step_of(rows)
     x, _ = all_moved(own[:, :M], step, own[:, M : 2 * M])
     x_out[...] = x
-    norm_out[...] = jnp.broadcast_to(jnp.sum(norm, axis=0, keepdims=True), norm_out.shape)
+    total = jnp.sum(rows, axis=0, keepdims=True)[:, 2 * CASES : 2 * CASES + 1]
+    norm_out[...] = jnp.broadcast_to(jnp.sqrt(total), norm_out.shape)
 
 
 VMEM_SPEC = pl.BlockSpec(memory_space=pltpu.VMEM)
@@ -401,11 +475,6 @@
     packed = with_mate(packed)
     near = near_kernel = with_near(to_near)
     far = far_kernel = with_far(to_far)
-    cases = lax.axis_size("case")
-    quarter = packed[QUARTER:]
-    quarters = jnp.broadcast_to(quarter[None], (cases,) + quarter.shape)
-    quarters = lax.all_to_all(quarters, "case", 0, 0)
-    mate_kernel = quarters.reshape(cases * BLK, CONTACT)
 
     shapes = [
         ((CASES, 3 * M), f32),
@@ -424,32 +493,52 @@
             dual_ops,
         ),
     )
-    copies, mate_kernel = lax.optimization_barrier((copies, mate_kernel))
-    for _ in range(1, ITERS):
+    for iteration in range(1, ITERS):
         sums = spread_sums(copies, "sub")
         mate = with_mate(to_mate)
         far = with_far(to_far)
         near = with_near(to_near)
-        own, others, copies, to_mate, to_near, to_far = call(
-            advance_kernel,
-            scalars + [VMEM_SPEC] * 12 + [HBM_SPEC],
-            shapes,
-            (
-                contact_ids, contact_count, sums, own, others, mate, near, far, mortar,
-                packed, match, mate_kernel, near_kernel, far_kernel, dual_ops,
-            ),
+        operands = (
+            contact_ids, contact_count, sums, own, others, mate, near, far, mortar, packed,
+            match, near_kernel, far_kernel, dual_ops,
         )
-    sums = spread_sums(copies, "sub")
+        if iteration < ITERS - 1:
+            own, others, copies, to_mate, to_near, to_far = call(
+                advance_kernel,
+                scalars + [VMEM_SPEC] * 11 + [HBM_SPEC],
+                shapes,
+                operands,
+            )
+    cases = lax.axis_size("case")
+    own, others, norms = call(
+        last_advance_kernel,
+        scalars + [VMEM_SPEC] * 11 + [HBM_SPEC],
+        [
+            ((CASES, 2 * M), f32),
+            ((CASES, CONTACT + 2 * BLK), f32),
+            ((cases, BLK), f32),
+        ],
+        operands,
+    )
+    norms = spread_sums(norms, "case")
+    (copies,) = call(
+        last_tail_kernel,
+        scalars + [VMEM_SPEC] * 5 + [HBM_SPEC],
+        [((devices, BLK), f32)],
+        (contact_ids, contact_count, own, others, mortar, packed, match, dual_ops),
+    )
+    lane = lax.broadcasted_iota(jnp.int32, (1, BLK), 1)
+    norm_row = jnp.where(lane == 2 * CASES, jnp.sum(norms, axis=0, keepdims=True), 0.0)
+    sums = spread_sums(copies + norm_row, "sub")
     x, norm = call(
         finish_kernel,
         [VMEM_SPEC, VMEM_SPEC],
-        [((CASES, M), f32), ((lax.axis_size("case"), BLK), f32)],
+        [((CASES, M), f32), ((1, BLK), f32)],
         (sums, own),
         scratch=False,
         grant=16,
     )
-    total = spread_sums(norm, "case").sum(0)
-    return (x, jnp.sqrt(total[:1]))
+    return (x, norm[0, :1])
 
 
 PREPARE_GRANT = 60

time: 192 us -> 183 us (0.953)
  blocking collectives: 33.9 us -> 26.9 us
  waiting for transfers between devices: 16.8 us -> 12.5 us
  starting transfers between devices: 111 us -> 114 us
    all_to_all x3 -> x4, starting transfers between devices: 47.5 us -> 60.3 us  [spread_sums(): rows = lax.all_to_all(copies.reshape(devices, 1, BLK), axis, 0, 0)]
    all_to_all x2 -> x1, blocking collectives: 33.9 us -> 26.9 us  [spread_sums(): rows = lax.all_to_all(copies.reshape(devices, 1, BLK), axis, 0, 0)]
    ppermute x12, starting transfers between devices: 59.6 us -> 53.9 us  [swapped(): lax.ppermute(value, 'sub', [(i, other(i) % devices) for i in range(device...]
    ppermute x12, waiting for transfers between devices: 16.8 us -> 11.9 us  [swapped(): lax.ppermute(value, 'sub', [(i, other(i) % devices) for i in range(device...]
    all_to_all x1 -> x0, starting transfers between devices: 3.9 us -> none  [on_device(): quarters = lax.all_to_all(quarters, 'case', 0, 0)]
    pallas_call x6 -> x7, Pallas kernels: 25 us -> 26.1 us  [call(): pl.pallas_call(kernel, in_specs=specs, out_specs=[VMEM_SPEC] * len(shapes...]
  transfers between devices with their start and end apart: 16 -> 16, of which waited for: 5 -> 6; matrix products, arithmetic and copies ran while one was open for 0% -> 0% of each run, Pallas kernels for 2% -> 2%
where the time goes in v4:
time: 183 us; the launch traced here: 182 us
  starting transfers between devices  114 us (62%)
  blocking collectives  26.9 us (15%)
  Pallas kernels  26.1 us (14%)
  waiting for transfers between devices  12.5 us (7%)
    all_to_all x4, starting transfers between devices, spread_sums(): rows = lax.all_to_all(copies.reshape(devices, 1, BLK), axis, 0, 0)  60.3 us
    ppermute x12, starting transfers between devices, swapped(): lax.ppermute(value, 'sub', [(i, other(i) % devices) for i in range(device...  53.9 us
    all_to_all x1, blocking collectives, spread_sums(): rows = lax.all_to_all(copies.reshape(devices, 1, BLK), axis, 0, 0)  26.9 us
    pallas_call x7, Pallas kernels, call(): pl.pallas_call(kernel, in_specs=specs, out_specs=[VMEM_SPEC] * len(shapes...  26.1 us
    ppermute x12, waiting for transfers between devices, swapped(): lax.ppermute(value, 'sub', [(i, other(i) % devices) for i in range(device...  11.9 us
  transfers between devices with their start and end apart: 16, of which 6 were waited for; matrix products, arithmetic and copies ran while one was open for 0% of the time, Pallas kernels for 2%

profile of v4, /device:TPU:1, one launch (start us, length us, event | category | flops | bytes accessed | tf_op | source)
XLA Modules:
  0.0 182.4 jit_solution(8711329346635131004)
XLA Ops:
  1.4 4.5 %shard_map.86 = (f32[16,1536]{1,0:T(8,128)}, bf16[528,512]{1,0:T(8,128)(2,1)}, bf16[704,128]{1,0:T(8,128)(2,1)}, bf16[704,128]{1,0:T(8,128)(2,1)}) custom-call(s32[1,4]{1,0:T(1,128)} %refs_0_.11, s32[1]{0:T(128)S(6)} %copy.14.refs_1_, f32[16,1536]{1,0:T(8,128)} %refs_2_.3, f32[16,1536]{1,0:T(8,128)} %refs_3_.1, bf16[512,128]{1,0:T(8,128)(2,1)} %bitcast.23, ...), custom_call_target="tpu_custom_call" | custom-call | tf_op jit(solution)/shard_map/pallas_call | solution.py:423
  5.9 8.3 %collective-permute-start.2 = (bf16[528,512]{1,0:T(8,128)(2,1)}, bf16[528,512]{1,0:T(8,128)(2,1)S(1)}, u32[]{:S(2)}, u32[]{:S(2)}) collective-permute-start(bf16[528,512]{1,0:T(8,128)(2,1)} %get-tuple-element.32), channel_id=1, source_target_pairs={{0,256},{4,260},{8,264},{12,268},{16,272},{20,276},{24,280},{28,28... | collective-permute-start | bytes 1622024 | tf_op jit(solution)/shard_map/ppermute | solution.py:435
  14.2 2.9 %collective-permute-start = (bf16[704,128]{1,0:T(8,128)(2,1)}, bf16[704,128]{1,0:T(8,128)(2,1)S(1)}, u32[]{:S(2)}, u32[]{:S(2)}) collective-permute-start(bf16[704,128]{1,0:T(8,128)(2,1)} %get-tuple-element.30), channel_id=1, source_target_pairs={{0,4},{4,0},{8,12},{12,8},{16,20},{20,16},{24,28},{28,24},{32,36},... | collective-permute-start | bytes 540680 | tf_op jit(solution)/shard_map/ppermute | solution.py:435
  17.1 3.9 %collective-permute-start.1 = (bf16[704,128]{1,0:T(8,128)(2,1)}, bf16[704,128]{1,0:T(8,128)(2,1)S(1)}, u32[]{:S(2)}, u32[]{:S(2)}) collective-permute-start(bf16[704,128]{1,0:T(8,128)(2,1)} %get-tuple-element.31), channel_id=1, source_target_pairs={{0,508},{4,8},{8,4},{12,16},{16,12},{20,24},{24,20},{28,32},{32,28... | collective-permute-start | bytes 540680 | tf_op jit(solution)/shard_map/ppermute | solution.py:435
  21.0 3.7 %collective-permute-done.1.refs_5_.refs_12_ = bf16[704,128]{1,0:T(8,128)(2,1)S(1)} collective-permute-done((bf16[704,128]{1,0:T(8,128)(2,1)}, bf16[704,128]{1,0:T(8,128)(2,1)S(1)}, u32[]{:S(2)}, u32[]{:S(2)}) %collective-permute-start.1) | collective-permute-done | bytes 180256 | tf_op jit(solution)/shard_map/ppermute | solution.py:435
  24.6 4.4 %collective-permute-done.2.refs_7_.refs_9_.refs_5_ = bf16[528,512]{1,0:T(8,128)(2,1)S(1)} collective-permute-done((bf16[528,512]{1,0:T(8,128)(2,1)}, bf16[528,512]{1,0:T(8,128)(2,1)S(1)}, u32[]{:S(2)}, u32[]{:S(2)}) %collective-permute-start.2) | collective-permute-done | bytes 540704 | tf_op jit(solution)/shard_map/ppermute | solution.py:435
  30.1 4.5 %shard_map.87 = (f32[16,4608]{1,0:T(8,128)S(1)}, f32[16,2304]{1,0:T(8,128)S(1)}, f32[128,128]{1,0:T(8,128)}, f32[16,512]{1,0:T(8,128)S(1)}, f32[16,640]{1,0:T(8,128)S(1)}, /*index=5*/f32[16,640]{1,0:T(8,128)S(1)}) custom-call(s32[1,4]{1,0:T(1,128)S(1)} %copy-done.6, s32[1]{0:T(128)S(6)} %copy.14.refs_1_, f32[16,1536]{1,0:T(8,128)S(1)} %copy-done.3, ...), custom_call_target="tpu_custom_call" | custom-call | tf_op jit(solution)/shard_map/pallas_call | solution.py:423
  34.5 28.1 %all-to-all-start = ((f32[128,1,128]{2,1,0:T(1,128)}), f32[128,1,128]{2,1,0:T(1,128)S(1)}, u32[]{:S(2)}, u32[]{:S(2)}) async-start(f32[128,1,128]{2,1,0:T(1,128)} %bitcast.3), calls=%async_computation | async-start | bytes 131072 | tf_op jit(solution)/shard_map/all_to_all | solution.py:453
  62.6 2.8 %collective-permute-start.4 = (f32[16,640]{1,0:T(8,128)S(1)}, f32[16,640]{1,0:T(8,128)S(1)}, u32[]{:S(2)}, u32[]{:S(2)}) collective-permute-start(f32[16,640]{1,0:T(8,128)S(1)} %get-tuple-element.37), channel_id=1, source_target_pairs={{0,4},{4,0},{8,12},{12,8},{16,20},{20,16},{24,28},{28,24},{32,36},... | collective-permute-start | bytes 122888 | tf_op jit(solution)/shard_map/ppermute | solution.py:435
  65.4 2.8 %collective-permute-start.5 = (f32[16,640]{1,0:T(8,128)S(1)}, f32[16,640]{1,0:T(8,128)S(1)}, u32[]{:S(2)}, u32[]{:S(2)}) collective-permute-start(f32[16,640]{1,0:T(8,128)S(1)} %get-tuple-element.38), channel_id=1, source_target_pairs={{0,508},{4,8},{8,4},{12,16},{16,12},{20,24},{24,20},{28,32},{32,28... | collective-permute-start | bytes 122888 | tf_op jit(solution)/shard_map/ppermute | solution.py:435
  68.2 7.3 %collective-permute-start.3 = (f32[16,512]{1,0:T(8,128)S(1)}, f32[16,512]{1,0:T(8,128)S(1)}, u32[]{:S(2)}, u32[]{:S(2)}) collective-permute-start(f32[16,512]{1,0:T(8,128)S(1)} %get-tuple-element.36), channel_id=1, source_target_pairs={{0,256},{4,260},{8,264},{12,268},{16,272},{20,276},{24,280},{28,28... | collective-permute-start | bytes 98312 | tf_op jit(solution)/shard_map/ppermute | solution.py:435
  76.9 4.7 %shard_map.88 = (f32[16,4608]{1,0:T(8,128)S(1)}, f32[16,2304]{1,0:T(8,128)S(1)}, f32[128,128]{1,0:T(8,128)}, f32[16,512]{1,0:T(8,128)S(1)}, f32[16,640]{1,0:T(8,128)S(1)}, /*index=5*/f32[16,640]{1,0:T(8,128)S(1)}) custom-call(s32[1,4]{1,0:T(1,128)S(1)} %copy-done.6, s32[1]{0:T(128)S(6)} %copy.14.refs_1_, f32[128,128]{1,0:T(8,128)S(1)} %bitcast.29, ...), custom_call_target="tpu_custom_call" | custom-call | tf_op jit(solution)/shard_map/pallas_call | solution.py:423
  81.6 14.2 %all-to-all-start.1 = ((f32[128,1,128]{2,1,0:T(1,128)}), f32[128,1,128]{2,1,0:T(1,128)S(1)}, u32[]{:S(2)}, u32[]{:S(2)}) async-start(f32[128,1,128]{2,1,0:T(1,128)} %bitcast.6), calls=%async_computation.1 | async-start | bytes 131072 | tf_op jit(solution)/shard_map/all_to_all | solution.py:453
  95.8 2.8 %collective-permute-start.7 = (f32[16,640]{1,0:T(8,128)S(1)}, f32[16,640]{1,0:T(8,128)S(1)}, u32[]{:S(2)}, u32[]{:S(2)}) collective-permute-start(f32[16,640]{1,0:T(8,128)S(1)} %get-tuple-element.43), channel_id=1, source_target_pairs={{0,4},{4,0},{8,12},{12,8},{16,20},{20,16},{24,28},{28,24},{32,36},... | collective-permute-start | bytes 122888 | tf_op jit(solution)/shard_map/ppermute | solution.py:435
  98.6 2.8 %collective-permute-start.8 = (f32[16,640]{1,0:T(8,128)S(1)}, f32[16,640]{1,0:T(8,128)S(1)}, u32[]{:S(2)}, u32[]{:S(2)}) collective-permute-start(f32[16,640]{1,0:T(8,128)S(1)} %get-tuple-element.44), channel_id=1, source_target_pairs={{0,508},{4,8},{8,4},{12,16},{16,12},{20,24},{24,20},{28,32},{32,28... | collective-permute-start | bytes 122888 | tf_op jit(solution)/shard_map/ppermute | solution.py:435
  101.4 7.3 %collective-permute-start.6 = (f32[16,512]{1,0:T(8,128)S(1)}, f32[16,512]{1,0:T(8,128)S(1)}, u32[]{:S(2)}, u32[]{:S(2)}) collective-permute-start(f32[16,512]{1,0:T(8,128)S(1)} %get-tuple-element.42), channel_id=1, source_target_pairs={{0,256},{4,260},{8,264},{12,268},{16,272},{20,276},{24,280},{28,28... | collective-permute-start | bytes 98312 | tf_op jit(solution)/shard_map/ppermute | solution.py:435
  110.0 4.7 %shard_map.89 = (f32[16,4608]{1,0:T(8,128)S(1)}, f32[16,2304]{1,0:T(8,128)S(1)}, f32[128,128]{1,0:T(8,128)}, f32[16,512]{1,0:T(8,128)S(1)}, f32[16,640]{1,0:T(8,128)S(1)}, /*index=5*/f32[16,640]{1,0:T(8,128)S(1)}) custom-call(s32[1,4]{1,0:T(1,128)S(1)} %copy-done.6, s32[1]{0:T(128)S(6)} %copy.14.refs_1_, f32[128,128]{1,0:T(8,128)S(1)} %bitcast.30, ...), custom_call_target="tpu_custom_call" | custom-call | tf_op jit(solution)/shard_map/pallas_call | solution.py:423
  114.8 14.1 %all-to-all-start.2 = ((f32[128,1,128]{2,1,0:T(1,128)}), f32[128,1,128]{2,1,0:T(1,128)S(1)}, u32[]{:S(2)}, u32[]{:S(2)}) async-start(f32[128,1,128]{2,1,0:T(1,128)} %bitcast.9), calls=%async_computation.2 | async-start | bytes 131072 | tf_op jit(solution)/shard_map/all_to_all | solution.py:453
  128.8 2.8 %collective-permute-start.10 = (f32[16,640]{1,0:T(8,128)S(1)}, f32[16,640]{1,0:T(8,128)S(1)}, u32[]{:S(2)}, u32[]{:S(2)}) collective-permute-start(f32[16,640]{1,0:T(8,128)S(1)} %get-tuple-element.49), channel_id=1, source_target_pairs={{0,4},{4,0},{8,12},{12,8},{16,20},{20,16},{24,28},{28,24},{32,36},... | collective-permute-start | bytes 122888 | tf_op jit(solution)/shard_map/ppermute | solution.py:435
  134.4 7.5 %collective-permute-start.9 = (f32[16,512]{1,0:T(8,128)S(1)}, f32[16,512]{1,0:T(8,128)S(1)}, u32[]{:S(2)}, u32[]{:S(2)}) collective-permute-start(f32[16,512]{1,0:T(8,128)S(1)} %get-tuple-element.48), channel_id=1, source_target_pairs={{0,256},{4,260},{8,264},{12,268},{16,272},{20,276},{24,280},{28,28... | collective-permute-start | bytes 98312 | tf_op jit(solution)/shard_map/ppermute | solution.py:435
  143.1 3.6 %shard_map.90 = (f32[16,3072]{1,0:T(8,128)S(1)}, f32[16,768]{1,0:T(8,128)S(1)}, f32[4,128]{1,0:T(4,128)}) custom-call(s32[1,4]{1,0:T(1,128)S(1)} %copy-done.6, s32[1]{0:T(128)S(6)} %copy.14.refs_1_, f32[128,128]{1,0:T(8,128)S(1)} %bitcast.31, f32[16,4608]{1,0:T(8,128)S(1)} %get-tuple-element.46.refs_3_, f32[16,2304]{1,0:T(8,128)S(1)} %get-tuple-element.47.refs_4_, ...), custom_call_target="tpu_custom_call" | custom-call | tf_op jit(solution)/shard_map/pallas_call | solution.py:423
  146.7 4.0 %all-to-all-start.3 = ((f32[4,1,128]{2,1,0:T(1,128)}), f32[4,1,128]{2,1,0:T(1,128)S(1)}, u32[]{:S(2)}, u32[]{:S(2)}) async-start(f32[4,1,128]{2,1,0:T(1,128)} %bitcast.12), calls=%async_computation.3 | async-start | bytes 4096 | tf_op jit(solution)/shard_map/all_to_all | solution.py:453
  150.7 3.4 %shard_map.91 = f32[128,128]{1,0:T(8,128)S(1)} custom-call(s32[1,4]{1,0:T(1,128)S(1)} %copy-done.6, s32[1]{0:T(128)S(6)} %copy.14.refs_1_, f32[16,3072]{1,0:T(8,128)S(1)} %get-tuple-element.51.refs_2_.own, f32[16,768]{1,0:T(8,128)S(1)} %get-tuple-element.52.refs_3_, bf16[512,128]{1,0:T(8,128)(2,1)S(1)} %bitcast.28, bf16[528,512]{1,0:T(8,128)(2,1)S(1)} %copy-done.1, ...), custom_call_target="tpu_custom_call" | custom-call | tf_op jit(solution)/shard_map/pallas_call | solution.py:423
  154.8 26.9 %all_to_all.25 = f32[128,1,128]{2,1,0:T(1,128)S(1)} all-to-all(f32[128,1,128]{2,1,0:T(1,128)S(1)} %bitcast.38), channel_id=1, replica_groups=mesh['sub'=128,'case'=4] {'sub'}, dimensions={0} | all-to-all | bytes 131072 | tf_op jit(solution)/shard_map/all_to_all | solution.py:453
  (33 shorter events, 9.0 us)
Async XLA Ops:
  0.6 28.4 %copy-start.6 = (s32[1,4]{1,0:T(1,128)S(1)}, s32[1,4]{1,0:T(1,128)}, u32[]{:S(2)}) copy-start(s32[1,4]{1,0:T(1,128)} %refs_0_.11) | copy-start | bytes 52
  0.6 28.4 %copy-start.3 = (f32[16,1536]{1,0:T(8,128)S(1)}, f32[16,1536]{1,0:T(8,128)}, u32[]{:S(2)}) copy-start(f32[16,1536]{1,0:T(8,128)} %refs_2_.3) | copy-start | bytes 294916
  0.7 28.4 %copy-start.2 = (bf16[1,4,128,128]{3,2,1,0:T(8,128)(2,1)S(1)}, bf16[1,4,128,128]{3,2,1,0:T(8,128)(2,1)}, u32[]{:S(2)}) copy-start(bf16[1,4,128,128]{3,2,1,0:T(8,128)(2,1)} %param.11) | copy-start | bytes 393220
  0.7 28.4 %copy-start.5 = (s32[1,2,128]{2,1,0:T(2,128)S(1)}, s32[1,2,128]{2,1,0:T(2,128)}, u32[]{:S(2)}) copy-start(s32[1,2,128]{2,1,0:T(2,128)} %param.10) | copy-start | bytes 3076
  5.9 23.1 %collective-permute-start.2 = (bf16[528,512]{1,0:T(8,128)(2,1)}, bf16[528,512]{1,0:T(8,128)(2,1)S(1)}, u32[]{:S(2)}, u32[]{:S(2)}) collective-permute-start(bf16[528,512]{1,0:T(8,128)(2,1)} %get-tuple-element.32), channel_id=1, source_target_pairs={{0,256},{4,260},{8,264},{12,268},{16,272},{20,276},{24,280},{28,28... | collective-permute-start | bytes 1622024 | tf_op jit(solution)/shard_map/ppermute | solution.py:435
  14.2 6.8 %collective-permute-start = (bf16[704,128]{1,0:T(8,128)(2,1)}, bf16[704,128]{1,0:T(8,128)(2,1)S(1)}, u32[]{:S(2)}, u32[]{:S(2)}) collective-permute-start(bf16[704,128]{1,0:T(8,128)(2,1)} %get-tuple-element.30), channel_id=1, source_target_pairs={{0,4},{4,0},{8,12},{12,8},{16,20},{20,16},{24,28},{28,24},{32,36},... | collective-permute-start | bytes 540680 | tf_op jit(solution)/shard_map/ppermute | solution.py:435
  17.1 7.6 %collective-permute-start.1 = (bf16[704,128]{1,0:T(8,128)(2,1)}, bf16[704,128]{1,0:T(8,128)(2,1)S(1)}, u32[]{:S(2)}, u32[]{:S(2)}) collective-permute-start(bf16[704,128]{1,0:T(8,128)(2,1)} %get-tuple-element.31), channel_id=1, source_target_pairs={{0,508},{4,8},{8,4},{12,16},{16,12},{20,24},{24,20},{28,32},{32,28... | collective-permute-start | bytes 540680 | tf_op jit(solution)/shard_map/ppermute | solution.py:435
  29.1 47.8 %copy-start = (bf16[528,512]{1,0:T(8,128)(2,1)}, bf16[528,512]{1,0:T(8,128)(2,1)S(1)}, u32[]{:S(2)}) copy-start(bf16[528,512]{1,0:T(8,128)(2,1)S(1)} %collective-permute-done.2.refs_7_.refs_9_.refs_5_) | copy-start | bytes 1622020
  29.1 1.0 copy-start.4
  34.5 42.3 %all-to-all-start = ((f32[128,1,128]{2,1,0:T(1,128)}), f32[128,1,128]{2,1,0:T(1,128)S(1)}, u32[]{:S(2)}, u32[]{:S(2)}) async-start(f32[128,1,128]{2,1,0:T(1,128)} %bitcast.3), calls=%async_computation | async-start | bytes 131072 | tf_op jit(solution)/shard_map/all_to_all | solution.py:453
  62.6 14.2 %collective-permute-start.4 = (f32[16,640]{1,0:T(8,128)S(1)}, f32[16,640]{1,0:T(8,128)S(1)}, u32[]{:S(2)}, u32[]{:S(2)}) collective-permute-start(f32[16,640]{1,0:T(8,128)S(1)} %get-tuple-element.37), channel_id=1, source_target_pairs={{0,4},{4,0},{8,12},{12,8},{16,20},{20,16},{24,28},{28,24},{32,36},... | collective-permute-start | bytes 122888 | tf_op jit(solution)/shard_map/ppermute | solution.py:435
  65.4 11.4 %collective-permute-start.5 = (f32[16,640]{1,0:T(8,128)S(1)}, f32[16,640]{1,0:T(8,128)S(1)}, u32[]{:S(2)}, u32[]{:S(2)}) collective-permute-start(f32[16,640]{1,0:T(8,128)S(1)} %get-tuple-element.38), channel_id=1, source_target_pairs={{0,508},{4,8},{8,4},{12,16},{16,12},{20,24},{24,20},{28,32},{32,28... | collective-permute-start | bytes 122888 | tf_op jit(solution)/shard_map/ppermute | solution.py:435
  68.2 8.7 %collective-permute-start.3 = (f32[16,512]{1,0:T(8,128)S(1)}, f32[16,512]{1,0:T(8,128)S(1)}, u32[]{:S(2)}, u32[]{:S(2)}) collective-permute-start(f32[16,512]{1,0:T(8,128)S(1)} %get-tuple-element.36), channel_id=1, source_target_pairs={{0,256},{4,260},{8,264},{12,268},{16,272},{20,276},{24,280},{28,28... | collective-permute-start | bytes 98312 | tf_op jit(solution)/shard_map/ppermute | solution.py:435
  81.6 61.5 %copy-start.1 = (bf16[528,512]{1,0:T(8,128)(2,1)S(1)}, bf16[528,512]{1,0:T(8,128)(2,1)}, u32[]{:S(2)}) copy-start(bf16[528,512]{1,0:T(8,128)(2,1)} %copy-done) | copy-start | bytes 1622020
  81.6 28.4 %all-to-all-start.1 = ((f32[128,1,128]{2,1,0:T(1,128)}), f32[128,1,128]{2,1,0:T(1,128)S(1)}, u32[]{:S(2)}, u32[]{:S(2)}) async-start(f32[128,1,128]{2,1,0:T(1,128)} %bitcast.6), calls=%async_computation.1 | async-start | bytes 131072 | tf_op jit(solution)/shard_map/all_to_all | solution.py:453
  95.8 14.2 %collective-permute-start.7 = (f32[16,640]{1,0:T(8,128)S(1)}, f32[16,640]{1,0:T(8,128)S(1)}, u32[]{:S(2)}, u32[]{:S(2)}) collective-permute-start(f32[16,640]{1,0:T(8,128)S(1)} %get-tuple-element.43), channel_id=1, source_target_pairs={{0,4},{4,0},{8,12},{12,8},{16,20},{20,16},{24,28},{28,24},{32,36},... | collective-permute-start | bytes 122888 | tf_op jit(solution)/shard_map/ppermute | solution.py:435
  98.6 11.4 %collective-permute-start.8 = (f32[16,640]{1,0:T(8,128)S(1)}, f32[16,640]{1,0:T(8,128)S(1)}, u32[]{:S(2)}, u32[]{:S(2)}) collective-permute-start(f32[16,640]{1,0:T(8,128)S(1)} %get-tuple-element.44), channel_id=1, source_target_pairs={{0,508},{4,8},{8,4},{12,16},{16,12},{20,24},{24,20},{28,32},{32,28... | collective-permute-start | bytes 122888 | tf_op jit(solution)/shard_map/ppermute | solution.py:435
  101.4 8.7 %collective-permute-start.6 = (f32[16,512]{1,0:T(8,128)S(1)}, f32[16,512]{1,0:T(8,128)S(1)}, u32[]{:S(2)}, u32[]{:S(2)}) collective-permute-start(f32[16,512]{1,0:T(8,128)S(1)} %get-tuple-element.42), channel_id=1, source_target_pairs={{0,256},{4,260},{8,264},{12,268},{16,272},{20,276},{24,280},{28,28... | collective-permute-start | bytes 98312 | tf_op jit(solution)/shard_map/ppermute | solution.py:435
  114.8 28.3 %all-to-all-start.2 = ((f32[128,1,128]{2,1,0:T(1,128)}), f32[128,1,128]{2,1,0:T(1,128)S(1)}, u32[]{:S(2)}, u32[]{:S(2)}) async-start(f32[128,1,128]{2,1,0:T(1,128)} %bitcast.9), calls=%async_computation.2 | async-start | bytes 131072 | tf_op jit(solution)/shard_map/all_to_all | solution.py:453
  128.8 14.2 %collective-permute-start.10 = (f32[16,640]{1,0:T(8,128)S(1)}, f32[16,640]{1,0:T(8,128)S(1)}, u32[]{:S(2)}, u32[]{:S(2)}) collective-permute-start(f32[16,640]{1,0:T(8,128)S(1)} %get-tuple-element.49), channel_id=1, source_target_pairs={{0,4},{4,0},{8,12},{12,8},{16,20},{20,16},{24,28},{28,24},{32,36},... | collective-permute-start | bytes 122888 | tf_op jit(solution)/shard_map/ppermute | solution.py:435
  131.6 11.4 %collective-permute-start.11 = (f32[16,640]{1,0:T(8,128)S(1)}, f32[16,640]{1,0:T(8,128)S(1)}, u32[]{:S(2)}, u32[]{:S(2)}) collective-permute-start(f32[16,640]{1,0:T(8,128)S(1)} %get-tuple-element.50), channel_id=1, source_target_pairs={{0,508},{4,8},{8,4},{12,16},{16,12},{20,24},{24,20},{28,32},{32,28... | collective-permute-start | bytes 122888 | tf_op jit(solution)/shard_map/ppermute | solution.py:435
  134.4 8.7 %collective-permute-start.9 = (f32[16,512]{1,0:T(8,128)S(1)}, f32[16,512]{1,0:T(8,128)S(1)}, u32[]{:S(2)}, u32[]{:S(2)}) collective-permute-start(f32[16,512]{1,0:T(8,128)S(1)} %get-tuple-element.48), channel_id=1, source_target_pairs={{0,256},{4,260},{8,264},{12,268},{16,272},{20,276},{24,280},{28,28... | collective-permute-start | bytes 98312 | tf_op jit(solution)/shard_map/ppermute | solution.py:435
  146.7 8.1 %all-to-all-start.3 = ((f32[4,1,128]{2,1,0:T(1,128)}), f32[4,1,128]{2,1,0:T(1,128)S(1)}, u32[]{:S(2)}, u32[]{:S(2)}) async-start(f32[4,1,128]{2,1,0:T(1,128)} %bitcast.12), calls=%async_computation.3 | async-start | bytes 4096 | tf_op jit(solution)/shard_map/all_to_all | solution.py:453

commit v5 on v4

--- a/solution.py
+++ b/solution.py
@@ -178,7 +178,7 @@
     near_x, near_lift = moved_by(near_x, step, near[:, BLK:])
     far_x, far_lift = moved_by(far_x, step, far[:, BLK:])
     part, mate_part = contact_terms(lift, mate_lift, statics, True)
-    mate_g = mate_g - step * mate + symmetric_dot(mate_lift, mate_kernel) + mate_part
+    mate_g = mate_g - step * mate + quarters_dot(mate_lift, *mate_kernel) + mate_part
     near_face = near_face - step * near[:, :BLK] + fine_dot(near_lift, near_kernel[...])
     far_face = far_face - step * far[:, :BLK] + fine_dot(far_lift, far_kernel[...])
     lifted = whole_dot(lift, rows)
@@ -212,11 +212,10 @@
     return piece
 
 
-TABLE = 4 * CASES
+TABLE = 2 * CASES
 SLOTS = TABLE + CASES
-UPPER = SLOTS + BLK
-PACKED = UPPER + 2 * BLK + BLK // 2
-SIDE = 12 * CASES
+PACKED = SLOTS + BLK
+SIDE = 6 * CASES
 
 
 def is_even():
@@ -228,44 +227,16 @@
     return high, (block - high.astype(f32)).astype(bf16)
 
 
-def upper_places():
-    half = BLK // 2
-    places = {}
+def quarters_dot(value, case, quarters):
+    blocks, total = split(value), None
     for k in range(4):
-        places[0, k] = [(UPPER, BLK, k)]
-    for k in range(1, 4):
-        places[1, k] = [(UPPER + BLK, BLK, k)]
-    places[3, 3] = [(UPPER + BLK, BLK, 0)]
-    for k in (2, 3):
-        lane = 2 * (k - 2)
-        places[2, k] = [(UPPER + 2 * BLK, half, lane), (UPPER + 2 * BLK, half, lane + 1)]
-    return places
-
-
-def store_upper(packed, dual_ref):
-    for (i, j), places in upper_places().items():
-        start = LOW + i * BLK
-        for row, size, lane in places:
-            block = dual_ref[start : start + size, LOW + j * BLK : LOW + (j + 1) * BLK]
-            packed[row : row + size, lane * BLK : (lane + 1) * BLK] = block
-            start = start + size
-
-
-def symmetric_dot(value, packed):
-    high, low = halves(value)
-    both = split(jnp.concatenate([high, low], axis=0))
-    blocks = {}
-    for key, places in upper_places().items():
-        parts = [packed[row : row + n, lane * BLK : (lane + 1) * BLK] for row, n, lane in places]
-        blocks[key] = parts[0] if len(parts) == 1 else jnp.concatenate(parts, axis=0)
-    outs = []
-    for j in range(4):
-        total = None
-        for i in range(4):
-            part = dot(both[i], blocks[min(i, j), max(i, j)], i > j)
-            total = part if total is None else total + part
-        outs.append(total[:CASES] + total[CASES:])
-    return jnp.concatenate(outs, axis=1)
+        index = lax.bitwise_xor(case, k)
+        block = blocks[0]
+        for i in range(1, 4):
+            block = jnp.where(index == i, blocks[i], block)
+        part = dot(jnp.concatenate(halves(block), axis=0), quarters[k])
+        total = part if total is None else total + part
+    return total[:CASES] + total[CASES:]
 
 
 def prepare_kernel(*refs):
@@ -274,23 +245,19 @@
     piece = whole_copy(dual_hbm, dual_ref, sems)
     even = is_even()
     for k in range(4):
-        packed[SLOTS:UPPER, k * BLK : (k + 1) * BLK] = mortar[k * BLK : (k + 1) * BLK, :]
+        packed[SLOTS:, k * BLK : (k + 1) * BLK] = mortar[k * BLK : (k + 1) * BLK, :]
     table = slot_table(ids, count).astype(bf16)
     packed[TABLE:SLOTS, :] = jnp.concatenate([table] * 4, axis=1)
     x = x_ref[...]
     q = whole_dot(x, [piece(k, True) for k in range(len(STARTS))]) - right_ref[...]
     q_ref[...] = q
-    store_upper(packed, dual_ref)
-    parts = halves(x[:, LOW:HIGH]) + halves(q[:, LOW:HIGH])
-    for k, part in enumerate(parts):
-        packed[k * CASES : (k + 1) * CASES, :] = part
+    packed[:CASES, :] = x[:, LOW:HIGH].astype(bf16)
+    packed[CASES:TABLE, :] = q[:, LOW:HIGH].astype(bf16)
     contacts = split(x[:, LOW:HIGH])
     both = [(near_ref,), (far_ref,)]
     for (ref,), face, grad in zip(both, faces_of(x, even), faces_of(q, even)):
         for k, block in enumerate([face, grad] + contacts):
-            high, low = halves(block)
-            ref[2 * k * CASES : (2 * k + 1) * CASES, :] = high
-            ref[(2 * k + 1) * CASES : (2 * k + 2) * CASES, :] = low
+            ref[k * CASES : (k + 1) * CASES, :] = block.astype(bf16)
     first, second = dual_ref[LOW:HIGH, :BLK], dual_ref[LOW:HIGH, BLK:LOW]
     near_ref[SIDE:, :] = chosen(even, second, first)
     far_ref[SIDE:, :] = chosen(even, first, second)
@@ -298,14 +265,14 @@
 
 def statics_of(ids, count, mortar, packed):
     own = [mortar[k * BLK : (k + 1) * BLK, :] for k in range(4)]
-    mate = [packed[SLOTS:UPPER, k * BLK : (k + 1) * BLK] for k in range(4)]
+    mate = [packed[SLOTS:, k * BLK : (k + 1) * BLK] for k in range(4)]
     mate_table = packed[TABLE:SLOTS, :BLK].astype(f32)
     return slots(slot_table(ids, count)), own, slots(mate_table), mate
 
 
 def side_values(ref):
-    parts = [ref[k * CASES : (k + 1) * CASES, :].astype(f32) for k in range(12)]
-    return jnp.concatenate([parts[2 * k] + parts[2 * k + 1] for k in range(6)], axis=1)
+    parts = [ref[k * CASES : (k + 1) * CASES, :].astype(f32) for k in range(6)]
+    return jnp.concatenate(parts, axis=1)
 
 
 def emit(outs, x, g, image, row, others):
@@ -330,8 +297,7 @@
     statics = statics_of(ids, count, mortar, packed)
     pick = picks(match[...], even)
     x = x_ref[...]
-    parts = [packed[k * CASES : (k + 1) * CASES, :].astype(f32) for k in range(4)]
-    mate = parts[0] + parts[1], parts[2] + parts[3]
+    mate = packed[:CASES, :].astype(f32), packed[CASES:TABLE, :].astype(f32)
     sides = side_values(near), side_values(far)
     g, others = begin(x, q_ref[...], mate, *sides, statics, pick, even)
     pieces = [piece(k, True) for k in range(len(STARTS))]
@@ -344,7 +310,8 @@
 
 def advanced(refs, piece):
     ids, count, sums, own, others, mate, near, far, mortar, packed, _ = refs[:11]
-    near_kernel, far_kernel = refs[11:13]
+    near_kernel, far_kernel, quarter, second, pair = refs[11:16]
+    quarters = (quarter[...], second[...], pair[:BLK, :], pair[BLK:, :])
     statics = statics_of(ids, count, mortar, packed)
     offsets = [sum(WIDTHS[:k]) for k in range(len(WIDTHS))]
     lift_rows = [(k * CHUNK, CHUNK, piece(k, True)[2]) for k in range(2)]
@@ -357,16 +324,16 @@
         far[...],
         statics,
         lift_rows,
-        (packed, near_kernel.at[SIDE:], far_kernel.at[SIDE:]),
+        ((lax.axis_index("case"), quarters), near_kernel.at[SIDE:], far_kernel.at[SIDE:]),
     )
     return x, g, others, statics
 
 
 def advance_kernel(*refs):
-    dual_hbm, outs, (dual_ref, sems) = refs[13], refs[14:20], refs[20:]
+    dual_hbm, outs, (dual_ref, sems) = refs[16], refs[17:23], refs[23:]
     piece = whole_copy(dual_hbm, dual_ref, sems)
     even = is_even()
-    x, g, others, statics = advanced(refs[:13], piece)
+    x, g, others, statics = advanced(refs[:16], piece)
     pick = picks(refs[10][...], even)
     pieces = [piece(k, k >= 2) for k in range(len(STARTS))]
     image, row = tail(g, others, statics, pick, even, pieces)
@@ -374,9 +341,9 @@
 
 
 def last_advance_kernel(*refs):
-    dual_hbm, (own_out, others_out, row_out), (dual_ref, sems) = refs[13], refs[14:17], refs[17:]
+    dual_hbm, (own_out, others_out, row_out), (dual_ref, sems) = refs[16], refs[17:20], refs[20:]
     piece = whole_copy(dual_hbm, dual_ref, sems, STARTS[:2])
-    x, g, others, _ = advanced(refs[:13], piece)
+    x, g, others, _ = advanced(refs[:16], piece)
     own_out[:, :M] = x
     own_out[:, M:] = g
     others_out[...] = jnp.concatenate([others[1], others[4], others[5]], axis=1)
@@ -448,6 +415,11 @@
     return swapped(value, lambda i: i + 1 if i % 2 else i - 1)
 
 
+def with_case(value, bit):
+    cases = lax.axis_size("case")
+    return lax.ppermute(value, "case", [(i, i ^ bit) for i in range(cases)])
+
+
 def spread_sums(copies, axis):
     devices = lax.axis_size(axis)
     rows = lax.all_to_all(copies.reshape(devices, 1, BLK), axis, 0, 0)
@@ -472,10 +444,13 @@
         (contact_ids, contact_count, multipliers, right_side, mortar, dual_ops),
         grant=PREPARE_GRANT,
     )
+    packed, dual_later = lax.optimization_barrier((packed, dual_ops))
     packed = with_mate(packed)
     near = near_kernel = with_near(to_near)
     far = far_kernel = with_far(to_far)
-
+    start = LOW + lax.rem(lax.axis_index("case"), 4) * BLK
+    quarter = lax.dynamic_slice(dual_later, (start, LOW), (BLK, CONTACT))
+    quarter = with_mate(quarter)
     shapes = [
         ((CASES, 3 * M), f32),
         ((CASES, sum(WIDTHS)), f32),
@@ -498,21 +473,24 @@
         mate = with_mate(to_mate)
         far = with_far(to_far)
         near = with_near(to_near)
+        if iteration == 1:
+            second = with_case(quarter, 1)
+            pair = with_case(jnp.concatenate([quarter, second]), 2)
         operands = (
             contact_ids, contact_count, sums, own, others, mate, near, far, mortar, packed,
-            match, near_kernel, far_kernel, dual_ops,
+            match, near_kernel, far_kernel, quarter, second, pair, dual_ops,
         )
         if iteration < ITERS - 1:
             own, others, copies, to_mate, to_near, to_far = call(
                 advance_kernel,
-                scalars + [VMEM_SPEC] * 11 + [HBM_SPEC],
+                scalars + [VMEM_SPEC] * 14 + [HBM_SPEC],
                 shapes,
                 operands,
             )
     cases = lax.axis_size("case")
     own, others, norms = call(
         last_advance_kernel,
-        scalars + [VMEM_SPEC] * 11 + [HBM_SPEC],
+        scalars + [VMEM_SPEC] * 14 + [HBM_SPEC],
         [
             ((CASES, 2 * M), f32),
             ((CASES, CONTACT + 2 * BLK), f32),

time: 183 us -> 192 us (1.049)
  starting transfers between devices: 114 us -> 123 us
  waiting for transfers between devices: 12.5 us -> 9.35 us
  local copies, waits for them, and re-layouts: 1.03 us -> 3.48 us
    ppermute x12 -> x13, starting transfers between devices: 53.9 us -> 64.1 us  [swapped(): lax.ppermute(value, 'sub', [(i, other(i) % devices) for i in range(device...]
    all_to_all x4, starting transfers between devices: 60.3 us -> 52.8 us  [spread_sums(): rows = lax.all_to_all(copies.reshape(devices, 1, BLK), axis, 0, 0)]
    ppermute x0 -> x2, starting transfers between devices: none -> 6.27 us  [with_case(): return lax.ppermute(value, 'case', [(i, i ^ bit) for i in range(cases)])]
    ppermute x12 -> x13, waiting for transfers between devices: 11.9 us -> 8.67 us  [swapped(): lax.ppermute(value, 'sub', [(i, other(i) % devices) for i in range(device...]
  transfers between devices with their start and end apart: 16 -> 19, of which waited for: 6 -> 5; matrix products, arithmetic and copies ran while one was open for 0% -> 0% of each run, Pallas kernels for 2% -> 4%
where the time goes in v5:
time: 192 us; the launch traced here: 191 us
  starting transfers between devices  123 us (64%)
  blocking collectives  26.9 us (14%)
  Pallas kernels  26.5 us (14%)
  waiting for transfers between devices  9.35 us (5%)
  local copies, waits for them, and re-layouts  3.48 us (2%)
    ppermute x13, starting transfers between devices, swapped(): lax.ppermute(value, 'sub', [(i, other(i) % devices) for i in range(device...  64.1 us
    all_to_all x4, starting transfers between devices, spread_sums(): rows = lax.all_to_all(copies.reshape(devices, 1, BLK), axis, 0, 0)  52.8 us
    all_to_all x1, blocking collectives, spread_sums(): rows = lax.all_to_all(copies.reshape(devices, 1, BLK), axis, 0, 0)  26.9 us
    pallas_call x7, Pallas kernels, call(): pl.pallas_call(kernel, in_specs=specs, out_specs=[VMEM_SPEC] * len(shapes...  26.5 us
    ppermute x13, waiting for transfers between devices, swapped(): lax.ppermute(value, 'sub', [(i, other(i) % devices) for i in range(device...  8.67 us
    ppermute x2, starting transfers between devices, with_case(): return lax.ppermute(value, 'case', [(i, i ^ bit) for i in range(cases)])  6.27 us
  transfers between devices with their start and end apart: 19, of which 5 were waited for; matrix products, arithmetic and copies ran while one was open for 0% of the time, Pallas kernels for 4%

profile of v5, /device:TPU:1, one launch (start us, length us, event | category | flops | bytes accessed | tf_op | source)
XLA Modules:
  0.0 191.0 jit_solution(1555792574681292028)
XLA Ops:
  1.4 4.4 %shard_map.86 = (f32[16,1536]{1,0:T(8,128)}, bf16[176,512]{1,0:T(8,128)(2,1)}, bf16[608,128]{1,0:T(8,128)(2,1)}, bf16[608,128]{1,0:T(8,128)(2,1)}) custom-call(s32[1,4]{1,0:T(1,128)} %refs_0_.11, s32[1]{0:T(128)S(6)} %copy.14.refs_1_, f32[16,1536]{1,0:T(8,128)} %refs_2_.3, f32[16,1536]{1,0:T(8,128)} %refs_3_.1, bf16[512,128]{1,0:T(8,128)(2,1)} %bitcast.23, ...), custom_call_target="tpu_custom_call" | custom-call | tf_op jit(solution)/shard_map/pallas_call | solution.py:390
  6.7 8.3 %collective-permute-start.6 = (bf16[128,512]{1,0:T(8,128)(2,1)S(1)}, bf16[128,512]{1,0:T(8,128)(2,1)S(1)}, u32[]{:S(2)}, u32[]{:S(2)}) collective-permute-start(bf16[128,512]{1,0:T(8,128)(2,1)S(1)} %constant_dynamic-slice_fusion), channel_id=1, source_target_pairs={{0,256},{4,260},{8,264},{12,268},{16,272},{20,276},{24,280},{28,28... | collective-permute-start | bytes 393224 | tf_op jit(solution)/shard_map/ppermute | solution.py:402
  15.0 4.9 %collective-permute-done.6.refs_13_ = bf16[128,512]{1,0:T(8,128)(2,1)S(1)} collective-permute-done((bf16[128,512]{1,0:T(8,128)(2,1)S(1)}, bf16[128,512]{1,0:T(8,128)(2,1)S(1)}, u32[]{:S(2)}, u32[]{:S(2)}) %collective-permute-start.6) | collective-permute-done | bytes 131104 | tf_op jit(solution)/shard_map/ppermute | solution.py:402
  21.8 7.5 %collective-permute-start = (bf16[608,128]{1,0:T(8,128)(2,1)}, bf16[608,128]{1,0:T(8,128)(2,1)S(1)}, u32[]{:S(2)}, u32[]{:S(2)}) collective-permute-start(bf16[608,128]{1,0:T(8,128)(2,1)} %get-tuple-element.32), channel_id=1, source_target_pairs={{0,4},{4,0},{8,12},{12,8},{16,20},{20,16},{24,28},{28,24},{32,36},... | collective-permute-start | bytes 466952 | tf_op jit(solution)/shard_map/ppermute | solution.py:402
  31.2 7.5 %collective-permute-start.2 = (bf16[176,512]{1,0:T(8,128)(2,1)}, bf16[176,512]{1,0:T(8,128)(2,1)S(1)}, u32[]{:S(2)}, u32[]{:S(2)}) collective-permute-start(bf16[176,512]{1,0:T(8,128)(2,1)} %get-tuple-element.35), channel_id=1, source_target_pairs={{0,256},{4,260},{8,264},{12,268},{16,272},{20,276},{24,280},{28,28... | collective-permute-start | bytes 540680 | tf_op jit(solution)/shard_map/ppermute | solution.py:402
  38.7 4.4 %collective-permute-start.8 = (bf16[256,512]{1,0:T(8,128)(2,1)S(1)}, bf16[256,512]{1,0:T(8,128)(2,1)S(1)}, u32[]{:S(2)}, u32[]{:S(2)}) collective-permute-start(bf16[256,512]{1,0:T(8,128)(2,1)S(1)} %pad_maximum_fusion), channel_id=1, source_target_pairs={{0,2},{1,3},{2,0},{3,1},{4,6},{5,7},{6,4},{7,5},{8,10},{9,11},{10,... | collective-permute-start | bytes 786440 | tf_op jit(solution)/shard_map/ppermute | solution.py:420
  44.1 4.4 %shard_map.87 = (f32[16,4608]{1,0:T(8,128)S(1)}, f32[16,2304]{1,0:T(8,128)S(1)}, f32[128,128]{1,0:T(8,128)}, f32[16,512]{1,0:T(8,128)S(1)}, f32[16,640]{1,0:T(8,128)S(1)}, /*index=5*/f32[16,640]{1,0:T(8,128)S(1)}) custom-call(s32[1,4]{1,0:T(1,128)S(1)} %copy-done.6, s32[1]{0:T(128)S(6)} %copy.14.refs_1_, f32[16,1536]{1,0:T(8,128)S(1)} %copy-done.1, ...), custom_call_target="tpu_custom_call" | custom-call | tf_op jit(solution)/shard_map/pallas_call | solution.py:390
  49.2 20.9 %all-to-all-start = ((f32[128,1,128]{2,1,0:T(1,128)}), f32[128,1,128]{2,1,0:T(1,128)S(1)}, u32[]{:S(2)}, u32[]{:S(2)}) async-start(f32[128,1,128]{2,1,0:T(1,128)} %bitcast.3), calls=%async_computation | async-start | bytes 131072 | tf_op jit(solution)/shard_map/all_to_all | solution.py:425
  70.1 2.8 %collective-permute-start.4 = (f32[16,640]{1,0:T(8,128)S(1)}, f32[16,640]{1,0:T(8,128)S(1)}, u32[]{:S(2)}, u32[]{:S(2)}) collective-permute-start(f32[16,640]{1,0:T(8,128)S(1)} %get-tuple-element.40), channel_id=1, source_target_pairs={{0,4},{4,0},{8,12},{12,8},{16,20},{20,16},{24,28},{28,24},{32,36},... | collective-permute-start | bytes 122888 | tf_op jit(solution)/shard_map/ppermute | solution.py:402
  73.0 2.8 %collective-permute-start.5 = (f32[16,640]{1,0:T(8,128)S(1)}, f32[16,640]{1,0:T(8,128)S(1)}, u32[]{:S(2)}, u32[]{:S(2)}) collective-permute-start(f32[16,640]{1,0:T(8,128)S(1)} %get-tuple-element.41), channel_id=1, source_target_pairs={{0,508},{4,8},{8,4},{12,16},{16,12},{20,24},{24,20},{28,32},{32,28... | collective-permute-start | bytes 122888 | tf_op jit(solution)/shard_map/ppermute | solution.py:402
  75.7 7.3 %collective-permute-start.3 = (f32[16,512]{1,0:T(8,128)S(1)}, f32[16,512]{1,0:T(8,128)S(1)}, u32[]{:S(2)}, u32[]{:S(2)}) collective-permute-start(f32[16,512]{1,0:T(8,128)S(1)} %get-tuple-element.39), channel_id=1, source_target_pairs={{0,256},{4,260},{8,264},{12,268},{16,272},{20,276},{24,280},{28,28... | collective-permute-start | bytes 98312 | tf_op jit(solution)/shard_map/ppermute | solution.py:402
  84.4 5.0 %shard_map.88 = (f32[16,4608]{1,0:T(8,128)}, f32[16,2304]{1,0:T(8,128)S(1)}, f32[128,128]{1,0:T(8,128)}, f32[16,512]{1,0:T(8,128)S(1)}, f32[16,640]{1,0:T(8,128)S(1)}, /*index=5*/f32[16,640]{1,0:T(8,128)S(1)}) custom-call(s32[1,4]{1,0:T(1,128)S(1)} %copy-done.6, s32[1]{0:T(128)S(6)} %copy.14.refs_1_, f32[128,128]{1,0:T(8,128)S(1)} %bitcast.29, ...), custom_call_target="tpu_custom_call" | custom-call | tf_op jit(solution)/shard_map/pallas_call | solution.py:390
  89.5 14.1 %all-to-all-start.1 = ((f32[128,1,128]{2,1,0:T(1,128)}), f32[128,1,128]{2,1,0:T(1,128)S(1)}, u32[]{:S(2)}, u32[]{:S(2)}) async-start(f32[128,1,128]{2,1,0:T(1,128)} %bitcast.6), calls=%async_computation.1 | async-start | bytes 131072 | tf_op jit(solution)/shard_map/all_to_all | solution.py:425
  103.5 2.8 %collective-permute-start.10 = (f32[16,640]{1,0:T(8,128)S(1)}, f32[16,640]{1,0:T(8,128)S(1)}, u32[]{:S(2)}, u32[]{:S(2)}) collective-permute-start(f32[16,640]{1,0:T(8,128)S(1)} %get-tuple-element.47), channel_id=1, source_target_pairs={{0,4},{4,0},{8,12},{12,8},{16,20},{20,16},{24,28},{28,24},{32,36},... | collective-permute-start | bytes 122888 | tf_op jit(solution)/shard_map/ppermute | solution.py:402
  106.3 2.8 %collective-permute-start.11 = (f32[16,640]{1,0:T(8,128)S(1)}, f32[16,640]{1,0:T(8,128)S(1)}, u32[]{:S(2)}, u32[]{:S(2)}) collective-permute-start(f32[16,640]{1,0:T(8,128)S(1)} %get-tuple-element.48), channel_id=1, source_target_pairs={{0,508},{4,8},{8,4},{12,16},{16,12},{20,24},{24,20},{28,32},{32,28... | collective-permute-start | bytes 122888 | tf_op jit(solution)/shard_map/ppermute | solution.py:402
  109.1 7.3 %collective-permute-start.9 = (f32[16,512]{1,0:T(8,128)S(1)}, f32[16,512]{1,0:T(8,128)S(1)}, u32[]{:S(2)}, u32[]{:S(2)}) collective-permute-start(f32[16,512]{1,0:T(8,128)S(1)} %get-tuple-element.46), channel_id=1, source_target_pairs={{0,256},{4,260},{8,264},{12,268},{16,272},{20,276},{24,280},{28,28... | collective-permute-start | bytes 98312 | tf_op jit(solution)/shard_map/ppermute | solution.py:402
  117.8 5.0 %shard_map.89 = (f32[16,4608]{1,0:T(8,128)}, f32[16,2304]{1,0:T(8,128)S(1)}, f32[128,128]{1,0:T(8,128)}, f32[16,512]{1,0:T(8,128)S(1)}, f32[16,640]{1,0:T(8,128)S(1)}, /*index=5*/f32[16,640]{1,0:T(8,128)S(1)}) custom-call(s32[1,4]{1,0:T(1,128)S(1)} %copy-done.6, s32[1]{0:T(128)S(6)} %copy.14.refs_1_, f32[128,128]{1,0:T(8,128)S(1)} %bitcast.31, ...), custom_call_target="tpu_custom_call" | custom-call | tf_op jit(solution)/shard_map/pallas_call | solution.py:390
  122.8 14.1 %all-to-all-start.2 = ((f32[128,1,128]{2,1,0:T(1,128)}), f32[128,1,128]{2,1,0:T(1,128)S(1)}, u32[]{:S(2)}, u32[]{:S(2)}) async-start(f32[128,1,128]{2,1,0:T(1,128)} %bitcast.9), calls=%async_computation.2 | async-start | bytes 131072 | tf_op jit(solution)/shard_map/all_to_all | solution.py:425
  136.9 2.8 %collective-permute-start.13 = (f32[16,640]{1,0:T(8,128)S(1)}, f32[16,640]{1,0:T(8,128)S(1)}, u32[]{:S(2)}, u32[]{:S(2)}) collective-permute-start(f32[16,640]{1,0:T(8,128)S(1)} %get-tuple-element.53), channel_id=1, source_target_pairs={{0,4},{4,0},{8,12},{12,8},{16,20},{20,16},{24,28},{28,24},{32,36},... | collective-permute-start | bytes 122888 | tf_op jit(solution)/shard_map/ppermute | solution.py:402
  142.5 7.5 %collective-permute-start.12 = (f32[16,512]{1,0:T(8,128)S(1)}, f32[16,512]{1,0:T(8,128)S(1)}, u32[]{:S(2)}, u32[]{:S(2)}) collective-permute-start(f32[16,512]{1,0:T(8,128)S(1)} %get-tuple-element.52), channel_id=1, source_target_pairs={{0,256},{4,260},{8,264},{12,268},{16,272},{20,276},{24,280},{28,28... | collective-permute-start | bytes 98312 | tf_op jit(solution)/shard_map/ppermute | solution.py:402
  152.1 3.4 %shard_map.90 = (f32[16,3072]{1,0:T(8,128)S(1)}, f32[16,768]{1,0:T(8,128)S(1)}, f32[4,128]{1,0:T(4,128)}) custom-call(s32[1,4]{1,0:T(1,128)S(1)} %copy-done.6, s32[1]{0:T(128)S(6)} %copy.14.refs_1_, f32[128,128]{1,0:T(8,128)S(1)} %bitcast.30, f32[16,4608]{1,0:T(8,128)S(1)} %copy-done.2, f32[16,2304]{1,0:T(8,128)S(1)} %get-tuple-element.51.refs_4_, ...), custom_call_target="tpu_custom_call" | custom-call | tf_op jit(solution)/shard_map/pallas_call | solution.py:390
  155.6 3.7 %all-to-all-start.3 = ((f32[4,1,128]{2,1,0:T(1,128)}), f32[4,1,128]{2,1,0:T(1,128)S(1)}, u32[]{:S(2)}, u32[]{:S(2)}) async-start(f32[4,1,128]{2,1,0:T(1,128)} %bitcast.12), calls=%async_computation.3 | async-start | bytes 4096 | tf_op jit(solution)/shard_map/all_to_all | solution.py:425
  159.3 3.4 %shard_map.91 = f32[128,128]{1,0:T(8,128)S(1)} custom-call(s32[1,4]{1,0:T(1,128)S(1)} %copy-done.6, s32[1]{0:T(128)S(6)} %copy.14.refs_1_, f32[16,3072]{1,0:T(8,128)S(1)} %get-tuple-element.55.refs_2_.own, f32[16,768]{1,0:T(8,128)S(1)} %get-tuple-element.56.refs_3_, bf16[512,128]{1,0:T(8,128)(2,1)S(1)} %bitcast.28, ...), custom_call_target="tpu_custom_call" | custom-call | tf_op jit(solution)/shard_map/pallas_call | solution.py:390
  163.4 26.9 %all_to_all.25 = f32[128,1,128]{2,1,0:T(1,128)S(1)} all-to-all(f32[128,1,128]{2,1,0:T(1,128)S(1)} %bitcast.38), channel_id=1, replica_groups=mesh['sub'=128,'case'=4] {'sub'}, dimensions={0} | all-to-all | bytes 131072 | tf_op jit(solution)/shard_map/all_to_all | solution.py:425
  (41 shorter events, 15.4 us)
Async XLA Ops:
  0.6 42.5 %copy-start.6 = (s32[1,4]{1,0:T(1,128)S(1)}, s32[1,4]{1,0:T(1,128)}, u32[]{:S(2)}) copy-start(s32[1,4]{1,0:T(1,128)} %refs_0_.11) | copy-start | bytes 52
  0.6 42.5 %copy-start.1 = (f32[16,1536]{1,0:T(8,128)S(1)}, f32[16,1536]{1,0:T(8,128)}, u32[]{:S(2)}) copy-start(f32[16,1536]{1,0:T(8,128)} %refs_2_.3) | copy-start | bytes 294916
  0.7 42.5 %copy-start = (bf16[1,4,128,128]{3,2,1,0:T(8,128)(2,1)S(1)}, bf16[1,4,128,128]{3,2,1,0:T(8,128)(2,1)}, u32[]{:S(2)}) copy-start(bf16[1,4,128,128]{3,2,1,0:T(8,128)(2,1)} %param.11) | copy-start | bytes 393220
  0.7 42.5 %copy-start.5 = (s32[1,2,128]{2,1,0:T(2,128)S(1)}, s32[1,2,128]{2,1,0:T(2,128)}, u32[]{:S(2)}) copy-start(s32[1,2,128]{2,1,0:T(2,128)} %param.10) | copy-start | bytes 3076
  6.7 13.2 %collective-permute-start.6 = (bf16[128,512]{1,0:T(8,128)(2,1)S(1)}, bf16[128,512]{1,0:T(8,128)(2,1)S(1)}, u32[]{:S(2)}, u32[]{:S(2)}) collective-permute-start(bf16[128,512]{1,0:T(8,128)(2,1)S(1)} %constant_dynamic-slice_fusion), channel_id=1, source_target_pairs={{0,256},{4,260},{8,264},{12,268},{16,272},{20,276},{24,280},{28,28... | collective-permute-start | bytes 393224 | tf_op jit(solution)/shard_map/ppermute | solution.py:402
  19.9 18.8 %collective-permute-start.7 = (bf16[128,512]{1,0:T(8,128)(2,1)S(1)}, bf16[128,512]{1,0:T(8,128)(2,1)S(1)}, u32[]{:S(2)}, u32[]{:S(2)}) collective-permute-start(bf16[128,512]{1,0:T(8,128)(2,1)S(1)} %collective-permute-done.6.refs_13_), channel_id=1, source_target_pairs={{0,1},{1,0},{2,3},{3,2},{4,5},{5,4},{6,7},{7,6},{8,9},{9,8},{10,11... | collective-permute-start | bytes 393224 | tf_op jit(solution)/shard_map/ppermute | solution.py:420
  21.8 21.3 %collective-permute-start = (bf16[608,128]{1,0:T(8,128)(2,1)}, bf16[608,128]{1,0:T(8,128)(2,1)S(1)}, u32[]{:S(2)}, u32[]{:S(2)}) collective-permute-start(bf16[608,128]{1,0:T(8,128)(2,1)} %get-tuple-element.32), channel_id=1, source_target_pairs={{0,4},{4,0},{8,12},{12,8},{16,20},{20,16},{24,28},{28,24},{32,36},... | collective-permute-start | bytes 466952 | tf_op jit(solution)/shard_map/ppermute | solution.py:402
  29.3 13.8 %collective-permute-start.1 = (bf16[608,128]{1,0:T(8,128)(2,1)}, bf16[608,128]{1,0:T(8,128)(2,1)S(1)}, u32[]{:S(2)}, u32[]{:S(2)}) collective-permute-start(bf16[608,128]{1,0:T(8,128)(2,1)} %get-tuple-element.33), channel_id=1, source_target_pairs={{0,508},{4,8},{8,4},{12,16},{16,12},{20,24},{24,20},{28,32},{32,28... | collective-permute-start | bytes 466952 | tf_op jit(solution)/shard_map/ppermute | solution.py:402
  31.2 11.9 %collective-permute-start.2 = (bf16[176,512]{1,0:T(8,128)(2,1)}, bf16[176,512]{1,0:T(8,128)(2,1)S(1)}, u32[]{:S(2)}, u32[]{:S(2)}) collective-permute-start(bf16[176,512]{1,0:T(8,128)(2,1)} %get-tuple-element.35), channel_id=1, source_target_pairs={{0,256},{4,260},{8,264},{12,268},{16,272},{20,276},{24,280},{28,28... | collective-permute-start | bytes 540680 | tf_op jit(solution)/shard_map/ppermute | solution.py:402
  38.7 45.7 %collective-permute-start.8 = (bf16[256,512]{1,0:T(8,128)(2,1)S(1)}, bf16[256,512]{1,0:T(8,128)(2,1)S(1)}, u32[]{:S(2)}, u32[]{:S(2)}) collective-permute-start(bf16[256,512]{1,0:T(8,128)(2,1)S(1)} %pad_maximum_fusion), channel_id=1, source_target_pairs={{0,2},{1,3},{2,0},{3,1},{4,6},{5,7},{6,4},{7,5},{8,10},{9,11},{10,... | collective-permute-start | bytes 786440 | tf_op jit(solution)/shard_map/ppermute | solution.py:420
  49.2 35.2 %all-to-all-start = ((f32[128,1,128]{2,1,0:T(1,128)}), f32[128,1,128]{2,1,0:T(1,128)S(1)}, u32[]{:S(2)}, u32[]{:S(2)}) async-start(f32[128,1,128]{2,1,0:T(1,128)} %bitcast.3), calls=%async_computation | async-start | bytes 131072 | tf_op jit(solution)/shard_map/all_to_all | solution.py:425
  70.1 14.2 %collective-permute-start.4 = (f32[16,640]{1,0:T(8,128)S(1)}, f32[16,640]{1,0:T(8,128)S(1)}, u32[]{:S(2)}, u32[]{:S(2)}) collective-permute-start(f32[16,640]{1,0:T(8,128)S(1)} %get-tuple-element.40), channel_id=1, source_target_pairs={{0,4},{4,0},{8,12},{12,8},{16,20},{20,16},{24,28},{28,24},{32,36},... | collective-permute-start | bytes 122888 | tf_op jit(solution)/shard_map/ppermute | solution.py:402
  73.0 11.4 %collective-permute-start.5 = (f32[16,640]{1,0:T(8,128)S(1)}, f32[16,640]{1,0:T(8,128)S(1)}, u32[]{:S(2)}, u32[]{:S(2)}) collective-permute-start(f32[16,640]{1,0:T(8,128)S(1)} %get-tuple-element.41), channel_id=1, source_target_pairs={{0,508},{4,8},{8,4},{12,16},{16,12},{20,24},{24,20},{28,32},{32,28... | collective-permute-start | bytes 122888 | tf_op jit(solution)/shard_map/ppermute | solution.py:402
  75.7 8.7 %collective-permute-start.3 = (f32[16,512]{1,0:T(8,128)S(1)}, f32[16,512]{1,0:T(8,128)S(1)}, u32[]{:S(2)}, u32[]{:S(2)}) collective-permute-start(f32[16,512]{1,0:T(8,128)S(1)} %get-tuple-element.39), channel_id=1, source_target_pairs={{0,256},{4,260},{8,264},{12,268},{16,272},{20,276},{24,280},{28,28... | collective-permute-start | bytes 98312 | tf_op jit(solution)/shard_map/ppermute | solution.py:402
  89.5 28.3 %all-to-all-start.1 = ((f32[128,1,128]{2,1,0:T(1,128)}), f32[128,1,128]{2,1,0:T(1,128)S(1)}, u32[]{:S(2)}, u32[]{:S(2)}) async-start(f32[128,1,128]{2,1,0:T(1,128)} %bitcast.6), calls=%async_computation.1 | async-start | bytes 131072 | tf_op jit(solution)/shard_map/all_to_all | solution.py:425
  103.5 14.2 %collective-permute-start.10 = (f32[16,640]{1,0:T(8,128)S(1)}, f32[16,640]{1,0:T(8,128)S(1)}, u32[]{:S(2)}, u32[]{:S(2)}) collective-permute-start(f32[16,640]{1,0:T(8,128)S(1)} %get-tuple-element.47), channel_id=1, source_target_pairs={{0,4},{4,0},{8,12},{12,8},{16,20},{20,16},{24,28},{28,24},{32,36},... | collective-permute-start | bytes 122888 | tf_op jit(solution)/shard_map/ppermute | solution.py:402
  106.3 11.4 %collective-permute-start.11 = (f32[16,640]{1,0:T(8,128)S(1)}, f32[16,640]{1,0:T(8,128)S(1)}, u32[]{:S(2)}, u32[]{:S(2)}) collective-permute-start(f32[16,640]{1,0:T(8,128)S(1)} %get-tuple-element.48), channel_id=1, source_target_pairs={{0,508},{4,8},{8,4},{12,16},{16,12},{20,24},{24,20},{28,32},{32,28... | collective-permute-start | bytes 122888 | tf_op jit(solution)/shard_map/ppermute | solution.py:402
  109.1 8.7 %collective-permute-start.9 = (f32[16,512]{1,0:T(8,128)S(1)}, f32[16,512]{1,0:T(8,128)S(1)}, u32[]{:S(2)}, u32[]{:S(2)}) collective-permute-start(f32[16,512]{1,0:T(8,128)S(1)} %get-tuple-element.46), channel_id=1, source_target_pairs={{0,256},{4,260},{8,264},{12,268},{16,272},{20,276},{24,280},{28,28... | collective-permute-start | bytes 98312 | tf_op jit(solution)/shard_map/ppermute | solution.py:402
  122.8 28.3 %all-to-all-start.2 = ((f32[128,1,128]{2,1,0:T(1,128)}), f32[128,1,128]{2,1,0:T(1,128)S(1)}, u32[]{:S(2)}, u32[]{:S(2)}) async-start(f32[128,1,128]{2,1,0:T(1,128)} %bitcast.9), calls=%async_computation.2 | async-start | bytes 131072 | tf_op jit(solution)/shard_map/all_to_all | solution.py:425
  136.9 14.2 %collective-permute-start.13 = (f32[16,640]{1,0:T(8,128)S(1)}, f32[16,640]{1,0:T(8,128)S(1)}, u32[]{:S(2)}, u32[]{:S(2)}) collective-permute-start(f32[16,640]{1,0:T(8,128)S(1)} %get-tuple-element.53), channel_id=1, source_target_pairs={{0,4},{4,0},{8,12},{12,8},{16,20},{20,16},{24,28},{28,24},{32,36},... | collective-permute-start | bytes 122888 | tf_op jit(solution)/shard_map/ppermute | solution.py:402
  139.7 11.4 %collective-permute-start.14 = (f32[16,640]{1,0:T(8,128)S(1)}, f32[16,640]{1,0:T(8,128)S(1)}, u32[]{:S(2)}, u32[]{:S(2)}) collective-permute-start(f32[16,640]{1,0:T(8,128)S(1)} %get-tuple-element.54), channel_id=1, source_target_pairs={{0,508},{4,8},{8,4},{12,16},{16,12},{20,24},{24,20},{28,32},{32,28... | collective-permute-start | bytes 122888 | tf_op jit(solution)/shard_map/ppermute | solution.py:402
  142.5 8.7 %collective-permute-start.12 = (f32[16,512]{1,0:T(8,128)S(1)}, f32[16,512]{1,0:T(8,128)S(1)}, u32[]{:S(2)}, u32[]{:S(2)}) collective-permute-start(f32[16,512]{1,0:T(8,128)S(1)} %get-tuple-element.52), channel_id=1, source_target_pairs={{0,256},{4,260},{8,264},{12,268},{16,272},{20,276},{24,280},{28,28... | collective-permute-start | bytes 98312 | tf_op jit(solution)/shard_map/ppermute | solution.py:402
  151.2 1.0 copy-start.2
  155.6 7.8 %all-to-all-start.3 = ((f32[4,1,128]{2,1,0:T(1,128)}), f32[4,1,128]{2,1,0:T(1,128)S(1)}, u32[]{:S(2)}, u32[]{:S(2)}) async-start(f32[4,1,128]{2,1,0:T(1,128)} %bitcast.12), calls=%async_computation.3 | async-start | bytes 4096 | tf_op jit(solution)/shard_map/all_to_all | solution.py:425
  (2 other events, 1.6 us)

commit v6 on v5

--- a/solution.py
+++ b/solution.py
@@ -178,7 +178,7 @@
     near_x, near_lift = moved_by(near_x, step, near[:, BLK:])
     far_x, far_lift = moved_by(far_x, step, far[:, BLK:])
     part, mate_part = contact_terms(lift, mate_lift, statics, True)
-    mate_g = mate_g - step * mate + quarters_dot(mate_lift, *mate_kernel) + mate_part
+    mate_g = mate_g - step * mate + symmetric_dot(mate_lift, *mate_kernel) + mate_part
     near_face = near_face - step * near[:, :BLK] + fine_dot(near_lift, near_kernel[...])
     far_face = far_face - step * far[:, :BLK] + fine_dot(far_lift, far_kernel[...])
     lifted = whole_dot(lift, rows)
@@ -214,7 +214,14 @@
 
 TABLE = 2 * CASES
 SLOTS = TABLE + CASES
-PACKED = SLOTS + BLK
+UPPER = SLOTS + BLK
+UNIT = BLK // 4
+HALF = 5 * UNIT
+PACKED = UPPER + HALF
+HALVES = (
+    ((0, 0), (0, 1), (0, 2), (0, 3), (1, 1)),
+    ((1, 2), (1, 3), (2, 2), (2, 3), (3, 3)),
+)
 SIDE = 6 * CASES
 
 
@@ -227,16 +234,38 @@
     return high, (block - high.astype(f32)).astype(bf16)
 
 
-def quarters_dot(value, case, quarters):
-    blocks, total = split(value), None
-    for k in range(4):
-        index = lax.bitwise_xor(case, k)
-        block = blocks[0]
-        for i in range(1, 4):
-            block = jnp.where(index == i, blocks[i], block)
-        part = dot(jnp.concatenate(halves(block), axis=0), quarters[k])
-        total = part if total is None else total + part
-    return total[:CASES] + total[CASES:]
+def is_odd_case():
+    return lax.rem(lax.axis_index("case"), 2) == 1
+
+
+def store_half(packed, dual_ref):
+    odd = is_odd_case()
+    for n in range(5):
+        for k in range(4):
+            pair = []
+            for half in HALVES:
+                row, lane = (LOW + BLK * place for place in half[n])
+                pair.append(dual_ref[row + k * UNIT : row + (k + 1) * UNIT, lane : lane + BLK])
+            rows = slice(UPPER + n * UNIT, UPPER + (n + 1) * UNIT)
+            packed[rows, k * BLK : (k + 1) * BLK] = jnp.where(odd, pair[1], pair[0])
+
+
+def symmetric_dot(value, mine, other):
+    odd = is_odd_case()
+    pieces = jnp.where(odd, other, mine), jnp.where(odd, mine, other)
+    blocks = {}
+    for half, piece in zip(HALVES, pieces):
+        for n, key in enumerate(half):
+            blocks[key] = jnp.concatenate(split(piece[n * UNIT : (n + 1) * UNIT]), axis=0)
+    both = [jnp.concatenate(halves(block), axis=0) for block in split(value)]
+    outs = []
+    for j in range(4):
+        total = None
+        for i in range(4):
+            part = dot(both[i], blocks[min(i, j), max(i, j)], i > j)
+            total = part if total is None else total + part
+        outs.append(total[:CASES] + total[CASES:])
+    return jnp.concatenate(outs, axis=1)
 
 
 def prepare_kernel(*refs):
@@ -245,12 +274,13 @@
     piece = whole_copy(dual_hbm, dual_ref, sems)
     even = is_even()
     for k in range(4):
-        packed[SLOTS:, k * BLK : (k + 1) * BLK] = mortar[k * BLK : (k + 1) * BLK, :]
+        packed[SLOTS:UPPER, k * BLK : (k + 1) * BLK] = mortar[k * BLK : (k + 1) * BLK, :]
     table = slot_table(ids, count).astype(bf16)
     packed[TABLE:SLOTS, :] = jnp.concatenate([table] * 4, axis=1)
     x = x_ref[...]
     q = whole_dot(x, [piece(k, True) for k in range(len(STARTS))]) - right_ref[...]
     q_ref[...] = q
+    store_half(packed, dual_ref)
     packed[:CASES, :] = x[:, LOW:HIGH].astype(bf16)
     packed[CASES:TABLE, :] = q[:, LOW:HIGH].astype(bf16)
     contacts = split(x[:, LOW:HIGH])
@@ -265,7 +295,7 @@
 
 def statics_of(ids, count, mortar, packed):
     own = [mortar[k * BLK : (k + 1) * BLK, :] for k in range(4)]
-    mate = [packed[SLOTS:, k * BLK : (k + 1) * BLK] for k in range(4)]
+    mate = [packed[SLOTS:UPPER, k * BLK : (k + 1) * BLK] for k in range(4)]
     mate_table = packed[TABLE:SLOTS, :BLK].astype(f32)
     return slots(slot_table(ids, count)), own, slots(mate_table), mate
 
@@ -310,8 +340,8 @@
 
 def advanced(refs, piece):
     ids, count, sums, own, others, mate, near, far, mortar, packed, _ = refs[:11]
-    near_kernel, far_kernel, quarter, second, pair = refs[11:16]
-    quarters = (quarter[...], second[...], pair[:BLK, :], pair[BLK:, :])
+    near_kernel, far_kernel, other_half = refs[11:14]
+    mate_kernel = packed[UPPER:, :], other_half[...]
     statics = statics_of(ids, count, mortar, packed)
     offsets = [sum(WIDTHS[:k]) for k in range(len(WIDTHS))]
     lift_rows = [(k * CHUNK, CHUNK, piece(k, True)[2]) for k in range(2)]
@@ -324,16 +354,16 @@
         far[...],
         statics,
         lift_rows,
-        ((lax.axis_index("case"), quarters), near_kernel.at[SIDE:], far_kernel.at[SIDE:]),
+        (mate_kernel, near_kernel.at[SIDE:], far_kernel.at[SIDE:]),
     )
     return x, g, others, statics
 
 
 def advance_kernel(*refs):
-    dual_hbm, outs, (dual_ref, sems) = refs[16], refs[17:23], refs[23:]
+    dual_hbm, outs, (dual_ref, sems) = refs[14], refs[15:21], refs[21:]
     piece = whole_copy(dual_hbm, dual_ref, sems)
     even = is_even()
-    x, g, others, statics = advanced(refs[:16], piece)
+    x, g, others, statics = advanced(refs[:14], piece)
     pick = picks(refs[10][...], even)
     pieces = [piece(k, k >= 2) for k in range(len(STARTS))]
     image, row = tail(g, others, statics, pick, even, pieces)
@@ -341,9 +371,9 @@
 
 
 def last_advance_kernel(*refs):
-    dual_hbm, (own_out, others_out, row_out), (dual_ref, sems) = refs[16], refs[17:20], refs[20:]
+    dual_hbm, (own_out, others_out, row_out), (dual_ref, sems) = refs[14], refs[15:18], refs[18:]
     piece = whole_copy(dual_hbm, dual_ref, sems, STARTS[:2])
-    x, g, others, _ = advanced(refs[:16], piece)
+    x, g, others, _ = advanced(refs[:14], piece)
     own_out[:, :M] = x
     own_out[:, M:] = g
     others_out[...] = jnp.concatenate([others[1], others[4], others[5]], axis=1)
@@ -444,13 +474,10 @@
         (contact_ids, contact_count, multipliers, right_side, mortar, dual_ops),
         grant=PREPARE_GRANT,
     )
-    packed, dual_later = lax.optimization_barrier((packed, dual_ops))
     packed = with_mate(packed)
     near = near_kernel = with_near(to_near)
     far = far_kernel = with_far(to_far)
-    start = LOW + lax.rem(lax.axis_index("case"), 4) * BLK
-    quarter = lax.dynamic_slice(dual_later, (start, LOW), (BLK, CONTACT))
-    quarter = with_mate(quarter)
+
     shapes = [
         ((CASES, 3 * M), f32),
         ((CASES, sum(WIDTHS)), f32),
@@ -474,23 +501,22 @@
         far = with_far(to_far)
         near = with_near(to_near)
         if iteration == 1:
-            second = with_case(quarter, 1)
-            pair = with_case(jnp.concatenate([quarter, second]), 2)
+            other_half = with_case(packed[UPPER:], 1)
         operands = (
             contact_ids, contact_count, sums, own, others, mate, near, far, mortar, packed,
-            match, near_kernel, far_kernel, quarter, second, pair, dual_ops,
+            match, near_kernel, far_kernel, other_half, dual_ops,
         )
         if iteration < ITERS - 1:
             own, others, copies, to_mate, to_near, to_far = call(
                 advance_kernel,
-                scalars + [VMEM_SPEC] * 14 + [HBM_SPEC],
+                scalars + [VMEM_SPEC] * 12 + [HBM_SPEC],
                 shapes,
                 operands,
             )
     cases = lax.axis_size("case")
     own, others, norms = call(
         last_advance_kernel,
-        scalars + [VMEM_SPEC] * 14 + [HBM_SPEC],
+        scalars + [VMEM_SPEC] * 12 + [HBM_SPEC],
         [
             ((CASES, 2 * M), f32),
             ((CASES, CONTACT + 2 * BLK), f32),

time: 192 us -> 177 us (0.922)
  starting transfers between devices: 123 us -> 114 us
  local copies, waits for them, and re-layouts: 3.48 us -> 0.92 us
  waiting for transfers between devices: 9.35 us -> 7.36 us
    ppermute x13 -> x12, starting transfers between devices: 64.1 us -> 53.9 us  [swapped(): lax.ppermute(value, 'sub', [(i, other(i) % devices) for i in range(device...]
    all_to_all x4, starting transfers between devices: 52.8 us -> 57.1 us  [spread_sums(): rows = lax.all_to_all(copies.reshape(devices, 1, BLK), axis, 0, 0)]
    ppermute x2 -> x1, starting transfers between devices: 6.27 us -> 3.01 us  [with_case(): return lax.ppermute(value, 'case', [(i, i ^ bit) for i in range(cases)])]
    ppermute x13 -> x12, waiting for transfers between devices: 8.67 us -> 6.69 us  [swapped(): lax.ppermute(value, 'sub', [(i, other(i) % devices) for i in range(device...]
  transfers between devices with their start and end apart: 19 -> 17, of which waited for: 5 -> 5; matrix products, arithmetic and copies ran while one was open for 0% -> 0% of each run, Pallas kernels for 4% -> 4%
where the time goes in v6:
time: 177 us; the launch traced here: 176 us
  starting transfers between devices  114 us (64%)
  blocking collectives  26.9 us (15%)
  Pallas kernels  25.5 us (14%)
  waiting for transfers between devices  7.36 us (4%)
    all_to_all x4, starting transfers between devices, spread_sums(): rows = lax.all_to_all(copies.reshape(devices, 1, BLK), axis, 0, 0)  57.1 us
    ppermute x12, starting transfers between devices, swapped(): lax.ppermute(value, 'sub', [(i, other(i) % devices) for i in range(device...  53.9 us
    all_to_all x1, blocking collectives, spread_sums(): rows = lax.all_to_all(copies.reshape(devices, 1, BLK), axis, 0, 0)  26.9 us
    pallas_call x7, Pallas kernels, call(): pl.pallas_call(kernel, in_specs=specs, out_specs=[VMEM_SPEC] * len(shapes...  25.5 us
    ppermute x12, waiting for transfers between devices, swapped(): lax.ppermute(value, 'sub', [(i, other(i) % devices) for i in range(device...  6.69 us
  transfers between devices with their start and end apart: 17, of which 5 were waited for; matrix products, arithmetic and copies ran while one was open for 0% of the time, Pallas kernels for 4%

profile of v6, /device:TPU:1, one launch (start us, length us, event | category | flops | bytes accessed | tf_op | source)
XLA Modules:
  0.0 176.4 jit_solution(6749486252662909444)
XLA Ops:
  1.4 4.4 %shard_map.86 = (f32[16,1536]{1,0:T(8,128)}, bf16[336,512]{1,0:T(8,128)(2,1)}, bf16[608,128]{1,0:T(8,128)(2,1)}, bf16[608,128]{1,0:T(8,128)(2,1)}) custom-call(s32[1,4]{1,0:T(1,128)} %refs_0_.11, s32[1]{0:T(128)S(6)} %copy.14.refs_1_, f32[16,1536]{1,0:T(8,128)} %refs_2_.3, f32[16,1536]{1,0:T(8,128)} %refs_3_.1, bf16[512,128]{1,0:T(8,128)(2,1)} %bitcast.23, ...), custom_call_target="tpu_custom_call" | custom-call | tf_op jit(solution)/shard_map/pallas_call | solution.py:420
  5.8 8.3 %collective-permute-start.2 = (bf16[336,512]{1,0:T(8,128)(2,1)}, bf16[336,512]{1,0:T(8,128)(2,1)S(1)}, u32[]{:S(2)}, u32[]{:S(2)}) collective-permute-start(bf16[336,512]{1,0:T(8,128)(2,1)} %get-tuple-element.32), channel_id=1, source_target_pairs={{0,256},{4,260},{8,264},{12,268},{16,272},{20,276},{24,280},{28,28... | collective-permute-start | bytes 1032200 | tf_op jit(solution)/shard_map/ppermute | solution.py:432
  14.1 2.9 %collective-permute-start = (bf16[608,128]{1,0:T(8,128)(2,1)}, bf16[608,128]{1,0:T(8,128)(2,1)S(1)}, u32[]{:S(2)}, u32[]{:S(2)}) collective-permute-start(bf16[608,128]{1,0:T(8,128)(2,1)} %get-tuple-element.30), channel_id=1, source_target_pairs={{0,4},{4,0},{8,12},{12,8},{16,20},{20,16},{24,28},{28,24},{32,36},... | collective-permute-start | bytes 466952 | tf_op jit(solution)/shard_map/ppermute | solution.py:432
  17.0 3.9 %collective-permute-start.1 = (bf16[608,128]{1,0:T(8,128)(2,1)}, bf16[608,128]{1,0:T(8,128)(2,1)S(1)}, u32[]{:S(2)}, u32[]{:S(2)}) collective-permute-start(bf16[608,128]{1,0:T(8,128)(2,1)} %get-tuple-element.31), channel_id=1, source_target_pairs={{0,508},{4,8},{8,4},{12,16},{16,12},{20,24},{24,20},{28,32},{32,28... | collective-permute-start | bytes 466952 | tf_op jit(solution)/shard_map/ppermute | solution.py:432
  20.9 2.9 %collective-permute-done.2.refs_7_.refs_9_.refs_5_ = bf16[336,512]{1,0:T(8,128)(2,1)S(1)} collective-permute-done((bf16[336,512]{1,0:T(8,128)(2,1)}, bf16[336,512]{1,0:T(8,128)(2,1)S(1)}, u32[]{:S(2)}, u32[]{:S(2)}) %collective-permute-start.2) | collective-permute-done | bytes 344096 | tf_op jit(solution)/shard_map/ppermute | solution.py:432
  23.8 3.0 %collective-permute-start.6 = (bf16[160,512]{1,0:T(8,128)(2,1)S(1)}, bf16[160,512]{1,0:T(8,128)(2,1)S(1)}, u32[]{:S(2)}, u32[]{:S(2)}) collective-permute-start(bf16[160,512]{1,0:T(8,128)(2,1)S(1)} %slice.8), channel_id=1, source_target_pairs={{0,1},{1,0},{2,3},{3,2},{4,5},{5,4},{6,7},{7,6},{8,9},{9,8},{10,11... | collective-permute-start | bytes 491528 | tf_op jit(solution)/shard_map/ppermute | solution.py:450
  27.8 4.4 %shard_map.87 = (f32[16,4608]{1,0:T(8,128)S(1)}, f32[16,2304]{1,0:T(8,128)S(1)}, f32[128,128]{1,0:T(8,128)}, f32[16,512]{1,0:T(8,128)S(1)}, f32[16,640]{1,0:T(8,128)S(1)}, /*index=5*/f32[16,640]{1,0:T(8,128)S(1)}) custom-call(s32[1,4]{1,0:T(1,128)S(1)} %copy-done.6, s32[1]{0:T(128)S(6)} %copy.14.refs_1_, f32[16,1536]{1,0:T(8,128)S(1)} %copy-done.3, ...), custom_call_target="tpu_custom_call" | custom-call | tf_op jit(solution)/shard_map/pallas_call | solution.py:420
  32.2 25.2 %all-to-all-start = ((f32[128,1,128]{2,1,0:T(1,128)}), f32[128,1,128]{2,1,0:T(1,128)S(1)}, u32[]{:S(2)}, u32[]{:S(2)}) async-start(f32[128,1,128]{2,1,0:T(1,128)} %bitcast.3), calls=%async_computation | async-start | bytes 131072 | tf_op jit(solution)/shard_map/all_to_all | solution.py:455
  57.4 2.8 %collective-permute-start.4 = (f32[16,640]{1,0:T(8,128)S(1)}, f32[16,640]{1,0:T(8,128)S(1)}, u32[]{:S(2)}, u32[]{:S(2)}) collective-permute-start(f32[16,640]{1,0:T(8,128)S(1)} %get-tuple-element.37), channel_id=1, source_target_pairs={{0,4},{4,0},{8,12},{12,8},{16,20},{20,16},{24,28},{28,24},{32,36},... | collective-permute-start | bytes 122888 | tf_op jit(solution)/shard_map/ppermute | solution.py:432
  60.2 2.8 %collective-permute-start.5 = (f32[16,640]{1,0:T(8,128)S(1)}, f32[16,640]{1,0:T(8,128)S(1)}, u32[]{:S(2)}, u32[]{:S(2)}) collective-permute-start(f32[16,640]{1,0:T(8,128)S(1)} %get-tuple-element.38), channel_id=1, source_target_pairs={{0,508},{4,8},{8,4},{12,16},{16,12},{20,24},{24,20},{28,32},{32,28... | collective-permute-start | bytes 122888 | tf_op jit(solution)/shard_map/ppermute | solution.py:432
  62.9 7.3 %collective-permute-start.3 = (f32[16,512]{1,0:T(8,128)S(1)}, f32[16,512]{1,0:T(8,128)S(1)}, u32[]{:S(2)}, u32[]{:S(2)}) collective-permute-start(f32[16,512]{1,0:T(8,128)S(1)} %get-tuple-element.36), channel_id=1, source_target_pairs={{0,256},{4,260},{8,264},{12,268},{16,272},{20,276},{24,280},{28,28... | collective-permute-start | bytes 98312 | tf_op jit(solution)/shard_map/ppermute | solution.py:432
  71.6 4.7 %shard_map.88 = (f32[16,4608]{1,0:T(8,128)S(1)}, f32[16,2304]{1,0:T(8,128)S(1)}, f32[128,128]{1,0:T(8,128)}, f32[16,512]{1,0:T(8,128)S(1)}, f32[16,640]{1,0:T(8,128)S(1)}, /*index=5*/f32[16,640]{1,0:T(8,128)S(1)}) custom-call(s32[1,4]{1,0:T(1,128)S(1)} %copy-done.6, s32[1]{0:T(128)S(6)} %copy.14.refs_1_, f32[128,128]{1,0:T(8,128)S(1)} %bitcast.29, ...), custom_call_target="tpu_custom_call" | custom-call | tf_op jit(solution)/shard_map/pallas_call | solution.py:420
  76.4 14.2 %all-to-all-start.1 = ((f32[128,1,128]{2,1,0:T(1,128)}), f32[128,1,128]{2,1,0:T(1,128)S(1)}, u32[]{:S(2)}, u32[]{:S(2)}) async-start(f32[128,1,128]{2,1,0:T(1,128)} %bitcast.6), calls=%async_computation.1 | async-start | bytes 131072 | tf_op jit(solution)/shard_map/all_to_all | solution.py:455
  90.6 2.8 %collective-permute-start.8 = (f32[16,640]{1,0:T(8,128)S(1)}, f32[16,640]{1,0:T(8,128)S(1)}, u32[]{:S(2)}, u32[]{:S(2)}) collective-permute-start(f32[16,640]{1,0:T(8,128)S(1)} %get-tuple-element.43), channel_id=1, source_target_pairs={{0,4},{4,0},{8,12},{12,8},{16,20},{20,16},{24,28},{28,24},{32,36},... | collective-permute-start | bytes 122888 | tf_op jit(solution)/shard_map/ppermute | solution.py:432
  93.4 2.8 %collective-permute-start.9 = (f32[16,640]{1,0:T(8,128)S(1)}, f32[16,640]{1,0:T(8,128)S(1)}, u32[]{:S(2)}, u32[]{:S(2)}) collective-permute-start(f32[16,640]{1,0:T(8,128)S(1)} %get-tuple-element.44), channel_id=1, source_target_pairs={{0,508},{4,8},{8,4},{12,16},{16,12},{20,24},{24,20},{28,32},{32,28... | collective-permute-start | bytes 122888 | tf_op jit(solution)/shard_map/ppermute | solution.py:432
  96.2 7.3 %collective-permute-start.7 = (f32[16,512]{1,0:T(8,128)S(1)}, f32[16,512]{1,0:T(8,128)S(1)}, u32[]{:S(2)}, u32[]{:S(2)}) collective-permute-start(f32[16,512]{1,0:T(8,128)S(1)} %get-tuple-element.42), channel_id=1, source_target_pairs={{0,256},{4,260},{8,264},{12,268},{16,272},{20,276},{24,280},{28,28... | collective-permute-start | bytes 98312 | tf_op jit(solution)/shard_map/ppermute | solution.py:432
  104.8 4.7 %shard_map.89 = (f32[16,4608]{1,0:T(8,128)S(1)}, f32[16,2304]{1,0:T(8,128)S(1)}, f32[128,128]{1,0:T(8,128)}, f32[16,512]{1,0:T(8,128)S(1)}, f32[16,640]{1,0:T(8,128)S(1)}, /*index=5*/f32[16,640]{1,0:T(8,128)S(1)}) custom-call(s32[1,4]{1,0:T(1,128)S(1)} %copy-done.6, s32[1]{0:T(128)S(6)} %copy.14.refs_1_, f32[128,128]{1,0:T(8,128)S(1)} %bitcast.30, ...), custom_call_target="tpu_custom_call" | custom-call | tf_op jit(solution)/shard_map/pallas_call | solution.py:420
  109.6 14.1 %all-to-all-start.2 = ((f32[128,1,128]{2,1,0:T(1,128)}), f32[128,1,128]{2,1,0:T(1,128)S(1)}, u32[]{:S(2)}, u32[]{:S(2)}) async-start(f32[128,1,128]{2,1,0:T(1,128)} %bitcast.9), calls=%async_computation.2 | async-start | bytes 131072 | tf_op jit(solution)/shard_map/all_to_all | solution.py:455
  123.6 2.8 %collective-permute-start.11 = (f32[16,640]{1,0:T(8,128)S(1)}, f32[16,640]{1,0:T(8,128)S(1)}, u32[]{:S(2)}, u32[]{:S(2)}) collective-permute-start(f32[16,640]{1,0:T(8,128)S(1)} %get-tuple-element.49), channel_id=1, source_target_pairs={{0,4},{4,0},{8,12},{12,8},{16,20},{20,16},{24,28},{28,24},{32,36},... | collective-permute-start | bytes 122888 | tf_op jit(solution)/shard_map/ppermute | solution.py:432
  129.2 7.5 %collective-permute-start.10 = (f32[16,512]{1,0:T(8,128)S(1)}, f32[16,512]{1,0:T(8,128)S(1)}, u32[]{:S(2)}, u32[]{:S(2)}) collective-permute-start(f32[16,512]{1,0:T(8,128)S(1)} %get-tuple-element.48), channel_id=1, source_target_pairs={{0,256},{4,260},{8,264},{12,268},{16,272},{20,276},{24,280},{28,28... | collective-permute-start | bytes 98312 | tf_op jit(solution)/shard_map/ppermute | solution.py:432
  137.9 3.0 %shard_map.90 = (f32[16,3072]{1,0:T(8,128)S(1)}, f32[16,768]{1,0:T(8,128)S(1)}, f32[4,128]{1,0:T(4,128)}) custom-call(s32[1,4]{1,0:T(1,128)S(1)} %copy-done.6, s32[1]{0:T(128)S(6)} %copy.14.refs_1_, f32[128,128]{1,0:T(8,128)S(1)} %bitcast.31, f32[16,4608]{1,0:T(8,128)S(1)} %get-tuple-element.46.refs_3_, f32[16,2304]{1,0:T(8,128)S(1)} %get-tuple-element.47.refs_4_, ...), custom_call_target="tpu_custom_call" | custom-call | tf_op jit(solution)/shard_map/pallas_call | solution.py:420
  140.9 3.7 %all-to-all-start.3 = ((f32[4,1,128]{2,1,0:T(1,128)}), f32[4,1,128]{2,1,0:T(1,128)S(1)}, u32[]{:S(2)}, u32[]{:S(2)}) async-start(f32[4,1,128]{2,1,0:T(1,128)} %bitcast.12), calls=%async_computation.3 | async-start | bytes 4096 | tf_op jit(solution)/shard_map/all_to_all | solution.py:455
  144.7 3.4 %shard_map.91 = f32[128,128]{1,0:T(8,128)S(1)} custom-call(s32[1,4]{1,0:T(1,128)S(1)} %copy-done.6, s32[1]{0:T(128)S(6)} %copy.14.refs_1_, f32[16,3072]{1,0:T(8,128)S(1)} %get-tuple-element.51.refs_2_.own, f32[16,768]{1,0:T(8,128)S(1)} %get-tuple-element.52.refs_3_, bf16[512,128]{1,0:T(8,128)(2,1)S(1)} %bitcast.28, bf16[336,512]{1,0:T(8,128)(2,1)S(1)} %copy-done.1, ...), custom_call_target="tpu_custom_call" | custom-call | tf_op jit(solution)/shard_map/pallas_call | solution.py:420
  148.8 26.9 %all_to_all.25 = f32[128,1,128]{2,1,0:T(1,128)S(1)} all-to-all(f32[128,1,128]{2,1,0:T(1,128)S(1)} %bitcast.38), channel_id=1, replica_groups=mesh['sub'=128,'case'=4] {'sub'}, dimensions={0} | all-to-all | bytes 131072 | tf_op jit(solution)/shard_map/all_to_all | solution.py:455
  (36 shorter events, 8.9 us)
Async XLA Ops:
  0.6 26.2 %copy-start.6 = (s32[1,4]{1,0:T(1,128)S(1)}, s32[1,4]{1,0:T(1,128)}, u32[]{:S(2)}) copy-start(s32[1,4]{1,0:T(1,128)} %refs_0_.11) | copy-start | bytes 52
  0.6 26.2 %copy-start.3 = (f32[16,1536]{1,0:T(8,128)S(1)}, f32[16,1536]{1,0:T(8,128)}, u32[]{:S(2)}) copy-start(f32[16,1536]{1,0:T(8,128)} %refs_2_.3) | copy-start | bytes 294916
  0.7 26.2 %copy-start.2 = (bf16[1,4,128,128]{3,2,1,0:T(8,128)(2,1)S(1)}, bf16[1,4,128,128]{3,2,1,0:T(8,128)(2,1)}, u32[]{:S(2)}) copy-start(bf16[1,4,128,128]{3,2,1,0:T(8,128)(2,1)} %param.11) | copy-start | bytes 393220
  0.7 26.2 %copy-start.5 = (s32[1,2,128]{2,1,0:T(2,128)S(1)}, s32[1,2,128]{2,1,0:T(2,128)}, u32[]{:S(2)}) copy-start(s32[1,2,128]{2,1,0:T(2,128)} %param.10) | copy-start | bytes 3076
  5.8 18.0 %collective-permute-start.2 = (bf16[336,512]{1,0:T(8,128)(2,1)}, bf16[336,512]{1,0:T(8,128)(2,1)S(1)}, u32[]{:S(2)}, u32[]{:S(2)}) collective-permute-start(bf16[336,512]{1,0:T(8,128)(2,1)} %get-tuple-element.32), channel_id=1, source_target_pairs={{0,256},{4,260},{8,264},{12,268},{16,272},{20,276},{24,280},{28,28... | collective-permute-start | bytes 1032200 | tf_op jit(solution)/shard_map/ppermute | solution.py:432
  14.1 12.7 %collective-permute-start = (bf16[608,128]{1,0:T(8,128)(2,1)}, bf16[608,128]{1,0:T(8,128)(2,1)S(1)}, u32[]{:S(2)}, u32[]{:S(2)}) collective-permute-start(bf16[608,128]{1,0:T(8,128)(2,1)} %get-tuple-element.30), channel_id=1, source_target_pairs={{0,4},{4,0},{8,12},{12,8},{16,20},{20,16},{24,28},{28,24},{32,36},... | collective-permute-start | bytes 466952 | tf_op jit(solution)/shard_map/ppermute | solution.py:432
  17.0 9.9 %collective-permute-start.1 = (bf16[608,128]{1,0:T(8,128)(2,1)}, bf16[608,128]{1,0:T(8,128)(2,1)S(1)}, u32[]{:S(2)}, u32[]{:S(2)}) collective-permute-start(bf16[608,128]{1,0:T(8,128)(2,1)} %get-tuple-element.31), channel_id=1, source_target_pairs={{0,508},{4,8},{8,4},{12,16},{16,12},{20,24},{24,20},{28,32},{32,28... | collective-permute-start | bytes 466952 | tf_op jit(solution)/shard_map/ppermute | solution.py:432
  23.8 47.9 %copy-start = (bf16[336,512]{1,0:T(8,128)(2,1)}, bf16[336,512]{1,0:T(8,128)(2,1)S(1)}, u32[]{:S(2)}) copy-start(bf16[336,512]{1,0:T(8,128)(2,1)S(1)} %collective-permute-done.2.refs_7_.refs_9_.refs_5_) | copy-start | bytes 1032196
  23.8 47.8 %collective-permute-start.6 = (bf16[160,512]{1,0:T(8,128)(2,1)S(1)}, bf16[160,512]{1,0:T(8,128)(2,1)S(1)}, u32[]{:S(2)}, u32[]{:S(2)}) collective-permute-start(bf16[160,512]{1,0:T(8,128)(2,1)S(1)} %slice.8), channel_id=1, source_target_pairs={{0,1},{1,0},{2,3},{3,2},{4,5},{5,4},{6,7},{7,6},{8,9},{9,8},{10,11... | collective-permute-start | bytes 491528 | tf_op jit(solution)/shard_map/ppermute | solution.py:450
  26.9 0.9 copy-start.4
  32.2 39.4 %all-to-all-start = ((f32[128,1,128]{2,1,0:T(1,128)}), f32[128,1,128]{2,1,0:T(1,128)S(1)}, u32[]{:S(2)}, u32[]{:S(2)}) async-start(f32[128,1,128]{2,1,0:T(1,128)} %bitcast.3), calls=%async_computation | async-start | bytes 131072 | tf_op jit(solution)/shard_map/all_to_all | solution.py:455
  57.4 14.2 %collective-permute-start.4 = (f32[16,640]{1,0:T(8,128)S(1)}, f32[16,640]{1,0:T(8,128)S(1)}, u32[]{:S(2)}, u32[]{:S(2)}) collective-permute-start(f32[16,640]{1,0:T(8,128)S(1)} %get-tuple-element.37), channel_id=1, source_target_pairs={{0,4},{4,0},{8,12},{12,8},{16,20},{20,16},{24,28},{28,24},{32,36},... | collective-permute-start | bytes 122888 | tf_op jit(solution)/shard_map/ppermute | solution.py:432
  60.2 11.4 %collective-permute-start.5 = (f32[16,640]{1,0:T(8,128)S(1)}, f32[16,640]{1,0:T(8,128)S(1)}, u32[]{:S(2)}, u32[]{:S(2)}) collective-permute-start(f32[16,640]{1,0:T(8,128)S(1)} %get-tuple-element.38), channel_id=1, source_target_pairs={{0,508},{4,8},{8,4},{12,16},{16,12},{20,24},{24,20},{28,32},{32,28... | collective-permute-start | bytes 122888 | tf_op jit(solution)/shard_map/ppermute | solution.py:432
  62.9 8.7 %collective-permute-start.3 = (f32[16,512]{1,0:T(8,128)S(1)}, f32[16,512]{1,0:T(8,128)S(1)}, u32[]{:S(2)}, u32[]{:S(2)}) collective-permute-start(f32[16,512]{1,0:T(8,128)S(1)} %get-tuple-element.36), channel_id=1, source_target_pairs={{0,256},{4,260},{8,264},{12,268},{16,272},{20,276},{24,280},{28,28... | collective-permute-start | bytes 98312 | tf_op jit(solution)/shard_map/ppermute | solution.py:432
  76.4 61.5 %copy-start.1 = (bf16[336,512]{1,0:T(8,128)(2,1)S(1)}, bf16[336,512]{1,0:T(8,128)(2,1)}, u32[]{:S(2)}) copy-start(bf16[336,512]{1,0:T(8,128)(2,1)} %copy-done) | copy-start | bytes 1032196
  76.4 28.4 %all-to-all-start.1 = ((f32[128,1,128]{2,1,0:T(1,128)}), f32[128,1,128]{2,1,0:T(1,128)S(1)}, u32[]{:S(2)}, u32[]{:S(2)}) async-start(f32[128,1,128]{2,1,0:T(1,128)} %bitcast.6), calls=%async_computation.1 | async-start | bytes 131072 | tf_op jit(solution)/shard_map/all_to_all | solution.py:455
  90.6 14.2 %collective-permute-start.8 = (f32[16,640]{1,0:T(8,128)S(1)}, f32[16,640]{1,0:T(8,128)S(1)}, u32[]{:S(2)}, u32[]{:S(2)}) collective-permute-start(f32[16,640]{1,0:T(8,128)S(1)} %get-tuple-element.43), channel_id=1, source_target_pairs={{0,4},{4,0},{8,12},{12,8},{16,20},{20,16},{24,28},{28,24},{32,36},... | collective-permute-start | bytes 122888 | tf_op jit(solution)/shard_map/ppermute | solution.py:432
  93.4 11.4 %collective-permute-start.9 = (f32[16,640]{1,0:T(8,128)S(1)}, f32[16,640]{1,0:T(8,128)S(1)}, u32[]{:S(2)}, u32[]{:S(2)}) collective-permute-start(f32[16,640]{1,0:T(8,128)S(1)} %get-tuple-element.44), channel_id=1, source_target_pairs={{0,508},{4,8},{8,4},{12,16},{16,12},{20,24},{24,20},{28,32},{32,28... | collective-permute-start | bytes 122888 | tf_op jit(solution)/shard_map/ppermute | solution.py:432
  96.2 8.7 %collective-permute-start.7 = (f32[16,512]{1,0:T(8,128)S(1)}, f32[16,512]{1,0:T(8,128)S(1)}, u32[]{:S(2)}, u32[]{:S(2)}) collective-permute-start(f32[16,512]{1,0:T(8,128)S(1)} %get-tuple-element.42), channel_id=1, source_target_pairs={{0,256},{4,260},{8,264},{12,268},{16,272},{20,276},{24,280},{28,28... | collective-permute-start | bytes 98312 | tf_op jit(solution)/shard_map/ppermute | solution.py:432
  109.6 28.3 %all-to-all-start.2 = ((f32[128,1,128]{2,1,0:T(1,128)}), f32[128,1,128]{2,1,0:T(1,128)S(1)}, u32[]{:S(2)}, u32[]{:S(2)}) async-start(f32[128,1,128]{2,1,0:T(1,128)} %bitcast.9), calls=%async_computation.2 | async-start | bytes 131072 | tf_op jit(solution)/shard_map/all_to_all | solution.py:455
  123.6 14.2 %collective-permute-start.11 = (f32[16,640]{1,0:T(8,128)S(1)}, f32[16,640]{1,0:T(8,128)S(1)}, u32[]{:S(2)}, u32[]{:S(2)}) collective-permute-start(f32[16,640]{1,0:T(8,128)S(1)} %get-tuple-element.49), channel_id=1, source_target_pairs={{0,4},{4,0},{8,12},{12,8},{16,20},{20,16},{24,28},{28,24},{32,36},... | collective-permute-start | bytes 122888 | tf_op jit(solution)/shard_map/ppermute | solution.py:432
  126.4 11.4 %collective-permute-start.12 = (f32[16,640]{1,0:T(8,128)S(1)}, f32[16,640]{1,0:T(8,128)S(1)}, u32[]{:S(2)}, u32[]{:S(2)}) collective-permute-start(f32[16,640]{1,0:T(8,128)S(1)} %get-tuple-element.50), channel_id=1, source_target_pairs={{0,508},{4,8},{8,4},{12,16},{16,12},{20,24},{24,20},{28,32},{32,28... | collective-permute-start | bytes 122888 | tf_op jit(solution)/shard_map/ppermute | solution.py:432
  129.2 8.7 %collective-permute-start.10 = (f32[16,512]{1,0:T(8,128)S(1)}, f32[16,512]{1,0:T(8,128)S(1)}, u32[]{:S(2)}, u32[]{:S(2)}) collective-permute-start(f32[16,512]{1,0:T(8,128)S(1)} %get-tuple-element.48), channel_id=1, source_target_pairs={{0,256},{4,260},{8,264},{12,268},{16,272},{20,276},{24,280},{28,28... | collective-permute-start | bytes 98312 | tf_op jit(solution)/shard_map/ppermute | solution.py:432
  140.9 7.8 %all-to-all-start.3 = ((f32[4,1,128]{2,1,0:T(1,128)}), f32[4,1,128]{2,1,0:T(1,128)S(1)}, u32[]{:S(2)}, u32[]{:S(2)}) async-start(f32[4,1,128]{2,1,0:T(1,128)} %bitcast.12), calls=%async_computation.3 | async-start | bytes 4096 | tf_op jit(solution)/shard_map/all_to_all | solution.py:455

commit v7 on v6

--- a/solution.py
+++ b/solution.py
@@ -212,7 +212,7 @@
     return piece
 
 
-TABLE = 2 * CASES
+TABLE = 0
 SLOTS = TABLE + CASES
 UPPER = SLOTS + BLK
 UNIT = BLK // 4
@@ -238,14 +238,14 @@
     return lax.rem(lax.axis_index("case"), 2) == 1
 
 
-def store_half(packed, dual_ref):
+def store_half(packed, block_ref):
     odd = is_odd_case()
     for n in range(5):
         for k in range(4):
             pair = []
             for half in HALVES:
-                row, lane = (LOW + BLK * place for place in half[n])
-                pair.append(dual_ref[row + k * UNIT : row + (k + 1) * UNIT, lane : lane + BLK])
+                row, lane = (BLK * place for place in half[n])
+                pair.append(block_ref[row + k * UNIT : row + (k + 1) * UNIT, lane : lane + BLK])
             rows = slice(UPPER + n * UNIT, UPPER + (n + 1) * UNIT)
             packed[rows, k * BLK : (k + 1) * BLK] = jnp.where(odd, pair[1], pair[0])
 
@@ -268,21 +268,27 @@
     return jnp.concatenate(outs, axis=1)
 
 
-def prepare_kernel(*refs):
-    ids, count, x_ref, right_ref, mortar, dual_hbm = refs[:6]
-    q_ref, packed, near_ref, far_ref, dual_ref, sems = refs[6:]
-    piece = whole_copy(dual_hbm, dual_ref, sems)
-    even = is_even()
+def pack_kernel(ids, count, mortar, dual_hbm, packed, block_ref, sem):
+    contact = pl.ds(LOW, CONTACT)
+    copy = pltpu.make_async_copy(dual_hbm.at[contact, contact], block_ref, sem)
+    copy.start()
     for k in range(4):
         packed[SLOTS:UPPER, k * BLK : (k + 1) * BLK] = mortar[k * BLK : (k + 1) * BLK, :]
     table = slot_table(ids, count).astype(bf16)
     packed[TABLE:SLOTS, :] = jnp.concatenate([table] * 4, axis=1)
+    copy.wait()
+    store_half(packed, block_ref)
+
+
+def prepare_kernel(*refs):
+    x_ref, right_ref, dual_hbm, q_ref, first_ref, near_ref, far_ref, dual_ref, sems = refs
+    piece = whole_copy(dual_hbm, dual_ref, sems)
+    even = is_even()
     x = x_ref[...]
     q = whole_dot(x, [piece(k, True) for k in range(len(STARTS))]) - right_ref[...]
     q_ref[...] = q
-    store_half(packed, dual_ref)
-    packed[:CASES, :] = x[:, LOW:HIGH].astype(bf16)
-    packed[CASES:TABLE, :] = q[:, LOW:HIGH].astype(bf16)
+    first_ref[:CASES, :] = x[:, LOW:HIGH].astype(bf16)
+    first_ref[CASES:, :] = q[:, LOW:HIGH].astype(bf16)
     contacts = split(x[:, LOW:HIGH])
     both = [(near_ref,), (far_ref,)]
     for (ref,), face, grad in zip(both, faces_of(x, even), faces_of(q, even)):
@@ -320,14 +326,14 @@
 
 
 def begin_kernel(*refs):
-    ids, count, x_ref, q_ref, near, far, mortar, packed, match, dual_hbm = refs[:10]
-    outs, (dual_ref, sems) = refs[10:16], refs[16:]
+    ids, count, x_ref, q_ref, first, near, far, mortar, packed, match, dual_hbm = refs[:11]
+    outs, (dual_ref, sems) = refs[11:17], refs[17:]
     piece = whole_copy(dual_hbm, dual_ref, sems)
     even = is_even()
     statics = statics_of(ids, count, mortar, packed)
     pick = picks(match[...], even)
     x = x_ref[...]
-    mate = packed[:CASES, :].astype(f32), packed[CASES:TABLE, :].astype(f32)
+    mate = first[:CASES, :].astype(f32), first[CASES:, :].astype(f32)
     sides = side_values(near), side_values(far)
     g, others = begin(x, q_ref[...], mate, *sides, statics, pick, even)
     pieces = [piece(k, True) for k in range(len(STARTS))]
@@ -415,14 +421,17 @@
 HBM_SPEC = pl.BlockSpec(memory_space=pltpu.HBM)
 
 
-def call(kernel, specs, shapes, operands, scratch=True, grant=52):
-    scratch_shapes = [pltpu.VMEM((M, M), bf16), pltpu.SemaphoreType.DMA((len(STARTS),))] if scratch else []
+WHOLE = [pltpu.VMEM((M, M), bf16), pltpu.SemaphoreType.DMA((len(STARTS),))]
+BLOCK = [pltpu.VMEM((CONTACT, CONTACT), bf16), pltpu.SemaphoreType.DMA]
+
+
+def call(kernel, specs, shapes, operands, scratch=WHOLE, grant=52):
     return pl.pallas_call(
         kernel,
         in_specs=specs,
         out_specs=[VMEM_SPEC] * len(shapes),
         out_shape=[jax.ShapeDtypeStruct(shape, kind) for shape, kind in shapes],
-        scratch_shapes=scratch_shapes,
+        scratch_shapes=scratch,
         compiler_params=pltpu.CompilerParams(vmem_limit_bytes=grant << 20),
     )(*operands)
 
@@ -462,19 +471,28 @@
     match = glue_match[0]
     scalars = [SMEM_SPEC, SMEM_SPEC]
 
-    q, packed, to_near, to_far = call(
+    (packed,) = call(
+        pack_kernel,
+        scalars + [VMEM_SPEC, HBM_SPEC],
+        [((PACKED, CONTACT), bf16)],
+        (contact_ids, contact_count, mortar, dual_ops),
+        scratch=BLOCK,
+        grant=PREPARE_GRANT,
+    )
+    packed = with_mate(packed)
+    q, first, to_near, to_far = call(
         prepare_kernel,
-        scalars + [VMEM_SPEC] * 3 + [HBM_SPEC],
+        [VMEM_SPEC] * 2 + [HBM_SPEC],
         [
             ((CASES, M), f32),
-            ((PACKED, CONTACT), bf16),
+            ((2 * CASES, CONTACT), bf16),
             ((SIDE + CONTACT, BLK), bf16),
             ((SIDE + CONTACT, BLK), bf16),
         ],
-        (contact_ids, contact_count, multipliers, right_side, mortar, dual_ops),
+        (multipliers, right_side, dual_ops),
         grant=PREPARE_GRANT,
     )
-    packed = with_mate(packed)
+    first = with_mate(first)
     near = near_kernel = with_near(to_near)
     far = far_kernel = with_far(to_far)
 
@@ -488,11 +506,11 @@
     ]
     own, others, copies, to_mate, to_near, to_far = call(
         begin_kernel,
-        scalars + [VMEM_SPEC] * 7 + [HBM_SPEC],
+        scalars + [VMEM_SPEC] * 8 + [HBM_SPEC],
         shapes,
         (
-            contact_ids, contact_count, multipliers, q, near, far, mortar, packed, match,
-            dual_ops,
+            contact_ids, contact_count, multipliers, q, first, near, far, mortar, packed,
+            match, dual_ops,
         ),
     )
     for iteration in range(1, ITERS):
@@ -539,7 +557,7 @@
         [VMEM_SPEC, VMEM_SPEC],
         [((CASES, M), f32), ((1, BLK), f32)],
         (sums, own),
-        scratch=False,
+        scratch=[],
         grant=16,
     )
     return (x, norm[0, :1])

time: 177 us -> 183 us (1.034)
  starting transfers between devices: 114 us -> 119 us
  Pallas kernels: 25.5 us -> 28.1 us
    ppermute x12 -> x13, starting transfers between devices: 53.9 us -> 62.1 us  [swapped(): lax.ppermute(value, 'sub', [(i, other(i) % devices) for i in range(device...]
    all_to_all x4, starting transfers between devices: 57.1 us -> 53.7 us  [spread_sums(): rows = lax.all_to_all(copies.reshape(devices, 1, BLK), axis, 0, 0)]
    pallas_call x7 -> x8, Pallas kernels: 25.5 us -> 28.1 us  [call(): pl.pallas_call(kernel, in_specs=specs, out_specs=[VMEM_SPEC] * len(shapes...]
    ppermute x12 -> x13, waiting for transfers between devices: 6.69 us -> 5.29 us  [swapped(): lax.ppermute(value, 'sub', [(i, other(i) % devices) for i in range(device...]
  transfers between devices with their start and end apart: 17 -> 18, of which waited for: 5 -> 5; matrix products, arithmetic and copies ran while one was open for 0% -> 0% of each run, Pallas kernels for 4% -> 7%
where the time goes in v7:
time: 183 us; the launch traced here: 182 us
  starting transfers between devices  119 us (65%)
  Pallas kernels  28.1 us (15%)
  blocking collectives  26.9 us (15%)
  waiting for transfers between devices  5.97 us (3%)
    ppermute x13, starting transfers between devices, swapped(): lax.ppermute(value, 'sub', [(i, other(i) % devices) for i in range(device...  62.1 us
    all_to_all x4, starting transfers between devices, spread_sums(): rows = lax.all_to_all(copies.reshape(devices, 1, BLK), axis, 0, 0)  53.7 us
    pallas_call x8, Pallas kernels, call(): pl.pallas_call(kernel, in_specs=specs, out_specs=[VMEM_SPEC] * len(shapes...  28.1 us
    all_to_all x1, blocking collectives, spread_sums(): rows = lax.all_to_all(copies.reshape(devices, 1, BLK), axis, 0, 0)  26.9 us
    ppermute x13, waiting for transfers between devices, swapped(): lax.ppermute(value, 'sub', [(i, other(i) % devices) for i in range(device...  5.29 us
  transfers between devices with their start and end apart: 18, of which 5 were waited for; matrix products, arithmetic and copies ran while one was open for 0% of the time, Pallas kernels for 7%

profile of v7, /device:TPU:1, one launch (start us, length us, event | category | flops | bytes accessed | tf_op | source)
XLA Modules:
  0.0 182.4 jit_solution(14245589420241738196)
XLA Ops:
  1.3 2.8 %shard_map.87 = bf16[304,512]{1,0:T(8,128)(2,1)} custom-call(s32[1,4]{1,0:T(1,128)} %refs_0_.11, s32[1]{0:T(128)S(6)} %copy.14.count.refs_1_, bf16[512,128]{1,0:T(8,128)(2,1)} %bitcast.23, bf16[1536,1536]{1,0:T(8,128)(2,1)} %refs_7_.1), custom_call_target="tpu_custom_call" | custom-call | tf_op jit(solution)/shard_map/pallas_call | solution.py:429
  4.1 8.3 %collective-permute-start.3 = (bf16[304,512]{1,0:T(8,128)(2,1)}, bf16[304,512]{1,0:T(8,128)(2,1)S(1)}, u32[]{:S(2)}, u32[]{:S(2)}) collective-permute-start(bf16[304,512]{1,0:T(8,128)(2,1)} %shard_map.87), channel_id=1, source_target_pairs={{0,256},{4,260},{8,264},{12,268},{16,272},{20,276},{24,280},{28,28... | collective-permute-start | bytes 933896 | tf_op jit(solution)/shard_map/ppermute | solution.py:441
  12.4 4.3 %shard_map.86 = (f32[16,1536]{1,0:T(8,128)}, bf16[32,512]{1,0:T(8,128)(2,1)}, bf16[608,128]{1,0:T(8,128)(2,1)}, bf16[608,128]{1,0:T(8,128)(2,1)}) custom-call(f32[16,1536]{1,0:T(8,128)} %refs_2_.3, f32[16,1536]{1,0:T(8,128)} %refs_1_.6, bf16[1536,1536]{1,0:T(8,128)(2,1)} %refs_7_.1), custom_call_target="tpu_custom_call" | custom-call | tf_op jit(solution)/shard_map/pallas_call | solution.py:429
  16.7 2.9 %collective-permute-start.1 = (bf16[608,128]{1,0:T(8,128)(2,1)}, bf16[608,128]{1,0:T(8,128)(2,1)S(1)}, u32[]{:S(2)}, u32[]{:S(2)}) collective-permute-start(bf16[608,128]{1,0:T(8,128)(2,1)} %get-tuple-element.31), channel_id=1, source_target_pairs={{0,4},{4,0},{8,12},{12,8},{16,20},{20,16},{24,28},{28,24},{32,36},... | collective-permute-start | bytes 466952 | tf_op jit(solution)/shard_map/ppermute | solution.py:441
  19.5 3.9 %collective-permute-start.2 = (bf16[608,128]{1,0:T(8,128)(2,1)}, bf16[608,128]{1,0:T(8,128)(2,1)S(1)}, u32[]{:S(2)}, u32[]{:S(2)}) collective-permute-start(bf16[608,128]{1,0:T(8,128)(2,1)} %get-tuple-element.32), channel_id=1, source_target_pairs={{0,508},{4,8},{8,4},{12,16},{16,12},{20,24},{24,20},{28,32},{32,28... | collective-permute-start | bytes 466952 | tf_op jit(solution)/shard_map/ppermute | solution.py:441
  23.5 3.1 %collective-permute-start.7 = (bf16[160,512]{1,0:T(8,128)(2,1)S(1)}, bf16[160,512]{1,0:T(8,128)(2,1)S(1)}, u32[]{:S(2)}, u32[]{:S(2)}) collective-permute-start(bf16[160,512]{1,0:T(8,128)(2,1)S(1)} %slice.8), channel_id=1, source_target_pairs={{0,1},{1,0},{2,3},{3,2},{4,5},{5,4},{6,7},{7,6},{8,9},{9,8},{10,11... | collective-permute-start | bytes 491528 | tf_op jit(solution)/shard_map/ppermute | solution.py:459
  26.6 8.2 %collective-permute-start = (bf16[32,512]{1,0:T(8,128)(2,1)}, bf16[32,512]{1,0:T(8,128)(2,1)S(1)}, u32[]{:S(2)}, u32[]{:S(2)}) collective-permute-start(bf16[32,512]{1,0:T(8,128)(2,1)} %get-tuple-element.30), channel_id=1, source_target_pairs={{0,256},{4,260},{8,264},{12,268},{16,272},{20,276},{24,280},{28,28... | collective-permute-start | bytes 98312 | tf_op jit(solution)/shard_map/ppermute | solution.py:441
  37.2 4.4 %shard_map.88 = (f32[16,4608]{1,0:T(8,128)S(1)}, f32[16,2304]{1,0:T(8,128)S(1)}, f32[128,128]{1,0:T(8,128)}, f32[16,512]{1,0:T(8,128)S(1)}, f32[16,640]{1,0:T(8,128)S(1)}, /*index=5*/f32[16,640]{1,0:T(8,128)S(1)}) custom-call(s32[1,4]{1,0:T(1,128)S(1)} %copy-done.6, s32[1]{0:T(128)S(6)} %copy.14.count.refs_1_, f32[16,1536]{1,0:T(8,128)S(1)} %copy-done.3, ...), custom_call_target="tpu_custom_call" | custom-call | tf_op jit(solution)/shard_map/pallas_call | solution.py:429
  41.7 21.7 %all-to-all-start = ((f32[128,1,128]{2,1,0:T(1,128)}), f32[128,1,128]{2,1,0:T(1,128)S(1)}, u32[]{:S(2)}, u32[]{:S(2)}) async-start(f32[128,1,128]{2,1,0:T(1,128)} %bitcast.3), calls=%async_computation | async-start | bytes 131072 | tf_op jit(solution)/shard_map/all_to_all | solution.py:464
  63.4 2.8 %collective-permute-start.5 = (f32[16,640]{1,0:T(8,128)S(1)}, f32[16,640]{1,0:T(8,128)S(1)}, u32[]{:S(2)}, u32[]{:S(2)}) collective-permute-start(f32[16,640]{1,0:T(8,128)S(1)} %get-tuple-element.37), channel_id=1, source_target_pairs={{0,4},{4,0},{8,12},{12,8},{16,20},{20,16},{24,28},{28,24},{32,36},... | collective-permute-start | bytes 122888 | tf_op jit(solution)/shard_map/ppermute | solution.py:441
  66.2 2.8 %collective-permute-start.6 = (f32[16,640]{1,0:T(8,128)S(1)}, f32[16,640]{1,0:T(8,128)S(1)}, u32[]{:S(2)}, u32[]{:S(2)}) collective-permute-start(f32[16,640]{1,0:T(8,128)S(1)} %get-tuple-element.38), channel_id=1, source_target_pairs={{0,508},{4,8},{8,4},{12,16},{16,12},{20,24},{24,20},{28,32},{32,28... | collective-permute-start | bytes 122888 | tf_op jit(solution)/shard_map/ppermute | solution.py:441
  69.0 7.3 %collective-permute-start.4 = (f32[16,512]{1,0:T(8,128)S(1)}, f32[16,512]{1,0:T(8,128)S(1)}, u32[]{:S(2)}, u32[]{:S(2)}) collective-permute-start(f32[16,512]{1,0:T(8,128)S(1)} %get-tuple-element.36), channel_id=1, source_target_pairs={{0,256},{4,260},{8,264},{12,268},{16,272},{20,276},{24,280},{28,28... | collective-permute-start | bytes 98312 | tf_op jit(solution)/shard_map/ppermute | solution.py:441
  77.7 4.7 %shard_map.89 = (f32[16,4608]{1,0:T(8,128)S(1)}, f32[16,2304]{1,0:T(8,128)S(1)}, f32[128,128]{1,0:T(8,128)}, f32[16,512]{1,0:T(8,128)S(1)}, f32[16,640]{1,0:T(8,128)S(1)}, /*index=5*/f32[16,640]{1,0:T(8,128)S(1)}) custom-call(s32[1,4]{1,0:T(1,128)S(1)} %copy-done.6, s32[1]{0:T(128)S(6)} %copy.14.count.refs_1_, f32[128,128]{1,0:T(8,128)S(1)} %bitcast.29, ...), custom_call_target="tpu_custom_call" | custom-call | tf_op jit(solution)/shard_map/pallas_call | solution.py:429
  82.4 14.2 %all-to-all-start.1 = ((f32[128,1,128]{2,1,0:T(1,128)}), f32[128,1,128]{2,1,0:T(1,128)S(1)}, u32[]{:S(2)}, u32[]{:S(2)}) async-start(f32[128,1,128]{2,1,0:T(1,128)} %bitcast.6), calls=%async_computation.1 | async-start | bytes 131072 | tf_op jit(solution)/shard_map/all_to_all | solution.py:464
  96.6 2.8 %collective-permute-start.9 = (f32[16,640]{1,0:T(8,128)S(1)}, f32[16,640]{1,0:T(8,128)S(1)}, u32[]{:S(2)}, u32[]{:S(2)}) collective-permute-start(f32[16,640]{1,0:T(8,128)S(1)} %get-tuple-element.43), channel_id=1, source_target_pairs={{0,4},{4,0},{8,12},{12,8},{16,20},{20,16},{24,28},{28,24},{32,36},... | collective-permute-start | bytes 122888 | tf_op jit(solution)/shard_map/ppermute | solution.py:441
  102.2 7.3 %collective-permute-start.8 = (f32[16,512]{1,0:T(8,128)S(1)}, f32[16,512]{1,0:T(8,128)S(1)}, u32[]{:S(2)}, u32[]{:S(2)}) collective-permute-start(f32[16,512]{1,0:T(8,128)S(1)} %get-tuple-element.42), channel_id=1, source_target_pairs={{0,256},{4,260},{8,264},{12,268},{16,272},{20,276},{24,280},{28,28... | collective-permute-start | bytes 98312 | tf_op jit(solution)/shard_map/ppermute | solution.py:441
  110.9 4.7 %shard_map.90 = (f32[16,4608]{1,0:T(8,128)S(1)}, f32[16,2304]{1,0:T(8,128)S(1)}, f32[128,128]{1,0:T(8,128)}, f32[16,512]{1,0:T(8,128)S(1)}, f32[16,640]{1,0:T(8,128)S(1)}, /*index=5*/f32[16,640]{1,0:T(8,128)S(1)}) custom-call(s32[1,4]{1,0:T(1,128)S(1)} %copy-done.6, s32[1]{0:T(128)S(6)} %copy.14.count.refs_1_, f32[128,128]{1,0:T(8,128)S(1)} %bitcast.30, ...), custom_call_target="tpu_custom_call" | custom-call | tf_op jit(solution)/shard_map/pallas_call | solution.py:429
  115.6 14.1 %all-to-all-start.2 = ((f32[128,1,128]{2,1,0:T(1,128)}), f32[128,1,128]{2,1,0:T(1,128)S(1)}, u32[]{:S(2)}, u32[]{:S(2)}) async-start(f32[128,1,128]{2,1,0:T(1,128)} %bitcast.9), calls=%async_computation.2 | async-start | bytes 131072 | tf_op jit(solution)/shard_map/all_to_all | solution.py:464
  129.6 2.8 %collective-permute-start.12 = (f32[16,640]{1,0:T(8,128)S(1)}, f32[16,640]{1,0:T(8,128)S(1)}, u32[]{:S(2)}, u32[]{:S(2)}) collective-permute-start(f32[16,640]{1,0:T(8,128)S(1)} %get-tuple-element.49), channel_id=1, source_target_pairs={{0,4},{4,0},{8,12},{12,8},{16,20},{20,16},{24,28},{28,24},{32,36},... | collective-permute-start | bytes 122888 | tf_op jit(solution)/shard_map/ppermute | solution.py:441
  135.2 7.5 %collective-permute-start.11 = (f32[16,512]{1,0:T(8,128)S(1)}, f32[16,512]{1,0:T(8,128)S(1)}, u32[]{:S(2)}, u32[]{:S(2)}) collective-permute-start(f32[16,512]{1,0:T(8,128)S(1)} %get-tuple-element.48), channel_id=1, source_target_pairs={{0,256},{4,260},{8,264},{12,268},{16,272},{20,276},{24,280},{28,28... | collective-permute-start | bytes 98312 | tf_op jit(solution)/shard_map/ppermute | solution.py:441
  143.9 3.0 %shard_map.91 = (f32[16,3072]{1,0:T(8,128)S(1)}, f32[16,768]{1,0:T(8,128)S(1)}, f32[4,128]{1,0:T(4,128)}) custom-call(s32[1,4]{1,0:T(1,128)S(1)} %copy-done.6, s32[1]{0:T(128)S(6)} %copy.14.count.refs_1_, f32[128,128]{1,0:T(8,128)S(1)} %bitcast.31, f32[16,4608]{1,0:T(8,128)S(1)} %get-tuple-element.46.refs_3_, f32[16,2304]{1,0:T(8,128)S(1)} %get-tuple-element.47.refs_4_, ...), custom_call_target="tpu_custom_call" | custom-call | tf_op jit(solution)/shard_map/pallas_call | solution.py:429
  146.9 3.7 %all-to-all-start.3 = ((f32[4,1,128]{2,1,0:T(1,128)}), f32[4,1,128]{2,1,0:T(1,128)S(1)}, u32[]{:S(2)}, u32[]{:S(2)}) async-start(f32[4,1,128]{2,1,0:T(1,128)} %bitcast.12), calls=%async_computation.3 | async-start | bytes 4096 | tf_op jit(solution)/shard_map/all_to_all | solution.py:464
  150.7 3.4 %shard_map.92 = f32[128,128]{1,0:T(8,128)S(1)} custom-call(s32[1,4]{1,0:T(1,128)S(1)} %copy-done.6, s32[1]{0:T(128)S(6)} %copy.14.count.refs_1_, f32[16,3072]{1,0:T(8,128)S(1)} %get-tuple-element.51.refs_2_.own, f32[16,768]{1,0:T(8,128)S(1)} %get-tuple-element.52.refs_3_, bf16[512,128]{1,0:T(8,128)(2,1)S(1)} %bitcast.28, bf16[304,512]{1,0:T(8,128)(2,1)S(1)} %copy-done.1, ...), custom_call_target="tpu_custom_call" | custom-call | tf_op jit(solution)/shard_map/pallas_call | solution.py:429
  154.8 26.9 %all_to_all.25 = f32[128,1,128]{2,1,0:T(1,128)S(1)} all-to-all(f32[128,1,128]{2,1,0:T(1,128)S(1)} %bitcast.38), channel_id=1, replica_groups=mesh['sub'=128,'case'=4] {'sub'}, dimensions={0} | all-to-all | bytes 131072 | tf_op jit(solution)/shard_map/all_to_all | solution.py:464
  (39 shorter events, 13.2 us)
Async XLA Ops:
  1.3 35.0 %copy-start.2 = (bf16[1,4,128,128]{3,2,1,0:T(8,128)(2,1)S(1)}, bf16[1,4,128,128]{3,2,1,0:T(8,128)(2,1)}, u32[]{:S(2)}) copy-start(bf16[1,4,128,128]{3,2,1,0:T(8,128)(2,1)} %param.11) | copy-start | bytes 393220
  1.3 35.0 %copy-start.3 = (f32[16,1536]{1,0:T(8,128)S(1)}, f32[16,1536]{1,0:T(8,128)}, u32[]{:S(2)}) copy-start(f32[16,1536]{1,0:T(8,128)} %refs_2_.3) | copy-start | bytes 294916
  1.3 35.0 %copy-start.5 = (s32[1,2,128]{2,1,0:T(2,128)S(1)}, s32[1,2,128]{2,1,0:T(2,128)}, u32[]{:S(2)}) copy-start(s32[1,2,128]{2,1,0:T(2,128)} %param.10) | copy-start | bytes 3076
  1.3 35.0 %copy-start.6 = (s32[1,4]{1,0:T(1,128)S(1)}, s32[1,4]{1,0:T(1,128)}, u32[]{:S(2)}) copy-start(s32[1,4]{1,0:T(1,128)} %refs_0_.11) | copy-start | bytes 52
  4.1 19.3 %collective-permute-start.3 = (bf16[304,512]{1,0:T(8,128)(2,1)}, bf16[304,512]{1,0:T(8,128)(2,1)S(1)}, u32[]{:S(2)}, u32[]{:S(2)}) collective-permute-start(bf16[304,512]{1,0:T(8,128)(2,1)} %shard_map.87), channel_id=1, source_target_pairs={{0,256},{4,260},{8,264},{12,268},{16,272},{20,276},{24,280},{28,28... | collective-permute-start | bytes 933896 | tf_op jit(solution)/shard_map/ppermute | solution.py:441
  16.7 19.6 %collective-permute-start.1 = (bf16[608,128]{1,0:T(8,128)(2,1)}, bf16[608,128]{1,0:T(8,128)(2,1)S(1)}, u32[]{:S(2)}, u32[]{:S(2)}) collective-permute-start(bf16[608,128]{1,0:T(8,128)(2,1)} %get-tuple-element.31), channel_id=1, source_target_pairs={{0,4},{4,0},{8,12},{12,8},{16,20},{20,16},{24,28},{28,24},{32,36},... | collective-permute-start | bytes 466952 | tf_op jit(solution)/shard_map/ppermute | solution.py:441
  19.5 16.8 %collective-permute-start.2 = (bf16[608,128]{1,0:T(8,128)(2,1)}, bf16[608,128]{1,0:T(8,128)(2,1)S(1)}, u32[]{:S(2)}, u32[]{:S(2)}) collective-permute-start(bf16[608,128]{1,0:T(8,128)(2,1)} %get-tuple-element.32), channel_id=1, source_target_pairs={{0,508},{4,8},{8,4},{12,16},{16,12},{20,24},{24,20},{28,32},{32,28... | collective-permute-start | bytes 466952 | tf_op jit(solution)/shard_map/ppermute | solution.py:441
  23.5 54.2 %copy-start = (bf16[304,512]{1,0:T(8,128)(2,1)}, bf16[304,512]{1,0:T(8,128)(2,1)S(1)}, u32[]{:S(2)}) copy-start(bf16[304,512]{1,0:T(8,128)(2,1)S(1)} %collective-permute-done.3.refs_8_.refs_9_.refs_5_) | copy-start | bytes 933892
  23.5 54.2 %collective-permute-start.7 = (bf16[160,512]{1,0:T(8,128)(2,1)S(1)}, bf16[160,512]{1,0:T(8,128)(2,1)S(1)}, u32[]{:S(2)}, u32[]{:S(2)}) collective-permute-start(bf16[160,512]{1,0:T(8,128)(2,1)S(1)} %slice.8), channel_id=1, source_target_pairs={{0,1},{1,0},{2,3},{3,2},{4,5},{5,4},{6,7},{7,6},{8,9},{9,8},{10,11... | collective-permute-start | bytes 491528 | tf_op jit(solution)/shard_map/ppermute | solution.py:459
  26.6 9.7 %collective-permute-start = (bf16[32,512]{1,0:T(8,128)(2,1)}, bf16[32,512]{1,0:T(8,128)(2,1)S(1)}, u32[]{:S(2)}, u32[]{:S(2)}) collective-permute-start(bf16[32,512]{1,0:T(8,128)(2,1)} %get-tuple-element.30), channel_id=1, source_target_pairs={{0,256},{4,260},{8,264},{12,268},{16,272},{20,276},{24,280},{28,28... | collective-permute-start | bytes 98312 | tf_op jit(solution)/shard_map/ppermute | solution.py:441
  41.7 36.0 %all-to-all-start = ((f32[128,1,128]{2,1,0:T(1,128)}), f32[128,1,128]{2,1,0:T(1,128)S(1)}, u32[]{:S(2)}, u32[]{:S(2)}) async-start(f32[128,1,128]{2,1,0:T(1,128)} %bitcast.3), calls=%async_computation | async-start | bytes 131072 | tf_op jit(solution)/shard_map/all_to_all | solution.py:464
  63.4 14.2 %collective-permute-start.5 = (f32[16,640]{1,0:T(8,128)S(1)}, f32[16,640]{1,0:T(8,128)S(1)}, u32[]{:S(2)}, u32[]{:S(2)}) collective-permute-start(f32[16,640]{1,0:T(8,128)S(1)} %get-tuple-element.37), channel_id=1, source_target_pairs={{0,4},{4,0},{8,12},{12,8},{16,20},{20,16},{24,28},{28,24},{32,36},... | collective-permute-start | bytes 122888 | tf_op jit(solution)/shard_map/ppermute | solution.py:441
  66.2 11.4 %collective-permute-start.6 = (f32[16,640]{1,0:T(8,128)S(1)}, f32[16,640]{1,0:T(8,128)S(1)}, u32[]{:S(2)}, u32[]{:S(2)}) collective-permute-start(f32[16,640]{1,0:T(8,128)S(1)} %get-tuple-element.38), channel_id=1, source_target_pairs={{0,508},{4,8},{8,4},{12,16},{16,12},{20,24},{24,20},{28,32},{32,28... | collective-permute-start | bytes 122888 | tf_op jit(solution)/shard_map/ppermute | solution.py:441
  69.0 8.7 %collective-permute-start.4 = (f32[16,512]{1,0:T(8,128)S(1)}, f32[16,512]{1,0:T(8,128)S(1)}, u32[]{:S(2)}, u32[]{:S(2)}) collective-permute-start(f32[16,512]{1,0:T(8,128)S(1)} %get-tuple-element.36), channel_id=1, source_target_pairs={{0,256},{4,260},{8,264},{12,268},{16,272},{20,276},{24,280},{28,28... | collective-permute-start | bytes 98312 | tf_op jit(solution)/shard_map/ppermute | solution.py:441
  82.4 61.5 %copy-start.1 = (bf16[304,512]{1,0:T(8,128)(2,1)S(1)}, bf16[304,512]{1,0:T(8,128)(2,1)}, u32[]{:S(2)}) copy-start(bf16[304,512]{1,0:T(8,128)(2,1)} %copy-done) | copy-start | bytes 933892
  82.4 28.4 %all-to-all-start.1 = ((f32[128,1,128]{2,1,0:T(1,128)}), f32[128,1,128]{2,1,0:T(1,128)S(1)}, u32[]{:S(2)}, u32[]{:S(2)}) async-start(f32[128,1,128]{2,1,0:T(1,128)} %bitcast.6), calls=%async_computation.1 | async-start | bytes 131072 | tf_op jit(solution)/shard_map/all_to_all | solution.py:464
  96.6 14.2 %collective-permute-start.9 = (f32[16,640]{1,0:T(8,128)S(1)}, f32[16,640]{1,0:T(8,128)S(1)}, u32[]{:S(2)}, u32[]{:S(2)}) collective-permute-start(f32[16,640]{1,0:T(8,128)S(1)} %get-tuple-element.43), channel_id=1, source_target_pairs={{0,4},{4,0},{8,12},{12,8},{16,20},{20,16},{24,28},{28,24},{32,36},... | collective-permute-start | bytes 122888 | tf_op jit(solution)/shard_map/ppermute | solution.py:441
  99.4 11.4 %collective-permute-start.10 = (f32[16,640]{1,0:T(8,128)S(1)}, f32[16,640]{1,0:T(8,128)S(1)}, u32[]{:S(2)}, u32[]{:S(2)}) collective-permute-start(f32[16,640]{1,0:T(8,128)S(1)} %get-tuple-element.44), channel_id=1, source_target_pairs={{0,508},{4,8},{8,4},{12,16},{16,12},{20,24},{24,20},{28,32},{32,28... | collective-permute-start | bytes 122888 | tf_op jit(solution)/shard_map/ppermute | solution.py:441
  102.2 8.7 %collective-permute-start.8 = (f32[16,512]{1,0:T(8,128)S(1)}, f32[16,512]{1,0:T(8,128)S(1)}, u32[]{:S(2)}, u32[]{:S(2)}) collective-permute-start(f32[16,512]{1,0:T(8,128)S(1)} %get-tuple-element.42), channel_id=1, source_target_pairs={{0,256},{4,260},{8,264},{12,268},{16,272},{20,276},{24,280},{28,28... | collective-permute-start | bytes 98312 | tf_op jit(solution)/shard_map/ppermute | solution.py:441
  115.6 28.3 %all-to-all-start.2 = ((f32[128,1,128]{2,1,0:T(1,128)}), f32[128,1,128]{2,1,0:T(1,128)S(1)}, u32[]{:S(2)}, u32[]{:S(2)}) async-start(f32[128,1,128]{2,1,0:T(1,128)} %bitcast.9), calls=%async_computation.2 | async-start | bytes 131072 | tf_op jit(solution)/shard_map/all_to_all | solution.py:464
  129.6 14.2 %collective-permute-start.12 = (f32[16,640]{1,0:T(8,128)S(1)}, f32[16,640]{1,0:T(8,128)S(1)}, u32[]{:S(2)}, u32[]{:S(2)}) collective-permute-start(f32[16,640]{1,0:T(8,128)S(1)} %get-tuple-element.49), channel_id=1, source_target_pairs={{0,4},{4,0},{8,12},{12,8},{16,20},{20,16},{24,28},{28,24},{32,36},... | collective-permute-start | bytes 122888 | tf_op jit(solution)/shard_map/ppermute | solution.py:441
  132.5 11.4 %collective-permute-start.13 = (f32[16,640]{1,0:T(8,128)S(1)}, f32[16,640]{1,0:T(8,128)S(1)}, u32[]{:S(2)}, u32[]{:S(2)}) collective-permute-start(f32[16,640]{1,0:T(8,128)S(1)} %get-tuple-element.50), channel_id=1, source_target_pairs={{0,508},{4,8},{8,4},{12,16},{16,12},{20,24},{24,20},{28,32},{32,28... | collective-permute-start | bytes 122888 | tf_op jit(solution)/shard_map/ppermute | solution.py:441
  135.2 8.7 %collective-permute-start.11 = (f32[16,512]{1,0:T(8,128)S(1)}, f32[16,512]{1,0:T(8,128)S(1)}, u32[]{:S(2)}, u32[]{:S(2)}) collective-permute-start(f32[16,512]{1,0:T(8,128)S(1)} %get-tuple-element.48), channel_id=1, source_target_pairs={{0,256},{4,260},{8,264},{12,268},{16,272},{20,276},{24,280},{28,28... | collective-permute-start | bytes 98312 | tf_op jit(solution)/shard_map/ppermute | solution.py:441
  146.9 7.8 %all-to-all-start.3 = ((f32[4,1,128]{2,1,0:T(1,128)}), f32[4,1,128]{2,1,0:T(1,128)S(1)}, u32[]{:S(2)}, u32[]{:S(2)}) async-start(f32[4,1,128]{2,1,0:T(1,128)} %bitcast.12), calls=%async_computation.3 | async-start | bytes 4096 | tf_op jit(solution)/shard_map/all_to_all | solution.py:464
  (1 other events, 0.9 us)

commit v8 on v7

--- a/solution.py
+++ b/solution.py
@@ -212,12 +212,8 @@
     return piece
 
 
-TABLE = 0
-SLOTS = TABLE + CASES
-UPPER = SLOTS + BLK
 UNIT = BLK // 4
 HALF = 5 * UNIT
-PACKED = UPPER + HALF
 HALVES = (
     ((0, 0), (0, 1), (0, 2), (0, 3), (1, 1)),
     ((1, 2), (1, 3), (2, 2), (2, 3), (3, 3)),
@@ -246,7 +242,7 @@
             for half in HALVES:
                 row, lane = (BLK * place for place in half[n])
                 pair.append(block_ref[row + k * UNIT : row + (k + 1) * UNIT, lane : lane + BLK])
-            rows = slice(UPPER + n * UNIT, UPPER + (n + 1) * UNIT)
+            rows = slice(n * UNIT, (n + 1) * UNIT)
             packed[rows, k * BLK : (k + 1) * BLK] = jnp.where(odd, pair[1], pair[0])
 
 
@@ -268,27 +264,26 @@
     return jnp.concatenate(outs, axis=1)
 
 
-def pack_kernel(ids, count, mortar, dual_hbm, packed, block_ref, sem):
+def pack_kernel(dual_hbm, packed, block_ref, sem):
     contact = pl.ds(LOW, CONTACT)
     copy = pltpu.make_async_copy(dual_hbm.at[contact, contact], block_ref, sem)
     copy.start()
-    for k in range(4):
-        packed[SLOTS:UPPER, k * BLK : (k + 1) * BLK] = mortar[k * BLK : (k + 1) * BLK, :]
-    table = slot_table(ids, count).astype(bf16)
-    packed[TABLE:SLOTS, :] = jnp.concatenate([table] * 4, axis=1)
     copy.wait()
     store_half(packed, block_ref)
 
 
 def prepare_kernel(*refs):
-    x_ref, right_ref, dual_hbm, q_ref, first_ref, near_ref, far_ref, dual_ref, sems = refs
+    ids, count, x_ref, right_ref, dual_hbm = refs[:5]
+    q_ref, first_ref, near_ref, far_ref, dual_ref, sems = refs[5:]
     piece = whole_copy(dual_hbm, dual_ref, sems)
     even = is_even()
     x = x_ref[...]
     q = whole_dot(x, [piece(k, True) for k in range(len(STARTS))]) - right_ref[...]
     q_ref[...] = q
     first_ref[:CASES, :] = x[:, LOW:HIGH].astype(bf16)
-    first_ref[CASES:, :] = q[:, LOW:HIGH].astype(bf16)
+    first_ref[CASES : 2 * CASES, :] = q[:, LOW:HIGH].astype(bf16)
+    table = slot_table(ids, count).astype(bf16)
+    first_ref[2 * CASES :, :] = jnp.concatenate([table] * 4, axis=1)
     contacts = split(x[:, LOW:HIGH])
     both = [(near_ref,), (far_ref,)]
     for (ref,), face, grad in zip(both, faces_of(x, even), faces_of(q, even)):
@@ -299,10 +294,11 @@
     far_ref[SIDE:, :] = chosen(even, first, second)
 
 
-def statics_of(ids, count, mortar, packed):
-    own = [mortar[k * BLK : (k + 1) * BLK, :] for k in range(4)]
-    mate = [packed[SLOTS:UPPER, k * BLK : (k + 1) * BLK] for k in range(4)]
-    mate_table = packed[TABLE:SLOTS, :BLK].astype(f32)
+def statics_of(ids, count, mortar, mate_mortar, first):
+    own, mate = [
+        [ref[k * BLK : (k + 1) * BLK, :] for k in range(4)] for ref in (mortar, mate_mortar)
+    ]
+    mate_table = first[2 * CASES :, :BLK].astype(f32)
     return slots(slot_table(ids, count)), own, slots(mate_table), mate
 
 
@@ -326,14 +322,14 @@
 
 
 def begin_kernel(*refs):
-    ids, count, x_ref, q_ref, first, near, far, mortar, packed, match, dual_hbm = refs[:11]
+    ids, count, x_ref, q_ref, first, near, far, mortar, mate_mortar, match, dual_hbm = refs[:11]
     outs, (dual_ref, sems) = refs[11:17], refs[17:]
     piece = whole_copy(dual_hbm, dual_ref, sems)
     even = is_even()
-    statics = statics_of(ids, count, mortar, packed)
+    statics = statics_of(ids, count, mortar, mate_mortar, first)
     pick = picks(match[...], even)
     x = x_ref[...]
-    mate = first[:CASES, :].astype(f32), first[CASES:, :].astype(f32)
+    mate = first[:CASES, :].astype(f32), first[CASES : 2 * CASES, :].astype(f32)
     sides = side_values(near), side_values(far)
     g, others = begin(x, q_ref[...], mate, *sides, statics, pick, even)
     pieces = [piece(k, True) for k in range(len(STARTS))]
@@ -345,10 +341,10 @@
 
 
 def advanced(refs, piece):
-    ids, count, sums, own, others, mate, near, far, mortar, packed, _ = refs[:11]
-    near_kernel, far_kernel, other_half = refs[11:14]
-    mate_kernel = packed[UPPER:, :], other_half[...]
-    statics = statics_of(ids, count, mortar, packed)
+    ids, count, sums, own, others, mate, near, far, mortar, mate_mortar, _ = refs[:11]
+    first, near_kernel, far_kernel, half, other_half = refs[11:16]
+    mate_kernel = half[...], other_half[...]
+    statics = statics_of(ids, count, mortar, mate_mortar, first)
     offsets = [sum(WIDTHS[:k]) for k in range(len(WIDTHS))]
     lift_rows = [(k * CHUNK, CHUNK, piece(k, True)[2]) for k in range(2)]
     x, g, others = advance(
@@ -366,10 +362,10 @@
 
 
 def advance_kernel(*refs):
-    dual_hbm, outs, (dual_ref, sems) = refs[14], refs[15:21], refs[21:]
+    dual_hbm, outs, (dual_ref, sems) = refs[16], refs[17:23], refs[23:]
     piece = whole_copy(dual_hbm, dual_ref, sems)
     even = is_even()
-    x, g, others, statics = advanced(refs[:14], piece)
+    x, g, others, statics = advanced(refs[:16], piece)
     pick = picks(refs[10][...], even)
     pieces = [piece(k, k >= 2) for k in range(len(STARTS))]
     image, row = tail(g, others, statics, pick, even, pieces)
@@ -377,9 +373,9 @@
 
 
 def last_advance_kernel(*refs):
-    dual_hbm, (own_out, others_out, row_out), (dual_ref, sems) = refs[14], refs[15:18], refs[18:]
+    dual_hbm, (own_out, others_out, row_out), (dual_ref, sems) = refs[16], refs[17:20], refs[20:]
     piece = whole_copy(dual_hbm, dual_ref, sems, STARTS[:2])
-    x, g, others, _ = advanced(refs[:14], piece)
+    x, g, others, _ = advanced(refs[:16], piece)
     own_out[:, :M] = x
     own_out[:, M:] = g
     others_out[...] = jnp.concatenate([others[1], others[4], others[5]], axis=1)
@@ -388,11 +384,11 @@
 
 
 def last_tail_kernel(*refs):
-    ids, count, own, others, mortar, packed, match, dual_hbm = refs[:8]
-    row_out, dual_ref, sems = refs[8:]
+    ids, count, own, others, mortar, mate_mortar, match, first, dual_hbm = refs[:9]
+    row_out, dual_ref, sems = refs[9:]
     piece = whole_copy(dual_hbm, dual_ref, sems)
     even = is_even()
-    statics = statics_of(ids, count, mortar, packed)
+    statics = statics_of(ids, count, mortar, mate_mortar, first)
     pick = picks(match[...], even)
     others = [
         None,
@@ -425,7 +421,7 @@
 BLOCK = [pltpu.VMEM((CONTACT, CONTACT), bf16), pltpu.SemaphoreType.DMA]
 
 
-def call(kernel, specs, shapes, operands, scratch=WHOLE, grant=52):
+def call(kernel, specs, shapes, operands, scratch=WHOLE, grant=50):
     return pl.pallas_call(
         kernel,
         in_specs=specs,
@@ -471,30 +467,25 @@
     match = glue_match[0]
     scalars = [SMEM_SPEC, SMEM_SPEC]
 
-    (packed,) = call(
-        pack_kernel,
-        scalars + [VMEM_SPEC, HBM_SPEC],
-        [((PACKED, CONTACT), bf16)],
-        (contact_ids, contact_count, mortar, dual_ops),
-        scratch=BLOCK,
-        grant=PREPARE_GRANT,
-    )
-    packed = with_mate(packed)
+    mate_mortar = with_mate(mortar)
     q, first, to_near, to_far = call(
         prepare_kernel,
-        [VMEM_SPEC] * 2 + [HBM_SPEC],
+        scalars + [VMEM_SPEC] * 2 + [HBM_SPEC],
         [
             ((CASES, M), f32),
-            ((2 * CASES, CONTACT), bf16),
+            ((3 * CASES, CONTACT), bf16),
             ((SIDE + CONTACT, BLK), bf16),
             ((SIDE + CONTACT, BLK), bf16),
         ],
-        (multipliers, right_side, dual_ops),
+        (contact_ids, contact_count, multipliers, right_side, dual_ops),
         grant=PREPARE_GRANT,
     )
+    first, dual_later = lax.optimization_barrier((first, dual_ops))
     first = with_mate(first)
     near = near_kernel = with_near(to_near)
     far = far_kernel = with_far(to_far)
+    (half,) = call(pack_kernel, [HBM_SPEC], [((HALF, CONTACT), bf16)], (dual_later,), scratch=BLOCK)
+    half = with_mate(half)
 
     shapes = [
         ((CASES, 3 * M), f32),
@@ -509,7 +500,7 @@
         scalars + [VMEM_SPEC] * 8 + [HBM_SPEC],
         shapes,
         (
-            contact_ids, contact_count, multipliers, q, first, near, far, mortar, packed,
+            contact_ids, contact_count, multipliers, q, first, near, far, mortar, mate_mortar,
             match, dual_ops,
         ),
     )
@@ -519,22 +510,22 @@
         far = with_far(to_far)
         near = with_near(to_near)
         if iteration == 1:
-            other_half = with_case(packed[UPPER:], 1)
+            other_half = with_case(half, 1)
         operands = (
-            contact_ids, contact_count, sums, own, others, mate, near, far, mortar, packed,
-            match, near_kernel, far_kernel, other_half, dual_ops,
+            contact_ids, contact_count, sums, own, others, mate, near, far, mortar,
+            mate_mortar, match, first, near_kernel, far_kernel, half, other_half, dual_ops,
         )
         if iteration < ITERS - 1:
             own, others, copies, to_mate, to_near, to_far = call(
                 advance_kernel,
-                scalars + [VMEM_SPEC] * 12 + [HBM_SPEC],
+                scalars + [VMEM_SPEC] * 14 + [HBM_SPEC],
                 shapes,
                 operands,
             )
     cases = lax.axis_size("case")
     own, others, norms = call(
         last_advance_kernel,
-        scalars + [VMEM_SPEC] * 12 + [HBM_SPEC],
+        scalars + [VMEM_SPEC] * 14 + [HBM_SPEC],
         [
             ((CASES, 2 * M), f32),
             ((CASES, CONTACT + 2 * BLK), f32),
@@ -545,9 +536,12 @@
     norms = spread_sums(norms, "case")
     (copies,) = call(
         last_tail_kernel,
-        scalars + [VMEM_SPEC] * 5 + [HBM_SPEC],
+        scalars + [VMEM_SPEC] * 6 + [HBM_SPEC],
         [((devices, BLK), f32)],
-        (contact_ids, contact_count, own, others, mortar, packed, match, dual_ops),
+        (
+            contact_ids, contact_count, own, others, mortar, mate_mortar, match, first,
+            dual_ops,
+        ),
     )
     lane = lax.broadcasted_iota(jnp.int32, (1, BLK), 1)
     norm_row = jnp.where(lane == 2 * CASES, jnp.sum(norms, axis=0, keepdims=True), 0.0)

time: 183 us -> 176 us (0.962)
  starting transfers between devices: 119 us -> 114 us
    all_to_all x4, starting transfers between devices: 53.7 us -> 48.2 us  [spread_sums(): rows = lax.all_to_all(copies.reshape(devices, 1, BLK), axis, 0, 0)]
    ppermute x13 -> x14, starting transfers between devices: 62.1 us -> 63.1 us  [swapped(): lax.ppermute(value, 'sub', [(i, other(i) % devices) for i in range(device...]
    ppermute x13 -> x14, waiting for transfers between devices: 5.29 us -> 5.32 us  [swapped(): lax.ppermute(value, 'sub', [(i, other(i) % devices) for i in range(device...]
  transfers between devices with their start and end apart: 18 -> 19, of which waited for: 5 -> 5; matrix products, arithmetic and copies ran while one was open for 0% -> 0% of each run, Pallas kernels for 7% -> 4%
where the time goes in v8:
time: 176 us
  starting transfers between devices  114 us (65%)
  blocking collectives  26.9 us (15%)
  Pallas kernels  26.6 us (15%)
  waiting for transfers between devices  5.99 us (3%)
    ppermute x14, starting transfers between devices, swapped(): lax.ppermute(value, 'sub', [(i, other(i) % devices) for i in range(device...  63.1 us
    all_to_all x4, starting transfers between devices, spread_sums(): rows = lax.all_to_all(copies.reshape(devices, 1, BLK), axis, 0, 0)  48.2 us
    all_to_all x1, blocking collectives, spread_sums(): rows = lax.all_to_all(copies.reshape(devices, 1, BLK), axis, 0, 0)  26.9 us
    pallas_call x8, Pallas kernels, call(): pl.pallas_call(kernel, in_specs=specs, out_specs=[VMEM_SPEC] * len(shapes...  26.6 us
    ppermute x14, waiting for transfers between devices, swapped(): lax.ppermute(value, 'sub', [(i, other(i) % devices) for i in range(device...  5.32 us
  transfers between devices with their start and end apart: 19, of which 5 were waited for; matrix products, arithmetic and copies ran while one was open for 0% of the time, Pallas kernels for 4%

profile of v8, /device:TPU:1, one launch (start us, length us, event | category | flops | bytes accessed | tf_op | source)
XLA Modules:
  0.0 175.6 jit_solution(15336173329416012139)
XLA Ops:
  1.3 4.4 %shard_map.86 = (f32[16,1536]{1,0:T(8,128)}, bf16[48,512]{1,0:T(8,128)(2,1)}, bf16[608,128]{1,0:T(8,128)(2,1)}, bf16[608,128]{1,0:T(8,128)(2,1)}) custom-call(s32[1,4]{1,0:T(1,128)} %refs_0_.11, s32[1]{0:T(128)S(6)} %copy.14.refs_1_, f32[16,1536]{1,0:T(8,128)} %refs_2_.3, f32[16,1536]{1,0:T(8,128)} %refs_3_.1, bf16[1536,1536]{1,0:T(8,128)(2,1)} %refs_8_.1), custom_call_target="tpu_custom_call" | custom-call | tf_op jit(solution)/shard_map/pallas_call | solution.py:425
  6.9 8.3 %collective-permute-start.7 = (bf16[160,512]{1,0:T(8,128)(2,1)S(1)}, bf16[160,512]{1,0:T(8,128)(2,1)S(1)}, u32[]{:S(2)}, u32[]{:S(2)}) collective-permute-start(bf16[160,512]{1,0:T(8,128)(2,1)S(1)} %shard_map.88), channel_id=1, source_target_pairs={{0,256},{4,260},{8,264},{12,268},{16,272},{20,276},{24,280},{28,28... | collective-permute-start | bytes 491528 | tf_op jit(solution)/shard_map/ppermute | solution.py:437
  15.2 2.9 %collective-permute-start.1 = (bf16[608,128]{1,0:T(8,128)(2,1)S(1)}, bf16[608,128]{1,0:T(8,128)(2,1)S(1)}, u32[]{:S(2)}, u32[]{:S(2)}) collective-permute-start(bf16[608,128]{1,0:T(8,128)(2,1)S(1)} %copy-done.6), channel_id=1, source_target_pairs={{0,4},{4,0},{8,12},{12,8},{16,20},{20,16},{24,28},{28,24},{32,36},... | collective-permute-start | bytes 466952 | tf_op jit(solution)/shard_map/ppermute | solution.py:437
  18.1 3.9 %collective-permute-start.2 = (bf16[608,128]{1,0:T(8,128)(2,1)S(1)}, bf16[608,128]{1,0:T(8,128)(2,1)S(1)}, u32[]{:S(2)}, u32[]{:S(2)}) collective-permute-start(bf16[608,128]{1,0:T(8,128)(2,1)S(1)} %copy-done.5), channel_id=1, source_target_pairs={{0,508},{4,8},{8,4},{12,16},{16,12},{20,24},{24,20},{28,32},{32,28... | collective-permute-start | bytes 466952 | tf_op jit(solution)/shard_map/ppermute | solution.py:437
  22.0 5.1 %collective-permute-start.3 = (bf16[512,128]{1,0:T(8,128)(2,1)S(1)}, bf16[512,128]{1,0:T(8,128)(2,1)S(1)}, u32[]{:S(2)}, u32[]{:S(2)}) collective-permute-start(bf16[512,128]{1,0:T(8,128)(2,1)S(1)} %bitcast.23), channel_id=1, source_target_pairs={{0,256},{4,260},{8,264},{12,268},{16,272},{20,276},{24,280},{28,28... | collective-permute-start | bytes 393224 | tf_op jit(solution)/shard_map/ppermute | solution.py:437
  27.1 4.1 %collective-permute-start = (bf16[48,512]{1,0:T(8,128)(2,1)S(1)}, bf16[48,512]{1,0:T(8,128)(2,1)S(1)}, u32[]{:S(2)}, u32[]{:S(2)}) collective-permute-start(bf16[48,512]{1,0:T(8,128)(2,1)S(1)} %copy-done.7), channel_id=1, source_target_pairs={{0,256},{4,260},{8,264},{12,268},{16,272},{20,276},{24,280},{28,28... | collective-permute-start | bytes 147464 | tf_op jit(solution)/shard_map/ppermute | solution.py:437
  31.2 3.1 %collective-permute-start.8 = (bf16[160,512]{1,0:T(8,128)(2,1)S(1)}, bf16[160,512]{1,0:T(8,128)(2,1)S(1)}, u32[]{:S(2)}, u32[]{:S(2)}) collective-permute-start(bf16[160,512]{1,0:T(8,128)(2,1)S(1)} %collective-permute-done.7.refs_14_), channel_id=1, source_target_pairs={{0,1},{1,0},{2,3},{3,2},{4,5},{5,4},{6,7},{7,6},{8,9},{9,8},{10,11... | collective-permute-start | bytes 491528 | tf_op jit(solution)/shard_map/ppermute | solution.py:455
  35.9 4.4 %shard_map.87 = (f32[16,4608]{1,0:T(8,128)S(1)}, f32[16,2304]{1,0:T(8,128)S(1)}, f32[128,128]{1,0:T(8,128)}, f32[16,512]{1,0:T(8,128)S(1)}, f32[16,640]{1,0:T(8,128)S(1)}, /*index=5*/f32[16,640]{1,0:T(8,128)S(1)}) custom-call(s32[1,4]{1,0:T(1,128)S(1)} %copy-done.4, s32[1]{0:T(128)S(6)} %copy.14.refs_1_, f32[16,1536]{1,0:T(8,128)S(1)} %copy-done.1, ...), custom_call_target="tpu_custom_call" | custom-call | tf_op jit(solution)/shard_map/pallas_call | solution.py:425
  40.4 16.0 %all-to-all-start = ((f32[128,1,128]{2,1,0:T(1,128)}), f32[128,1,128]{2,1,0:T(1,128)S(1)}, u32[]{:S(2)}, u32[]{:S(2)}) async-start(f32[128,1,128]{2,1,0:T(1,128)} %bitcast.3), calls=%async_computation | async-start | bytes 131072 | tf_op jit(solution)/shard_map/all_to_all | solution.py:460
  56.4 2.8 %collective-permute-start.5 = (f32[16,640]{1,0:T(8,128)S(1)}, f32[16,640]{1,0:T(8,128)S(1)}, u32[]{:S(2)}, u32[]{:S(2)}) collective-permute-start(f32[16,640]{1,0:T(8,128)S(1)} %get-tuple-element.40), channel_id=1, source_target_pairs={{0,4},{4,0},{8,12},{12,8},{16,20},{20,16},{24,28},{28,24},{32,36},... | collective-permute-start | bytes 122888 | tf_op jit(solution)/shard_map/ppermute | solution.py:437
  59.2 2.8 %collective-permute-start.6 = (f32[16,640]{1,0:T(8,128)S(1)}, f32[16,640]{1,0:T(8,128)S(1)}, u32[]{:S(2)}, u32[]{:S(2)}) collective-permute-start(f32[16,640]{1,0:T(8,128)S(1)} %get-tuple-element.41), channel_id=1, source_target_pairs={{0,508},{4,8},{8,4},{12,16},{16,12},{20,24},{24,20},{28,32},{32,28... | collective-permute-start | bytes 122888 | tf_op jit(solution)/shard_map/ppermute | solution.py:437
  62.0 7.3 %collective-permute-start.4 = (f32[16,512]{1,0:T(8,128)S(1)}, f32[16,512]{1,0:T(8,128)S(1)}, u32[]{:S(2)}, u32[]{:S(2)}) collective-permute-start(f32[16,512]{1,0:T(8,128)S(1)} %get-tuple-element.39), channel_id=1, source_target_pairs={{0,256},{4,260},{8,264},{12,268},{16,272},{20,276},{24,280},{28,28... | collective-permute-start | bytes 98312 | tf_op jit(solution)/shard_map/ppermute | solution.py:437
  70.7 4.7 %shard_map.89 = (f32[16,4608]{1,0:T(8,128)S(1)}, f32[16,2304]{1,0:T(8,128)S(1)}, f32[128,128]{1,0:T(8,128)}, f32[16,512]{1,0:T(8,128)S(1)}, f32[16,640]{1,0:T(8,128)S(1)}, /*index=5*/f32[16,640]{1,0:T(8,128)S(1)}) custom-call(s32[1,4]{1,0:T(1,128)S(1)} %copy-done.4, s32[1]{0:T(128)S(6)} %copy.14.refs_1_, f32[128,128]{1,0:T(8,128)S(1)} %bitcast.29, ...), custom_call_target="tpu_custom_call" | custom-call | tf_op jit(solution)/shard_map/pallas_call | solution.py:425
  75.4 14.1 %all-to-all-start.1 = ((f32[128,1,128]{2,1,0:T(1,128)}), f32[128,1,128]{2,1,0:T(1,128)S(1)}, u32[]{:S(2)}, u32[]{:S(2)}) async-start(f32[128,1,128]{2,1,0:T(1,128)} %bitcast.6), calls=%async_computation.1 | async-start | bytes 131072 | tf_op jit(solution)/shard_map/all_to_all | solution.py:460
  89.5 2.8 %collective-permute-start.10 = (f32[16,640]{1,0:T(8,128)S(1)}, f32[16,640]{1,0:T(8,128)S(1)}, u32[]{:S(2)}, u32[]{:S(2)}) collective-permute-start(f32[16,640]{1,0:T(8,128)S(1)} %get-tuple-element.47), channel_id=1, source_target_pairs={{0,4},{4,0},{8,12},{12,8},{16,20},{20,16},{24,28},{28,24},{32,36},... | collective-permute-start | bytes 122888 | tf_op jit(solution)/shard_map/ppermute | solution.py:437
  95.1 7.3 %collective-permute-start.9 = (f32[16,512]{1,0:T(8,128)S(1)}, f32[16,512]{1,0:T(8,128)S(1)}, u32[]{:S(2)}, u32[]{:S(2)}) collective-permute-start(f32[16,512]{1,0:T(8,128)S(1)} %get-tuple-element.46), channel_id=1, source_target_pairs={{0,256},{4,260},{8,264},{12,268},{16,272},{20,276},{24,280},{28,28... | collective-permute-start | bytes 98312 | tf_op jit(solution)/shard_map/ppermute | solution.py:437
  103.7 4.7 %shard_map.90 = (f32[16,4608]{1,0:T(8,128)S(1)}, f32[16,2304]{1,0:T(8,128)S(1)}, f32[128,128]{1,0:T(8,128)}, f32[16,512]{1,0:T(8,128)S(1)}, f32[16,640]{1,0:T(8,128)S(1)}, /*index=5*/f32[16,640]{1,0:T(8,128)S(1)}) custom-call(s32[1,4]{1,0:T(1,128)S(1)} %copy-done.4, s32[1]{0:T(128)S(6)} %copy.14.refs_1_, f32[128,128]{1,0:T(8,128)S(1)} %bitcast.31, ...), custom_call_target="tpu_custom_call" | custom-call | tf_op jit(solution)/shard_map/pallas_call | solution.py:425
  108.5 14.1 %all-to-all-start.2 = ((f32[128,1,128]{2,1,0:T(1,128)}), f32[128,1,128]{2,1,0:T(1,128)S(1)}, u32[]{:S(2)}, u32[]{:S(2)}) async-start(f32[128,1,128]{2,1,0:T(1,128)} %bitcast.9), calls=%async_computation.2 | async-start | bytes 131072 | tf_op jit(solution)/shard_map/all_to_all | solution.py:460
  122.5 2.8 %collective-permute-start.13 = (f32[16,640]{1,0:T(8,128)S(1)}, f32[16,640]{1,0:T(8,128)S(1)}, u32[]{:S(2)}, u32[]{:S(2)}) collective-permute-start(f32[16,640]{1,0:T(8,128)S(1)} %get-tuple-element.53), channel_id=1, source_target_pairs={{0,4},{4,0},{8,12},{12,8},{16,20},{20,16},{24,28},{28,24},{32,36},... | collective-permute-start | bytes 122888 | tf_op jit(solution)/shard_map/ppermute | solution.py:437
  128.1 7.5 %collective-permute-start.12 = (f32[16,512]{1,0:T(8,128)S(1)}, f32[16,512]{1,0:T(8,128)S(1)}, u32[]{:S(2)}, u32[]{:S(2)}) collective-permute-start(f32[16,512]{1,0:T(8,128)S(1)} %get-tuple-element.52), channel_id=1, source_target_pairs={{0,256},{4,260},{8,264},{12,268},{16,272},{20,276},{24,280},{28,28... | collective-permute-start | bytes 98312 | tf_op jit(solution)/shard_map/ppermute | solution.py:437
  136.8 3.0 %shard_map.91 = (f32[16,3072]{1,0:T(8,128)S(1)}, f32[16,768]{1,0:T(8,128)S(1)}, f32[4,128]{1,0:T(4,128)}) custom-call(s32[1,4]{1,0:T(1,128)S(1)} %copy-done.4, s32[1]{0:T(128)S(6)} %copy.14.refs_1_, f32[128,128]{1,0:T(8,128)S(1)} %bitcast.30, f32[16,4608]{1,0:T(8,128)S(1)} %get-tuple-element.50.refs_3_, f32[16,2304]{1,0:T(8,128)S(1)} %get-tuple-element.51.refs_4_, ...), custom_call_target="tpu_custom_call" | custom-call | tf_op jit(solution)/shard_map/pallas_call | solution.py:425
  139.8 4.0 %all-to-all-start.3 = ((f32[4,1,128]{2,1,0:T(1,128)}), f32[4,1,128]{2,1,0:T(1,128)S(1)}, u32[]{:S(2)}, u32[]{:S(2)}) async-start(f32[4,1,128]{2,1,0:T(1,128)} %bitcast.12), calls=%async_computation.3 | async-start | bytes 4096 | tf_op jit(solution)/shard_map/all_to_all | solution.py:460
  143.9 3.4 %shard_map.92 = f32[128,128]{1,0:T(8,128)S(1)} custom-call(s32[1,4]{1,0:T(1,128)S(1)} %copy-done.4, s32[1]{0:T(128)S(6)} %copy.14.refs_1_, f32[16,3072]{1,0:T(8,128)S(1)} %get-tuple-element.55.refs_2_.own, f32[16,768]{1,0:T(8,128)S(1)} %get-tuple-element.56.refs_3_, bf16[512,128]{1,0:T(8,128)(2,1)S(1)} %bitcast.28, ...), custom_call_target="tpu_custom_call" | custom-call | tf_op jit(solution)/shard_map/pallas_call | solution.py:425
  148.0 26.9 %all_to_all.25 = f32[128,1,128]{2,1,0:T(1,128)S(1)} all-to-all(f32[128,1,128]{2,1,0:T(1,128)S(1)} %bitcast.38), channel_id=1, replica_groups=mesh['sub'=128,'case'=4] {'sub'}, dimensions={0} | all-to-all | bytes 131072 | tf_op jit(solution)/shard_map/all_to_all | solution.py:460
  (42 shorter events, 13.5 us)
Async XLA Ops:
  1.3 34.6 %copy-start.1 = (f32[16,1536]{1,0:T(8,128)S(1)}, f32[16,1536]{1,0:T(8,128)}, u32[]{:S(2)}) copy-start(f32[16,1536]{1,0:T(8,128)} %refs_2_.3) | copy-start | bytes 294916
  1.3 34.6 %copy-start.3 = (s32[1,2,128]{2,1,0:T(2,128)S(1)}, s32[1,2,128]{2,1,0:T(2,128)}, u32[]{:S(2)}) copy-start(s32[1,2,128]{2,1,0:T(2,128)} %param.10) | copy-start | bytes 3076
  1.3 34.6 %copy-start.4 = (s32[1,4]{1,0:T(1,128)S(1)}, s32[1,4]{1,0:T(1,128)}, u32[]{:S(2)}) copy-start(s32[1,4]{1,0:T(1,128)} %refs_0_.11) | copy-start | bytes 52
  5.7 21.4 %copy-start.7 = (bf16[48,512]{1,0:T(8,128)(2,1)S(1)}, bf16[48,512]{1,0:T(8,128)(2,1)}, u32[]{:S(2)}) copy-start(bf16[48,512]{1,0:T(8,128)(2,1)} %get-tuple-element.33) | copy-start | bytes 147460
  5.7 30.2 %copy-start.2 = (f32[16,1536]{1,0:T(8,128)S(1)}, f32[16,1536]{1,0:T(8,128)}, u32[]{:S(2)}) copy-start(f32[16,1536]{1,0:T(8,128)} %get-tuple-element.31.refs_3_) | copy-start | bytes 294916
  6.9 24.3 %collective-permute-start.7 = (bf16[160,512]{1,0:T(8,128)(2,1)S(1)}, bf16[160,512]{1,0:T(8,128)(2,1)S(1)}, u32[]{:S(2)}, u32[]{:S(2)}) collective-permute-start(bf16[160,512]{1,0:T(8,128)(2,1)S(1)} %shard_map.88), channel_id=1, source_target_pairs={{0,256},{4,260},{8,264},{12,268},{16,272},{20,276},{24,280},{28,28... | collective-permute-start | bytes 491528 | tf_op jit(solution)/shard_map/ppermute | solution.py:437
  15.2 20.7 %collective-permute-start.1 = (bf16[608,128]{1,0:T(8,128)(2,1)S(1)}, bf16[608,128]{1,0:T(8,128)(2,1)S(1)}, u32[]{:S(2)}, u32[]{:S(2)}) collective-permute-start(bf16[608,128]{1,0:T(8,128)(2,1)S(1)} %copy-done.6), channel_id=1, source_target_pairs={{0,4},{4,0},{8,12},{12,8},{16,20},{20,16},{24,28},{28,24},{32,36},... | collective-permute-start | bytes 466952 | tf_op jit(solution)/shard_map/ppermute | solution.py:437
  18.1 17.8 %collective-permute-start.2 = (bf16[608,128]{1,0:T(8,128)(2,1)S(1)}, bf16[608,128]{1,0:T(8,128)(2,1)S(1)}, u32[]{:S(2)}, u32[]{:S(2)}) collective-permute-start(bf16[608,128]{1,0:T(8,128)(2,1)S(1)} %copy-done.5), channel_id=1, source_target_pairs={{0,508},{4,8},{8,4},{12,16},{16,12},{20,24},{24,20},{28,32},{32,28... | collective-permute-start | bytes 466952 | tf_op jit(solution)/shard_map/ppermute | solution.py:437
  22.0 13.9 %collective-permute-start.3 = (bf16[512,128]{1,0:T(8,128)(2,1)S(1)}, bf16[512,128]{1,0:T(8,128)(2,1)S(1)}, u32[]{:S(2)}, u32[]{:S(2)}) collective-permute-start(bf16[512,128]{1,0:T(8,128)(2,1)S(1)} %bitcast.23), channel_id=1, source_target_pairs={{0,256},{4,260},{8,264},{12,268},{16,272},{20,276},{24,280},{28,28... | collective-permute-start | bytes 393224 | tf_op jit(solution)/shard_map/ppermute | solution.py:437
  27.1 8.8 %collective-permute-start = (bf16[48,512]{1,0:T(8,128)(2,1)S(1)}, bf16[48,512]{1,0:T(8,128)(2,1)S(1)}, u32[]{:S(2)}, u32[]{:S(2)}) collective-permute-start(bf16[48,512]{1,0:T(8,128)(2,1)S(1)} %copy-done.7), channel_id=1, source_target_pairs={{0,256},{4,260},{8,264},{12,268},{16,272},{20,276},{24,280},{28,28... | collective-permute-start | bytes 147464 | tf_op jit(solution)/shard_map/ppermute | solution.py:437
  31.2 39.5 %collective-permute-start.8 = (bf16[160,512]{1,0:T(8,128)(2,1)S(1)}, bf16[160,512]{1,0:T(8,128)(2,1)S(1)}, u32[]{:S(2)}, u32[]{:S(2)}) collective-permute-start(bf16[160,512]{1,0:T(8,128)(2,1)S(1)} %collective-permute-done.7.refs_14_), channel_id=1, source_target_pairs={{0,1},{1,0},{2,3},{3,2},{4,5},{5,4},{6,7},{7,6},{8,9},{9,8},{10,11... | collective-permute-start | bytes 491528 | tf_op jit(solution)/shard_map/ppermute | solution.py:455
  40.4 30.3 %all-to-all-start = ((f32[128,1,128]{2,1,0:T(1,128)}), f32[128,1,128]{2,1,0:T(1,128)S(1)}, u32[]{:S(2)}, u32[]{:S(2)}) async-start(f32[128,1,128]{2,1,0:T(1,128)} %bitcast.3), calls=%async_computation | async-start | bytes 131072 | tf_op jit(solution)/shard_map/all_to_all | solution.py:460
  56.4 14.2 %collective-permute-start.5 = (f32[16,640]{1,0:T(8,128)S(1)}, f32[16,640]{1,0:T(8,128)S(1)}, u32[]{:S(2)}, u32[]{:S(2)}) collective-permute-start(f32[16,640]{1,0:T(8,128)S(1)} %get-tuple-element.40), channel_id=1, source_target_pairs={{0,4},{4,0},{8,12},{12,8},{16,20},{20,16},{24,28},{28,24},{32,36},... | collective-permute-start | bytes 122888 | tf_op jit(solution)/shard_map/ppermute | solution.py:437
  59.2 11.4 %collective-permute-start.6 = (f32[16,640]{1,0:T(8,128)S(1)}, f32[16,640]{1,0:T(8,128)S(1)}, u32[]{:S(2)}, u32[]{:S(2)}) collective-permute-start(f32[16,640]{1,0:T(8,128)S(1)} %get-tuple-element.41), channel_id=1, source_target_pairs={{0,508},{4,8},{8,4},{12,16},{16,12},{20,24},{24,20},{28,32},{32,28... | collective-permute-start | bytes 122888 | tf_op jit(solution)/shard_map/ppermute | solution.py:437
  62.0 8.7 %collective-permute-start.4 = (f32[16,512]{1,0:T(8,128)S(1)}, f32[16,512]{1,0:T(8,128)S(1)}, u32[]{:S(2)}, u32[]{:S(2)}) collective-permute-start(f32[16,512]{1,0:T(8,128)S(1)} %get-tuple-element.39), channel_id=1, source_target_pairs={{0,256},{4,260},{8,264},{12,268},{16,272},{20,276},{24,280},{28,28... | collective-permute-start | bytes 98312 | tf_op jit(solution)/shard_map/ppermute | solution.py:437
  75.4 28.3 %all-to-all-start.1 = ((f32[128,1,128]{2,1,0:T(1,128)}), f32[128,1,128]{2,1,0:T(1,128)S(1)}, u32[]{:S(2)}, u32[]{:S(2)}) async-start(f32[128,1,128]{2,1,0:T(1,128)} %bitcast.6), calls=%async_computation.1 | async-start | bytes 131072 | tf_op jit(solution)/shard_map/all_to_all | solution.py:460
  89.5 14.2 %collective-permute-start.10 = (f32[16,640]{1,0:T(8,128)S(1)}, f32[16,640]{1,0:T(8,128)S(1)}, u32[]{:S(2)}, u32[]{:S(2)}) collective-permute-start(f32[16,640]{1,0:T(8,128)S(1)} %get-tuple-element.47), channel_id=1, source_target_pairs={{0,4},{4,0},{8,12},{12,8},{16,20},{20,16},{24,28},{28,24},{32,36},... | collective-permute-start | bytes 122888 | tf_op jit(solution)/shard_map/ppermute | solution.py:437
  92.3 11.4 %collective-permute-start.11 = (f32[16,640]{1,0:T(8,128)S(1)}, f32[16,640]{1,0:T(8,128)S(1)}, u32[]{:S(2)}, u32[]{:S(2)}) collective-permute-start(f32[16,640]{1,0:T(8,128)S(1)} %get-tuple-element.48), channel_id=1, source_target_pairs={{0,508},{4,8},{8,4},{12,16},{16,12},{20,24},{24,20},{28,32},{32,28... | collective-permute-start | bytes 122888 | tf_op jit(solution)/shard_map/ppermute | solution.py:437
  95.1 8.7 %collective-permute-start.9 = (f32[16,512]{1,0:T(8,128)S(1)}, f32[16,512]{1,0:T(8,128)S(1)}, u32[]{:S(2)}, u32[]{:S(2)}) collective-permute-start(f32[16,512]{1,0:T(8,128)S(1)} %get-tuple-element.46), channel_id=1, source_target_pairs={{0,256},{4,260},{8,264},{12,268},{16,272},{20,276},{24,280},{28,28... | collective-permute-start | bytes 98312 | tf_op jit(solution)/shard_map/ppermute | solution.py:437
  108.5 28.3 %all-to-all-start.2 = ((f32[128,1,128]{2,1,0:T(1,128)}), f32[128,1,128]{2,1,0:T(1,128)S(1)}, u32[]{:S(2)}, u32[]{:S(2)}) async-start(f32[128,1,128]{2,1,0:T(1,128)} %bitcast.9), calls=%async_computation.2 | async-start | bytes 131072 | tf_op jit(solution)/shard_map/all_to_all | solution.py:460
  122.5 14.2 %collective-permute-start.13 = (f32[16,640]{1,0:T(8,128)S(1)}, f32[16,640]{1,0:T(8,128)S(1)}, u32[]{:S(2)}, u32[]{:S(2)}) collective-permute-start(f32[16,640]{1,0:T(8,128)S(1)} %get-tuple-element.53), channel_id=1, source_target_pairs={{0,4},{4,0},{8,12},{12,8},{16,20},{20,16},{24,28},{28,24},{32,36},... | collective-permute-start | bytes 122888 | tf_op jit(solution)/shard_map/ppermute | solution.py:437
  125.3 11.4 %collective-permute-start.14 = (f32[16,640]{1,0:T(8,128)S(1)}, f32[16,640]{1,0:T(8,128)S(1)}, u32[]{:S(2)}, u32[]{:S(2)}) collective-permute-start(f32[16,640]{1,0:T(8,128)S(1)} %get-tuple-element.54), channel_id=1, source_target_pairs={{0,508},{4,8},{8,4},{12,16},{16,12},{20,24},{24,20},{28,32},{32,28... | collective-permute-start | bytes 122888 | tf_op jit(solution)/shard_map/ppermute | solution.py:437
  128.1 8.7 %collective-permute-start.12 = (f32[16,512]{1,0:T(8,128)S(1)}, f32[16,512]{1,0:T(8,128)S(1)}, u32[]{:S(2)}, u32[]{:S(2)}) collective-permute-start(f32[16,512]{1,0:T(8,128)S(1)} %get-tuple-element.52), channel_id=1, source_target_pairs={{0,256},{4,260},{8,264},{12,268},{16,272},{20,276},{24,280},{28,28... | collective-permute-start | bytes 98312 | tf_op jit(solution)/shard_map/ppermute | solution.py:437
  139.8 8.1 %all-to-all-start.3 = ((f32[4,1,128]{2,1,0:T(1,128)}), f32[4,1,128]{2,1,0:T(1,128)S(1)}, u32[]{:S(2)}, u32[]{:S(2)}) async-start(f32[4,1,128]{2,1,0:T(1,128)} %bitcast.12), calls=%async_computation.3 | async-start | bytes 4096 | tf_op jit(solution)/shard_map/all_to_all | solution.py:460
  (3 other events, 42.5 us)
